TPU v7x, 32 devices: a whole 2x2x4 slice. The times are simulated.
32 devices in a mesh: seq: 8 (over y, x, core), pipe: 4 (over z).
Axes of the slice: x: 2, y: 2, z: 4, core: 2. Of those that a mesh axis runs over, the one named last changes fastest.
Arguments:
- section_input: bfloat16 [4, 1024, 4096], P('pipe', 'seq'), may hold values from -6 to 6
- out_grad: bfloat16 [4, 1024, 4096], P('pipe', 'seq'), may hold values from -6 to 6
- conv_filter: float32 [4, 1024, 4096], P('pipe', None, 'seq'), may hold values from -2 to 2
- short_taps: float32 [4, 3, 3, 4096], P('pipe'), may hold values from -3 to 3
Outputs:
- grad_prev: bfloat16 [4, 1024, 4096], P('pipe', 'seq')
- filter_grad: float32 [4, 1024, 4096], P('pipe', None, 'seq')
All inputs are finite; a program needn't handle non-finite values.
Results may differ from a plain program's by a relative error of at most 0.011.
Values may be sent and summed in bfloat16 or wider, within the bound.
No kernel may reach another device: no remote copies, remote signals or barrier semaphores. Data moves between devices by JAX's collectives and lax.ppermute only.
A program may use at most 128 MiB of HBM per device.

v0:
```python
import math

import jax
import jax.numpy as jnp
from jax import lax
from jax.sharding import PartitionSpec as P


def passed_along(shard, axis, by):
    count = lax.axis_size(axis)
    pairs = [(i, i + by) for i in range(count) if 0 <= i + by < count]
    return lax.ppermute(shard, axis, pairs)


def shifted(block, axis, distance):
    devices = range(lax.axis_size(axis))
    route = [((i - distance) % len(devices), i) for i in devices]
    return lax.ppermute(block, axis, route)


def phase_table(row_count, col_count, modulus, direction):
    row_ids = lax.broadcasted_iota(jnp.int32, (row_count, col_count), 0)
    col_ids = lax.broadcasted_iota(jnp.int32, (row_count, col_count), 1)
    residue = row_ids * col_ids % modulus
    angles = direction * 2.0 * math.pi / modulus * residue.astype(jnp.float32)
    return (jnp.cos(angles), jnp.sin(angles))


def highest(pattern, first_op, second_op):
    return jnp.einsum(pattern, first_op, second_op, precision=lax.Precision.HIGHEST)


def forward_spectrum(signal, half_q, width_p):
    full_q = 2 * half_q
    blocks = signal.reshape(half_q, width_p, signal.shape[1])
    fq_re, fq_im = phase_table(full_q, half_q, full_q, -1.0)
    section_re = highest("kq,qpc->kpc", fq_re, blocks)
    section_im = highest("kq,qpc->kpc", fq_im, blocks)
    tw_re, tw_im = phase_table(full_q, width_p, full_q * width_p, -1.0)
    turned_re = section_re * tw_re[:, :, None] - section_im * tw_im[:, :, None]
    turned_im = section_re * tw_im[:, :, None] + section_im * tw_re[:, :, None]
    fp_re, fp_im = phase_table(width_p, width_p, width_p, -1.0)
    out_re = highest("jp,kpc->jkc", fp_re, turned_re) - highest("jp,kpc->jkc", fp_im, turned_im)
    out_im = highest("jp,kpc->jkc", fp_re, turned_im) + highest("jp,kpc->jkc", fp_im, turned_re)
    return (out_re, out_im)


def inverse_field(spec_re, spec_im, half_q, width_p):
    full_q = 2 * half_q
    gp_re, gp_im = phase_table(width_p, width_p, width_p, 1.0)
    section_re = highest("mn,nqc->mqc", gp_re, spec_re) - highest("mn,nqc->mqc", gp_im, spec_im)
    section_im = highest("mn,nqc->mqc", gp_re, spec_im) + highest("mn,nqc->mqc", gp_im, spec_re)
    tw_re, tw_im = phase_table(width_p, full_q, full_q * width_p, 1.0)
    turned_re = section_re * tw_re[:, :, None] - section_im * tw_im[:, :, None]
    turned_im = section_re * tw_im[:, :, None] + section_im * tw_re[:, :, None]
    gq_re, gq_im = phase_table(half_q, full_q, full_q, 1.0)
    result = highest("aq,mqc->amc", gq_re, turned_re) - highest("aq,mqc->amc", gq_im, turned_im)
    return result.reshape(half_q * width_p, spec_re.shape[2]) / (full_q * width_p)


def convolve(first_sig, second_sig, half_q, width_p):
    one_re, one_im = forward_spectrum(first_sig, half_q, width_p)
    two_re, two_im = forward_spectrum(second_sig, half_q, width_p)
    return inverse_field(
        one_re * two_re - one_im * two_im, one_re * two_im + one_im * two_re, half_q, width_p
    )


def correlate(first_sig, second_sig, half_q, width_p):
    one_re, one_im = forward_spectrum(first_sig, half_q, width_p)
    two_re, two_im = forward_spectrum(second_sig, half_q, width_p)
    return inverse_field(
        one_re * two_re + one_im * two_im, one_re * two_im - one_im * two_re, half_q, width_p
    )


def spectral_pass(product, adjoint, kernel, half_q):
    seq_rows = product.shape[0]
    width_p = seq_rows // half_q
    grad_scale = 1.0 / math.sqrt(seq_rows)
    combined = convolve(product, kernel, half_q, width_p)
    backward = correlate(kernel, adjoint, half_q, width_p)
    filter_grad = correlate(product, adjoint, half_q, width_p)
    return (combined, backward, filter_grad * grad_scale)


def shards(section_input, out_grad, conv_filter, short_taps):
    inputs = section_input[0]
    upstream = out_grad[0]
    kernel = conv_filter[0]
    tap_table = short_taps[0]
    length_dev = inputs.shape[0]
    reach_rows = tap_table.shape[1] - 1
    earlier = passed_along(inputs[length_dev - reach_rows :], "seq", 1)
    padded = jnp.concatenate([earlier, inputs], axis=0).astype(jnp.float32)
    streams = []
    for stream_idx in range(3):
        combined_rows = jnp.zeros((length_dev, inputs.shape[1]), jnp.float32)
        for tap_idx in range(reach_rows + 1):
            start_row = reach_rows - tap_idx
            combined_rows = (
                combined_rows
                + tap_table[stream_idx, tap_idx] * padded[start_row : start_row + length_dev]
            )
        streams.append(combined_rows.astype(jnp.bfloat16))
    query_rows, key_rows, value_rows = streams
    half_q = lax.axis_size("seq")
    product = key_rows.astype(jnp.float32) * value_rows.astype(jnp.float32)
    adjoint = upstream.astype(jnp.float32) * query_rows.astype(jnp.float32)
    prod_cols, adj_cols = (
        lax.all_to_all(product, "seq", split_axis=1, concat_axis=0, tiled=True),
        lax.all_to_all(adjoint, "seq", split_axis=1, concat_axis=0, tiled=True),
    )
    mixed_cols, back_cols, filter_grad = spectral_pass(prod_cols, adj_cols, kernel, half_q)
    mixed_rows, back_rows = (
        lax.all_to_all(mixed_cols, "seq", split_axis=0, concat_axis=1, tiled=True),
        lax.all_to_all(back_cols, "seq", split_axis=0, concat_axis=1, tiled=True),
    )
    grad_query = (upstream.astype(jnp.float32) * mixed_rows).astype(jnp.bfloat16)
    grad_key = (back_rows * value_rows.astype(jnp.float32)).astype(jnp.bfloat16)
    grad_value = (back_rows * key_rows.astype(jnp.float32)).astype(jnp.bfloat16)
    later_rows = passed_along(
        (grad_query[:reach_rows], grad_key[:reach_rows], grad_value[:reach_rows]), "seq", -1
    )
    summed = jnp.zeros((length_dev, inputs.shape[1]), jnp.float32)
    grad_list = (grad_query, grad_key, grad_value)
    for stream_idx in range(3):
        extended = jnp.concatenate([grad_list[stream_idx], later_rows[stream_idx]], axis=0).astype(
            jnp.float32
        )
        for tap_idx in range(reach_rows + 1):
            summed = (
                summed + tap_table[stream_idx, tap_idx] * extended[tap_idx : tap_idx + length_dev]
            )
    grad_input = summed.astype(jnp.bfloat16)
    received = shifted(grad_input[None], "pipe", -1)
    return (received, filter_grad[None])


def solution(mesh):
    return jax.shard_map(
        shards,
        mesh=mesh,
        in_specs=(
            P("pipe", "seq", None),
            P("pipe", "seq", None),
            P("pipe", None, "seq"),
            P("pipe", None, None, None),
        ),
        out_specs=(P("pipe", "seq", None), P("pipe", None, "seq")),
        check_vma=False,
    )
```

profile of v0, /device:TPU:0, one launch (start us, length us, event | category | flops | bytes accessed | tf_op | source)
XLA Modules:
  0.0 420.1 jit_solution(4597146611515120087)
XLA Ops:
  1.7 2.4 collective-permute-start
  5.2 2.3 copy.145
  7.4 1.6 copy.144
  10.5 2.3 maximum_convert_fusion
  12.8 8.4 %convert_multiply_fusion.3 = (f32[128,4096]{0,1:T(8,128)}, bf16[128,4096]{0,1:T(8,128)(2,1)}, bf16[128,4096]{0,1:T(8,128)(2,1)}, f32[128,4096]{0,1:T(8,128)}) fusion(f32[130,4096]{0,1:T(8,128)S(1)} %maximum_convert_fusion, f32[4096]{0:T(1024)S(1)} %bitcast.163, f32[4096]{0:T(1024)S(1)} %bitcast.165, f32[4096]{0:T(1024)S(1)} %bitcast.167, ...), kind=kLoop, calls=%fused_computation.57 | loop fusion | flops 12582912 | bytes 13778944 | tf_op jit(solution)/shard_map/mul | solution.py:108
  21.2 2.9 copy.167
  24.1 5.0 %all-to-all-start.2 = ((f32[128,8,512]{2,0,1:T(8,128)}), f32[128,8,512]{2,0,1:T(8,128)}, u32[]{:S(2)}, u32[]{:S(2)}) async-start(f32[128,8,512]{2,0,1:T(8,128)} %copy.167), calls=%async_computation.2 | async-start | bytes 4194304 | tf_op jit(solution)/shard_map/all_to_all | solution.py:112
  29.1 2.9 copy.147
  32.0 23.8 %all-to-all-done.2 = f32[128,8,512]{2,0,1:T(8,128)} async-done(((f32[128,8,512]{2,0,1:T(8,128)}), f32[128,8,512]{2,0,1:T(8,128)}, u32[]{:S(2)}, u32[]{:S(2)}) %all-to-all-start.2) | async-done | bytes 2097184 | tf_op jit(solution)/shard_map/all_to_all | solution.py:112
  55.9 4.5 %all-to-all-start = ((f32[128,8,512]{2,0,1:T(8,128)}), f32[128,8,512]{2,0,1:T(8,128)}, u32[]{:S(2)}, u32[]{:S(2)}) async-start(f32[128,8,512]{2,0,1:T(8,128)} %copy.147), calls=%async_computation | async-start | bytes 4194304 | tf_op jit(solution)/shard_map/all_to_all | solution.py:111
  60.8 5.6 %fusion.76 = f32[16,128,512]{2,0,1:T(8,128)} fusion(f32[8,128,512]{2,1,0:T(8,128)S(1)} %bitcast.148), kind=kOutput, calls=%fused_computation.112 | convolution fusion | flops 100665088 | bytes 6291456 | tf_op jit(solution)/shard_map/kq,qpc->kpc/dot_general | solution.py:30
  66.4 5.7 %fusion.78 = f32[16,128,512]{2,0,1:T(8,128)} fusion(f32[8,128,512]{2,1,0:T(8,128)S(1)} %bitcast.147), kind=kOutput, calls=%fused_computation.114 | convolution fusion | flops 100665088 | bytes 6291456 | tf_op jit(solution)/shard_map/kq,qpc->kpc/dot_general | solution.py:30
  72.1 7.3 %fusion.66 = f32[16,128,512]{2,0,1:T(8,128)} fusion(f32[128,8,512]{2,0,1:T(8,128)} %all-to-all-done.2), kind=kOutput, calls=%fused_computation.96 | convolution fusion | flops 100665088 | bytes 6291456 | tf_op jit(solution)/shard_map/kq,qpc->kpc/dot_general | solution.py:30
  79.4 7.4 %fusion.68 = f32[16,128,512]{2,0,1:T(8,128)} fusion(f32[128,8,512]{2,0,1:T(8,128)} %all-to-all-done.2), kind=kOutput, calls=%fused_computation.98 | convolution fusion | flops 100665088 | bytes 6291456 | tf_op jit(solution)/shard_map/kq,qpc->kpc/dot_general | solution.py:30
  87.1 7.4 %fusion.72 = f32[16,128,512]{2,0,1:T(8,128)} fusion(f32[128,8,512]{2,0,1:T(8,128)} %all-to-all-done), kind=kOutput, calls=%fused_computation.102 | convolution fusion | flops 100665088 | bytes 6291456 | tf_op jit(solution)/shard_map/kq,qpc->kpc/dot_general | solution.py:30
  94.5 15.5 %multiply_subtract_fusion.8 = (f32[16,128,512]{2,0,1:T(8,128)}, f32[16,128,512]{2,0,1:T(8,128)}, f32[16,128,512]{2,0,1:T(8,128)}, f32[16,128,512]{2,0,1:T(8,128)...) fusion(f32[16,128,512]{2,0,1:T(8,128)} %fusion.72, f32[16,128]{0,1:T(8,128)S(1)} %copy.150, ...), kind=kOutput, calls=%fused_computation.29 | convolution fusion | flops 119539456 | bytes 48250880 | tf_op jit(solution)/shard_map/kq,qpc->kpc/dot_general | solution.py:30
  110.0 8.9 %fusion.22 = f32[128,16,512]{2,0,1:T(8,128)S(1)} fusion(f32[16,128,512]{2,0,1:T(8,128)} %get-tuple-element.45), kind=kOutput, calls=%fused_computation.40 | convolution fusion | flops 1610842112 | bytes 8388608 | tf_op jit(solution)/shard_map/jp,kpc->jkc/dot_general | solution.py:30
  118.8 6.0 %fusion.20 = f32[128,16,512]{2,0,1:T(8,128)S(1)} fusion(f32[16,128,512]{2,0,1:T(8,128)S(1)} %copy-done.5), kind=kOutput, calls=%fused_computation.38 | convolution fusion | flops 1610842112 | bytes 8388608 | tf_op jit(solution)/shard_map/jp,kpc->jkc/dot_general | solution.py:30
  124.9 6.2 %fusion.14 = f32[128,16,512]{2,0,1:T(8,128)S(1)} fusion(f32[16,128,512]{2,0,1:T(8,128)S(1)} %copy-done.4), kind=kOutput, calls=%fused_computation.32 | convolution fusion | flops 1610842112 | bytes 8388608 | tf_op jit(solution)/shard_map/jp,kpc->jkc/dot_general | solution.py:30
  131.1 6.0 %fusion.12 = f32[128,16,512]{2,0,1:T(8,128)S(1)} fusion(f32[16,128,512]{2,0,1:T(8,128)S(1)} %copy-done.4), kind=kOutput, calls=%fused_computation.30 | convolution fusion | flops 1610842112 | bytes 8388608 | tf_op jit(solution)/shard_map/jp,kpc->jkc/dot_general | solution.py:30
  137.1 6.2 %fusion.30 = f32[128,16,512]{2,0,1:T(8,128)S(1)} fusion(f32[16,128,512]{2,0,1:T(8,128)S(1)} %copy-done.3), kind=kOutput, calls=%fused_computation.48 | convolution fusion | flops 1610842112 | bytes 8388608 | tf_op jit(solution)/shard_map/jp,kpc->jkc/dot_general | solution.py:30
  143.3 7.3 %fusion.28 = f32[128,16,512]{2,0,1:T(8,128)} fusion(f32[16,128,512]{2,0,1:T(8,128)S(1)} %copy-done.3), kind=kOutput, calls=%fused_computation.46 | convolution fusion | flops 1610842112 | bytes 8388608 | tf_op jit(solution)/shard_map/jp,kpc->jkc/dot_general | solution.py:30
  150.6 7.2 %fusion.42 = f32[128,16,512]{2,0,1:T(8,128)} fusion(f32[128,16,512]{2,0,1:T(8,128)S(1)} %fusion.22, f32[16,128,512]{2,0,1:T(8,128)S(1)} %copy-done.2), kind=kOutput, calls=%fused_computation.61 | convolution fusion | flops 1611890688 | bytes 12582912 | tf_op jit(solution)/shard_map/jp,kpc->jkc/dot_general | solution.py:30
  157.8 7.3 %fusion.45 = f32[128,16,512]{2,0,1:T(8,128)} fusion(f32[128,16,512]{2,0,1:T(8,128)S(1)} %fusion.20, f32[16,128,512]{2,0,1:T(8,128)S(1)} %copy-done.2), kind=kOutput, calls=%fused_computation.62 | convolution fusion | flops 1611890688 | bytes 12582912 | tf_op jit(solution)/shard_map/jp,kpc->jkc/dot_general | solution.py:30
  165.1 7.2 %fusion.48 = f32[128,16,512]{2,0,1:T(8,128)} fusion(f32[128,16,512]{2,0,1:T(8,128)S(1)} %fusion.14, f32[16,128,512]{2,0,1:T(8,128)S(1)} %get-tuple-element.48), kind=kOutput, calls=%fused_computation.63 | convolution fusion | flops 1611890688 | bytes 12582912 | tf_op jit(solution)/shard_map/jp,kpc->jkc/dot_general | solution.py:30
  172.4 7.6 %fusion.51 = f32[128,16,512]{2,0,1:T(8,128)} fusion(f32[128,16,512]{2,0,1:T(8,128)S(1)} %fusion.12, f32[16,128,512]{2,0,1:T(8,128)S(1)} %get-tuple-element.48), kind=kOutput, calls=%fused_computation.64 | convolution fusion | flops 1611890688 | bytes 12582912 | tf_op jit(solution)/shard_map/jp,kpc->jkc/dot_general | solution.py:30
  180.0 7.2 %fusion.36 = f32[128,16,512]{2,0,1:T(8,128)} fusion(f32[128,16,512]{2,0,1:T(8,128)S(1)} %fusion.30, f32[16,128,512]{2,0,1:T(8,128)S(1)} %copy-done.6), kind=kOutput, calls=%fused_computation.59 | convolution fusion | flops 1611890688 | bytes 12582912 | tf_op jit(solution)/shard_map/jp,kpc->jkc/dot_general | solution.py:30
  187.2 22.3 %multiply_add_fusion.1 = (f32[128,16,512]{2,0,1:T(8,128)}, f32[128,16,512]{2,0,1:T(8,128)}, f32[128,16,512]{2,0,1:T(8,128)}, f32[128,16,512]{2,0,1:T(8,128)}, f3...) fusion(f32[128,16,512]{2,0,1:T(8,128)} %fusion.51, f32[128,16,512]{2,0,1:T(8,128)} %fusion.36, ...), kind=kOutput, calls=%fused_computation.15 | convolution fusion | flops 1630765056 | bytes 54525952 | tf_op jit(solution)/shard_map/jp,kpc->jkc/dot_general | solution.py:30
  209.6 6.3 %fusion.119 = f32[128,16,512]{2,0,1:T(8,128)S(1)} fusion(f32[128,16,512]{2,0,1:T(8,128)} %get-tuple-element.32), kind=kOutput, calls=%fused_computation.153 | convolution fusion | flops 1610842112 | bytes 8388608 | tf_op jit(solution)/shard_map/mn,nqc->mqc/dot_general | solution.py:30
  215.9 4.0 fusion.117
  219.9 5.7 %convolution_subtract_fusion.2 = f32[128,16,512]{2,0,1:T(8,128)} fusion(f32[128,16,512]{2,0,1:T(8,128)S(1)} %fusion.119, f32[128,16,512]{2,0,1:T(8,128)S(1)} %copy-done.12), kind=kOutput, calls=%fused_computation.70 | convolution fusion | flops 1611890688 | bytes 12582912 | tf_op jit(solution)/shard_map/mn,nqc->mqc/dot_general | solution.py:30
  225.6 5.9 %convolution_add_fusion.2 = f32[128,16,512]{2,0,1:T(8,128)} fusion(f32[128,16,512]{2,0,1:T(8,128)S(1)} %fusion.117, f32[128,16,512]{2,0,1:T(8,128)S(1)} %copy-done.11), kind=kOutput, calls=%fused_computation.69 | convolution fusion | flops 1611890688 | bytes 12582912 | tf_op jit(solution)/shard_map/mn,nqc->mqc/dot_general | solution.py:30
  231.6 4.0 fusion.115
  235.6 4.0 fusion.113
  239.6 5.7 %convolution_subtract_fusion.1 = f32[128,16,512]{2,0,1:T(8,128)} fusion(f32[128,16,512]{2,0,1:T(8,128)S(1)} %fusion.115, f32[128,16,512]{2,0,1:T(8,128)S(1)} %copy-done.10), kind=kOutput, calls=%fused_computation.68 | convolution fusion | flops 1611890688 | bytes 12582912 | tf_op jit(solution)/shard_map/mn,nqc->mqc/dot_general | solution.py:30
  245.3 6.1 %convolution_add_fusion.1 = f32[128,16,512]{2,0,1:T(8,128)} fusion(f32[128,16,512]{2,0,1:T(8,128)S(1)} %fusion.113, f32[128,16,512]{2,0,1:T(8,128)S(1)} %copy-done.9), kind=kOutput, calls=%fused_computation.67 | convolution fusion | flops 1611890688 | bytes 12582912 | tf_op jit(solution)/shard_map/mn,nqc->mqc/dot_general | solution.py:30
  251.4 4.0 fusion.111
  255.5 5.6 %fusion.109 = f32[128,16,512]{2,0,1:T(8,128)} fusion(f32[128,16,512]{2,0,1:T(8,128)S(1)} %copy-done.8), kind=kOutput, calls=%fused_computation.143 | convolution fusion | flops 1610842112 | bytes 8388608 | tf_op jit(solution)/shard_map/mn,nqc->mqc/dot_general | solution.py:30
  261.1 5.7 %convolution_subtract_fusion = f32[128,16,512]{2,0,1:T(8,128)} fusion(f32[128,16,512]{2,0,1:T(8,128)S(1)} %fusion.111, f32[128,16,512]{2,0,1:T(8,128)S(1)} %copy-done.8), kind=kOutput, calls=%fused_computation.66 | convolution fusion | flops 1611890688 | bytes 12582912 | tf_op jit(solution)/shard_map/mn,nqc->mqc/dot_general | solution.py:30
  266.7 18.3 %multiply_subtract_fusion = (f32[128,16,512]{2,0,1:T(8,128)}, f32[128,16,512]{2,0,1:T(8,128)}, f32[128,16,512]{2,0,1:T(8,128)}, f32[128,16,512]{2,0,1:T(8,128)},...) fusion(f32[128,16,512]{2,0,1:T(8,128)} %convolution_subtract_fusion, f32[128,16]{0,1:T(8,128)S(1)} %get-tuple-element.53, ...), kind=kOutput, calls=%fused_computation.13 | convolution fusion | flops 1630765056 | bytes 54542336 | tf_op jit(solution)/shard_map/mn,nqc->mqc/dot_general | solution.py:30
  285.0 7.0 %fusion.8 = f32[8,128,512]{2,0,1:T(8,128)S(1)} fusion(f32[128,16,512]{2,0,1:T(8,128)} %get-tuple-element.51), kind=kOutput, calls=%fused_computation.8 | convolution fusion | flops 100665088 | bytes 6291456 | tf_op jit(solution)/shard_map/aq,mqc->amc/dot_general | solution.py:30
  292.1 4.5 %subtract_multiply_fusion.2 = f32[8,128,512]{2,0,1:T(8,128)S(1)} fusion(f32[8,128,512]{2,0,1:T(8,128)S(1)} %fusion.8, f32[128,16,512]{2,0,1:T(8,128)S(1)} %copy-done.17), kind=kOutput, calls=%fused_computation.107 | convolution fusion | flops 101713664 | bytes 8388608 | tf_op jit(solution)/shard_map/aq,mqc->amc/dot_general | solution.py:30
  296.6 2.6 copy.163
  299.2 4.8 %all-to-all-start.1 = ((f32[8,128,512]{2,1,0:T(8,128)}), f32[8,128,512]{2,1,0:T(8,128)}, u32[]{:S(2)}, u32[]{:S(2)}) async-start(f32[8,128,512]{2,1,0:T(8,128)} %copy.163), calls=%async_computation.1 | async-start | bytes 4194304 | tf_op jit(solution)/shard_map/all_to_all | solution.py:116
  304.0 7.0 %fusion.4 = f32[8,128,512]{2,0,1:T(8,128)S(1)} fusion(f32[128,16,512]{2,0,1:T(8,128)} %get-tuple-element.49), kind=kOutput, calls=%fused_computation.4 | convolution fusion | flops 100665088 | bytes 6291456 | tf_op jit(solution)/shard_map/aq,mqc->amc/dot_general | solution.py:30
  311.0 4.5 %subtract_multiply_fusion.1 = f32[8,128,512]{2,0,1:T(8,128)S(1)} fusion(f32[8,128,512]{2,0,1:T(8,128)S(1)} %fusion.4, f32[128,16,512]{2,0,1:T(8,128)S(1)} %copy-done.16), kind=kOutput, calls=%fused_computation.105 | convolution fusion | flops 101713664 | bytes 8388608 | tf_op jit(solution)/shard_map/aq,mqc->amc/dot_general | solution.py:30
  315.5 2.5 copy.175
  318.1 12.6 %all-to-all-done.1 = f32[8,128,512]{2,1,0:T(8,128)} async-done(((f32[8,128,512]{2,1,0:T(8,128)}), f32[8,128,512]{2,1,0:T(8,128)}, u32[]{:S(2)}, u32[]{:S(2)}) %all-to-all-start.1) | async-done | bytes 2097184 | tf_op jit(solution)/shard_map/all_to_all | solution.py:116
  330.6 4.4 %all-to-all-start.3 = ((f32[8,128,512]{2,1,0:T(8,128)}), f32[8,128,512]{2,1,0:T(8,128)}, u32[]{:S(2)}, u32[]{:S(2)}) async-start(f32[8,128,512]{2,1,0:T(8,128)} %copy.175), calls=%async_computation.3 | async-start | bytes 4194304 | tf_op jit(solution)/shard_map/all_to_all | solution.py:117
  335.0 2.9 copy.164
  337.9 1.8 fusion.56
  341.4 20.2 %all-to-all-done.3 = f32[8,128,512]{2,1,0:T(8,128)} async-done(((f32[8,128,512]{2,1,0:T(8,128)}), f32[8,128,512]{2,1,0:T(8,128)}, u32[]{:S(2)}, u32[]{:S(2)}) %all-to-all-start.3) | async-done | bytes 2097184 | tf_op jit(solution)/shard_map/all_to_all | solution.py:117
  361.6 2.9 copy.176
  364.5 2.6 fusion.55
  369.2 1.5 collective-permute-start.3
  372.0 3.6 maximum_convert_fusion.1
  376.1 2.4 maximum_convert_fusion.2
  379.4 1.8 copy-done.13
  381.2 10.9 %fusion.88 = bf16[1,128,4096]{1,2,0:T(8,128)(2,1)S(1)} fusion(f32[130,4096]{0,1:T(8,128)S(1)} %maximum_convert_fusion.3, f32[4096]{0:T(1024)S(1)} %bitcast.164, f32[4096]{0:T(1024)S(1)} %bitcast.166, f32[4096]{0:T(1024)S(1)} %bitcast.168, f32[130,4096]{0,1:T(8,128)} %maximum_convert_fusion.2, f32[4096]{0:T(1024)S(1)} %bitcast.170, f32[4096]{0:T(1024)S(1)} %bitcast.172, ...), kind=kLoop, calls=%fused_computation.118 | loop fusion | flops 9437184 | bytes 20070400 | tf_op jit(solution)/shard_map/broadcast_in_dim | solution.py:136
  392.1 3.7 collective-permute-start.4
  395.9 4.4 %fusion = f32[8,128,512]{2,0,1:T(8,128)S(1)} fusion(f32[128,16,512]{2,0,1:T(8,128)S(1)} %copy-done.15), kind=kOutput, calls=%fused_computation | convolution fusion | flops 100665088 | bytes 6291456 | tf_op jit(solution)/shard_map/aq,mqc->amc/dot_general | solution.py:30
  400.3 4.5 %subtract_multiply_fusion = f32[8,128,512]{2,0,1:T(8,128)S(1)} fusion(f32[8,128,512]{2,0,1:T(8,128)S(1)} %fusion, f32[128,16,512]{2,0,1:T(8,128)S(1)} %copy-done.14), kind=kOutput, calls=%fused_computation.104 | convolution fusion | flops 101713664 | bytes 8388608 | tf_op jit(solution)/shard_map/aq,mqc->amc/dot_general | solution.py:30
  404.9 2.5 copy.183
  407.4 11.3 %collective-permute-done.4 = bf16[1,128,4096]{1,2,0:T(8,128)(2,1)S(1)} collective-permute-done((bf16[1,128,4096]{1,2,0:T(8,128)(2,1)S(1)}, bf16[1,128,4096]{1,2,0:T(8,128)(2,1)S(1)}, u32[]{:S(2)}, u32[]{:S(2)}) %collective-permute-start.4) | collective-permute-done | bytes 1048608 | tf_op jit(solution)/shard_map/ppermute | solution.py:18
  (63 shorter events, 12.0 us)
Async XLA Ops:
  0.6 60.2 %copy-start = (f32[1,1024,512]{2,1,0:T(8,128)S(1)}, f32[1,1024,512]{2,1,0:T(8,128)}, u32[]{:S(2)}) copy-start(f32[1,1024,512]{2,1,0:T(8,128)} %param.6) | copy-start | bytes 6291460
  1.7 7.4 %collective-permute-start = (bf16[2,4096]{1,0:T(2,128)(2,1)S(1)}, bf16[2,4096]{1,0:T(2,128)(2,1)S(1)}, u32[]{:S(2)}, u32[]{:S(2)}) collective-permute-start(bf16[2,4096]{1,0:T(2,128)(2,1)S(1)} %slice_bitcast_fusion), channel_id=1, source_target_pairs={{0,4},{4,8},{8,12},{12,16},{16,20},{20,24},{24,28},{1,5},{5,9},{9,... | collective-permute-start | bytes 49160 | tf_op jit(solution)/shard_map/ppermute | solution.py:12
  9.0 12.1 %copy-start.18 = (bf16[1,128,4096]{1,2,0:T(8,128)(2,1)}, bf16[1,128,4096]{1,2,0:T(8,128)(2,1)S(1)}, u32[]{:S(2)}) copy-start(bf16[1,128,4096]{1,2,0:T(8,128)(2,1)S(1)} %copy.144) | copy-start | bytes 3145732
  24.1 31.8 %all-to-all-start.2 = ((f32[128,8,512]{2,0,1:T(8,128)}), f32[128,8,512]{2,0,1:T(8,128)}, u32[]{:S(2)}, u32[]{:S(2)}) async-start(f32[128,8,512]{2,0,1:T(8,128)} %copy.167), calls=%async_computation.2 | async-start | bytes 4194304 | tf_op jit(solution)/shard_map/all_to_all | solution.py:112
  55.9 31.2 %all-to-all-start = ((f32[128,8,512]{2,0,1:T(8,128)}), f32[128,8,512]{2,0,1:T(8,128)}, u32[]{:S(2)}, u32[]{:S(2)}) async-start(f32[128,8,512]{2,0,1:T(8,128)} %copy.147), calls=%async_computation | async-start | bytes 4194304 | tf_op jit(solution)/shard_map/all_to_all | solution.py:111
  109.9 8.9 %copy-start.5 = (f32[16,128,512]{2,0,1:T(8,128)S(1)}, f32[16,128,512]{2,0,1:T(8,128)}, u32[]{:S(2)}) copy-start(f32[16,128,512]{2,0,1:T(8,128)} %get-tuple-element.45) | copy-start | bytes 12582916
  118.8 6.0 %copy-start.4 = (f32[16,128,512]{2,0,1:T(8,128)S(1)}, f32[16,128,512]{2,0,1:T(8,128)}, u32[]{:S(2)}) copy-start(f32[16,128,512]{2,0,1:T(8,128)} %get-tuple-element.47) | copy-start | bytes 12582916
  131.1 6.0 %copy-start.3 = (f32[16,128,512]{2,0,1:T(8,128)S(1)}, f32[16,128,512]{2,0,1:T(8,128)}, u32[]{:S(2)}) copy-start(f32[16,128,512]{2,0,1:T(8,128)} %get-tuple-element.18) | copy-start | bytes 12582916
  143.3 7.3 %copy-start.2 = (f32[16,128,512]{2,0,1:T(8,128)S(1)}, f32[16,128,512]{2,0,1:T(8,128)}, u32[]{:S(2)}) copy-start(f32[16,128,512]{2,0,1:T(8,128)} %get-tuple-element.46) | copy-start | bytes 12582916
  172.4 7.6 %copy-start.6 = (f32[16,128,512]{2,0,1:T(8,128)S(1)}, f32[16,128,512]{2,0,1:T(8,128)}, u32[]{:S(2)}) copy-start(f32[16,128,512]{2,0,1:T(8,128)} %get-tuple-element.17) | copy-start | bytes 12582916
  209.6 6.3 %copy-start.12 = (f32[128,16,512]{2,0,1:T(8,128)S(1)}, f32[128,16,512]{2,0,1:T(8,128)}, u32[]{:S(2)}) copy-start(f32[128,16,512]{2,0,1:T(8,128)} %get-tuple-element.31) | copy-start | bytes 12582916
  219.9 5.8 %copy-start.11 = (f32[128,16,512]{2,0,1:T(8,128)S(1)}, f32[128,16,512]{2,0,1:T(8,128)}, u32[]{:S(2)}) copy-start(f32[128,16,512]{2,0,1:T(8,128)} %get-tuple-element.32) | copy-start | bytes 12582916
  225.6 5.9 %copy-start.9 = (f32[128,16,512]{2,0,1:T(8,128)S(1)}, f32[128,16,512]{2,0,1:T(8,128)}, u32[]{:S(2)}) copy-start(f32[128,16,512]{2,0,1:T(8,128)} %get-tuple-element.30) | copy-start | bytes 12582916
  231.5 4.0 copy-start.10
  245.3 6.1 %copy-start.7 = (f32[128,16,512]{2,0,1:T(8,128)S(1)}, f32[128,16,512]{2,0,1:T(8,128)}, u32[]{:S(2)}) copy-start(f32[128,16,512]{2,0,1:T(8,128)} %get-tuple-element.11) | copy-start | bytes 12582916
  251.4 4.0 copy-start.8
  285.0 7.0 %copy-start.17 = (f32[128,16,512]{2,0,1:T(8,128)S(1)}, f32[128,16,512]{2,0,1:T(8,128)}, u32[]{:S(2)}) copy-start(f32[128,16,512]{2,0,1:T(8,128)} %get-tuple-element.52) | copy-start | bytes 12582916
  299.2 31.4 %all-to-all-start.1 = ((f32[8,128,512]{2,1,0:T(8,128)}), f32[8,128,512]{2,1,0:T(8,128)}, u32[]{:S(2)}, u32[]{:S(2)}) async-start(f32[8,128,512]{2,1,0:T(8,128)} %copy.163), calls=%async_computation.1 | async-start | bytes 4194304 | tf_op jit(solution)/shard_map/all_to_all | solution.py:116
  304.0 7.0 %copy-start.16 = (f32[128,16,512]{2,0,1:T(8,128)S(1)}, f32[128,16,512]{2,0,1:T(8,128)}, u32[]{:S(2)}) copy-start(f32[128,16,512]{2,0,1:T(8,128)} %get-tuple-element.50) | copy-start | bytes 12582916
  318.1 19.9 %copy-start.19 = (bf16[1,128,4096]{1,2,0:T(8,128)(2,1)S(1)}, bf16[1,128,4096]{1,2,0:T(8,128)(2,1)}, u32[]{:S(2)}) copy-start(bf16[1,128,4096]{1,2,0:T(8,128)(2,1)} %copy-done.18) | copy-start | bytes 3145732
  330.6 31.0 %all-to-all-start.3 = ((f32[8,128,512]{2,1,0:T(8,128)}), f32[8,128,512]{2,1,0:T(8,128)}, u32[]{:S(2)}, u32[]{:S(2)}) async-start(f32[8,128,512]{2,1,0:T(8,128)} %copy.175), calls=%async_computation.3 | async-start | bytes 4194304 | tf_op jit(solution)/shard_map/all_to_all | solution.py:117
  340.1 30.5 %collective-permute-start.1 = (bf16[2,4096]{1,0:T(2,128)(2,1)S(1)}, bf16[2,4096]{1,0:T(2,128)(2,1)S(1)}, u32[]{:S(2)}, u32[]{:S(2)}) collective-permute-start(bf16[2,4096]{1,0:T(2,128)(2,1)S(1)} %copy.165), channel_id=1, source_target_pairs={{4,0},{8,4},{12,8},{16,12},{20,16},{24,20},{28,24},{5,1},{9,5},{13... | collective-permute-start | bytes 49160 | tf_op jit(solution)/shard_map/ppermute | solution.py:12
  367.5 8.1 %collective-permute-start.2 = (bf16[2,4096]{1,0:T(2,128)(2,1)S(1)}, bf16[2,4096]{1,0:T(2,128)(2,1)S(1)}, u32[]{:S(2)}, u32[]{:S(2)}) collective-permute-start(bf16[2,4096]{1,0:T(2,128)(2,1)S(1)} %copy.177), channel_id=1, source_target_pairs={{4,0},{8,4},{12,8},{16,12},{20,16},{24,20},{28,24},{5,1},{9,5},{13... | collective-permute-start | bytes 49160 | tf_op jit(solution)/shard_map/ppermute | solution.py:12
  369.2 9.4 %collective-permute-start.3 = (bf16[2,4096]{1,0:T(2,128)(2,1)S(1)}, bf16[2,4096]{1,0:T(2,128)(2,1)S(1)}, u32[]{:S(2)}, u32[]{:S(2)}) collective-permute-start(bf16[2,4096]{1,0:T(2,128)(2,1)S(1)} %copy.179), channel_id=1, source_target_pairs={{4,0},{8,4},{12,8},{16,12},{20,16},{24,20},{28,24},{5,1},{9,5},{13... | collective-permute-start | bytes 49160 | tf_op jit(solution)/shard_map/ppermute | solution.py:12
  379.0 2.2 copy-start.13
  381.2 14.6 %copy-start.15 = (f32[128,16,512]{2,0,1:T(8,128)S(1)}, f32[128,16,512]{2,0,1:T(8,128)}, u32[]{:S(2)}) copy-start(f32[128,16,512]{2,0,1:T(8,128)} %get-tuple-element.24) | copy-start | bytes 12582916
  392.1 8.2 %copy-start.14 = (f32[128,16,512]{2,0,1:T(8,128)S(1)}, f32[128,16,512]{2,0,1:T(8,128)}, u32[]{:S(2)}) copy-start(f32[128,16,512]{2,0,1:T(8,128)} %get-tuple-element.23) | copy-start | bytes 12582916
  392.1 26.5 %collective-permute-start.4 = (bf16[1,128,4096]{1,2,0:T(8,128)(2,1)S(1)}, bf16[1,128,4096]{1,2,0:T(8,128)(2,1)S(1)}, u32[]{:S(2)}, u32[]{:S(2)}) collective-permute-start(bf16[1,128,4096]{1,2,0:T(8,128)(2,1)S(1)} %fusion.88), channel_id=1, source_target_pairs={{1,0},{2,1},{3,2},{0,3},{5,4},{6,5},{7,6},{4,7},{9,8},{10,9},{11,1... | collective-permute-start | bytes 3145736 | tf_op jit(solution)/shard_map/ppermute | solution.py:18
  400.3 19.6 %copy-start.1 = (f32[1,1024,512]{2,1,0:T(8,128)S(1)}, f32[1,1024,512]{2,1,0:T(8,128)}, u32[]{:S(2)}) copy-start(f32[1,1024,512]{2,1,0:T(8,128)} %param.6) | copy-start | bytes 6291460
where the time goes:
time: 425 us; the launch traced here: 420 us
  matrix products  256 us (60%)
  waiting for transfers between devices  68.1 us (16%)
  local copies, waits for them, and re-layouts  33.7 us (8%)
  other arithmetic  32.5 us (8%)
  starting transfers between devices  28.8 us (7%)
    dot_general x36, matrix products, highest(): jnp.einsum(pattern, first_op, second_op, precision=lax.Precision.HIGHEST)  256 us
    all_to_all x1, waiting for transfers between devices, shards(): lax.all_to_all(adjoint, 'seq', split_axis=1, concat_axis=0, tiled=True)  23.8 us
    all_to_all x1, waiting for transfers between devices, shards(): lax.all_to_all(back_cols, 'seq', split_axis=0, concat_axis=1, tiled=True)  20.2 us
    all_to_all x1, waiting for transfers between devices, shards(): lax.all_to_all(mixed_cols, 'seq', split_axis=0, concat_axis=1, tiled=True)  12.6 us
    ppermute x1, waiting for transfers between devices, shifted(): return lax.ppermute(block, axis, route)  11.3 us
    broadcast_in_dim x1, other arithmetic, shards(): received = shifted(grad_input[None], 'pipe', -1)  10.9 us
  transfers between devices with their start and end apart: 9, of which 5 were waited for; matrix products, arithmetic and copies ran while one was open for 19% of the time, Pallas kernels for 0%

commit v1 on v0

v1 whole, which is shorter than its diff:
```python
import math

import jax
import jax.numpy as jnp
import numpy as np
from jax import lax
from jax.experimental import pallas as pl
from jax.experimental.pallas import tpu as pltpu
from jax.sharding import PartitionSpec as P

FREQ_BLOCK = 256
ROW_BLOCK = 256
STEP = 32
DENSE_ROWS = 1024
VMEM_BYTES = 56 * 1024 * 1024


def angle_tables(rows):
    def pair(outer, inner):
        angles = 2.0 * np.pi / (4 * rows) * (np.outer(outer, inner) % (4 * rows))
        return np.cos(angles), np.sin(angles)

    places = np.arange(rows)
    freqs = 4 * np.arange(rows) + 1
    coarse = STEP * np.arange(rows // STEP)
    fine = np.arange(STEP)
    by_place = pair(4 * coarse, places) + pair(4 * fine + 1, places)
    by_freq = pair(coarse, freqs) + pair(fine, freqs)
    return np.stack(by_place).astype(np.float32), np.stack(by_freq).astype(np.float32)


def turned(coarse_cos, coarse_sin, fine_cos, fine_sin):
    real = coarse_cos * fine_cos - coarse_sin * fine_sin
    imag = coarse_sin * fine_cos + coarse_cos * fine_sin
    return real, -imag


def table_kernel(place_ref, freq_ref, kernel_ref, fwd_ref, inv_ref, spec_ref, kernel_low):
    step = pl.program_id(0)
    rows = place_ref.shape[2]
    freq_block = fwd_ref.shape[0] // 2
    row_block = inv_ref.shape[0]

    @pl.when(step == 0)
    def _():
        kernel_low[...] = kernel_ref[...].astype(jnp.bfloat16)

    for part in range(freq_block // STEP):
        coarse = step * (freq_block // STEP) + part
        real, imag = turned(
            place_ref[0, pl.ds(coarse, 1), :],
            place_ref[1, pl.ds(coarse, 1), :],
            place_ref[2],
            place_ref[3],
        )
        fwd_ref[part * STEP : (part + 1) * STEP, :] = real.astype(jnp.bfloat16)
        fwd_ref[freq_block + part * STEP : freq_block + (part + 1) * STEP, :] = imag.astype(
            jnp.bfloat16
        )
    for part in range(row_block // STEP):
        coarse = step * (row_block // STEP) + part
        real, imag = turned(
            freq_ref[0, pl.ds(coarse, 1), :],
            freq_ref[1, pl.ds(coarse, 1), :],
            freq_ref[2],
            freq_ref[3],
        )
        real = (real * (1.0 / rows)).astype(jnp.bfloat16)
        imag = (imag * (1.0 / rows)).astype(jnp.bfloat16)
        for block in range(rows // freq_block):
            start = 2 * block * freq_block
            source = slice(block * freq_block, (block + 1) * freq_block)
            into = slice(part * STEP, (part + 1) * STEP)
            inv_ref[into, start : start + freq_block] = real[:, source]
            inv_ref[into, start + freq_block : start + 2 * freq_block] = imag[:, source]
    spec_ref[...] = jnp.dot(fwd_ref[...], kernel_low[...], preferred_element_type=jnp.float32)


def tables(kernel):
    rows, width = kernel.shape
    by_place, by_freq = angle_tables(rows)
    steps = rows // FREQ_BLOCK
    whole = lambda step: (0, 0, 0)
    return pl.pallas_call(
        table_kernel,
        grid=(steps,),
        in_specs=[
            pl.BlockSpec(by_place.shape, whole),
            pl.BlockSpec(by_freq.shape, whole),
            pl.BlockSpec((rows, width), lambda step: (0, 0)),
        ],
        out_specs=[
            pl.BlockSpec((2 * FREQ_BLOCK, rows), lambda step: (step, 0)),
            pl.BlockSpec((ROW_BLOCK, 2 * rows), lambda step: (step, 0)),
            pl.BlockSpec((2 * FREQ_BLOCK, width), lambda step: (step, 0)),
        ],
        out_shape=[
            jax.ShapeDtypeStruct((2 * rows, rows), jnp.bfloat16),
            jax.ShapeDtypeStruct((rows, 2 * rows), jnp.bfloat16),
            jax.ShapeDtypeStruct((2 * rows, width), jnp.float32),
        ],
        scratch_shapes=[pltpu.VMEM((rows, width), jnp.bfloat16)],
        compiler_params=pltpu.CompilerParams(vmem_limit_bytes=VMEM_BYTES),
        cost_estimate=pl.CostEstimate(
            flops=4 * rows * rows * width, bytes_accessed=16 * rows * rows, transcendentals=0
        ),
        name="tables",
    )(jnp.asarray(by_place), jnp.asarray(by_freq), kernel)


PAD = 8
CHUNK = 64


def section_kernel(
    x_ref, g_ref, tap_ref, fwd_ref, inv_ref, spec_ref,
    out_ref, filt_ref,
    padded, signals, key_rows, value_rows, mixed, later,
):
    step = pl.program_id(0)
    rows, width = x_ref.shape
    freq_block = fwd_ref.shape[0] // 2
    row_block = inv_ref.shape[0]
    freq_steps = rows // freq_block
    row_steps = rows // row_block

    @pl.when(step == 0)
    def _():
        padded[0:PAD, :] = jnp.zeros((PAD, width), jnp.float32)
        padded[PAD:, :] = x_ref[...].astype(jnp.float32)
        taps = [tap_ref[i : i + 1, :] for i in range(9)]

        @pl.loop(0, rows // CHUNK)
        def _(chunk):
            start = pl.multiple_of(chunk * CHUNK, CHUNK)
            window = padded[pl.ds(start, CHUNK + PAD), :]
            moved = [window[PAD - i : PAD - i + CHUNK, :] for i in range(3)]
            query, key, value = (
                (taps[3 * s] * moved[0] + taps[3 * s + 1] * moved[1] + taps[3 * s + 2] * moved[2])
                .astype(jnp.bfloat16)
                .astype(jnp.float32)
                for s in range(3)
            )
            here = pl.ds(start, CHUNK)
            key_rows[here, :] = key
            value_rows[here, :] = value
            signals[here, 0:width] = (key * value).astype(jnp.bfloat16)
            signals[here, width:] = (g_ref[here, :].astype(jnp.float32) * query).astype(
                jnp.bfloat16
            )

        later[...] = jnp.zeros(later.shape, jnp.float32)

    @pl.when(step < freq_steps)
    def _():
        both = jnp.dot(fwd_ref[...], signals[...], preferred_element_type=jnp.float32)
        p_re, p_im = both[:freq_block, :width], both[freq_block:, :width]
        a_re, a_im = both[:freq_block, width:], both[freq_block:, width:]
        h_re, h_im = spec_ref[:freq_block, :], spec_ref[freq_block:, :]
        start = pl.multiple_of(step * 2 * freq_block, 2 * freq_block)
        reals, imags = pl.ds(start, freq_block), pl.ds(start + freq_block, freq_block)
        mixed[reals, 0:width] = (p_re * h_re - p_im * h_im).astype(jnp.bfloat16)
        mixed[imags, 0:width] = (p_re * h_im + p_im * h_re).astype(jnp.bfloat16)
        mixed[reals, width : 2 * width] = (h_re * a_re + h_im * a_im).astype(jnp.bfloat16)
        mixed[imags, width : 2 * width] = (h_re * a_im - h_im * a_re).astype(jnp.bfloat16)
        mixed[reals, 2 * width :] = (p_re * a_re + p_im * a_im).astype(jnp.bfloat16)
        mixed[imags, 2 * width :] = (p_re * a_im - p_im * a_re).astype(jnp.bfloat16)

    @pl.when(step >= freq_steps)
    def _():
        block = row_steps - 1 - (step - freq_steps)
        start = pl.multiple_of(block * row_block, row_block)
        here = pl.ds(start, row_block)
        result = jnp.dot(inv_ref[...], mixed[...], preferred_element_type=jnp.float32)
        combined, backward = result[:, 0:width], result[:, width : 2 * width]
        filt_ref[...] = result[:, 2 * width :] * (1.0 / math.sqrt(rows))
        low = lambda v: v.astype(jnp.bfloat16).astype(jnp.float32)
        grads = (
            low(g_ref[here, :].astype(jnp.float32) * combined),
            low(backward * value_rows[here, :]),
            low(backward * key_rows[here, :]),
        )
        shifts = []
        for i in range(3):
            shifts.append(
                tap_ref[i : i + 1, :] * grads[0]
                + tap_ref[3 + i : 4 + i, :] * grads[1]
                + tap_ref[6 + i : 7 + i, :] * grads[2]
            )
        for i in (1, 2):
            later[i - 1, 0:row_block, :] = shifts[i]
        total = shifts[0] + later[0, 1 : 1 + row_block, :] + later[1, 2 : 2 + row_block, :]
        out_ref[...] = total.astype(jnp.bfloat16)
        for i in (1, 2):
            later[i - 1, row_block : row_block + PAD, :] = shifts[i][0:PAD, :]


def section(x, g, taps, fwd, inv, spec):
    rows, width = x.shape
    freq_steps, row_steps = rows // FREQ_BLOCK, rows // ROW_BLOCK
    forward = lambda step: (jnp.minimum(step, freq_steps - 1), 0)
    inverse = lambda step: (row_steps - 1 - jnp.maximum(step - freq_steps, 0), 0)
    once = lambda step: (0, 0)
    return pl.pallas_call(
        section_kernel,
        grid=(freq_steps + row_steps,),
        in_specs=[
            pl.BlockSpec((rows, width), once),
            pl.BlockSpec((rows, width), once),
            pl.BlockSpec(taps.shape, once),
            pl.BlockSpec((2 * FREQ_BLOCK, rows), forward),
            pl.BlockSpec((ROW_BLOCK, 2 * rows), inverse),
            pl.BlockSpec((2 * FREQ_BLOCK, width), forward),
        ],
        out_specs=[
            pl.BlockSpec((ROW_BLOCK, width), inverse),
            pl.BlockSpec((ROW_BLOCK, width), inverse),
        ],
        out_shape=[
            jax.ShapeDtypeStruct((rows, width), jnp.bfloat16),
            jax.ShapeDtypeStruct((rows, width), jnp.float32),
        ],
        scratch_shapes=[
            pltpu.VMEM((rows + PAD, width), jnp.float32),
            pltpu.VMEM((rows, 2 * width), jnp.bfloat16),
            pltpu.VMEM((rows, width), jnp.float32),
            pltpu.VMEM((rows, width), jnp.float32),
            pltpu.VMEM((2 * rows, 3 * width), jnp.bfloat16),
            pltpu.VMEM((2, ROW_BLOCK + PAD, width), jnp.float32),
        ],
        compiler_params=pltpu.CompilerParams(vmem_limit_bytes=VMEM_BYTES),
        cost_estimate=pl.CostEstimate(
            flops=20 * rows * rows * width,
            bytes_accessed=8 * rows * rows + 20 * rows * width,
            transcendentals=0,
        ),
        name="section",
    )(x, g, taps, fwd, inv, spec)


def phase_table(row_count, col_count, modulus, direction):
    row_ids = lax.broadcasted_iota(jnp.int32, (row_count, col_count), 0)
    col_ids = lax.broadcasted_iota(jnp.int32, (row_count, col_count), 1)
    residue = row_ids * col_ids % modulus
    angles = direction * 2.0 * math.pi / modulus * residue.astype(jnp.float32)
    return (jnp.cos(angles), jnp.sin(angles))


def highest(pattern, first_op, second_op):
    return jnp.einsum(pattern, first_op, second_op, precision=lax.Precision.HIGHEST)


def forward_spectrum(signal, half_q, width_p):
    full_q = 2 * half_q
    blocks = signal.reshape(half_q, width_p, signal.shape[1])
    fq_re, fq_im = phase_table(full_q, half_q, full_q, -1.0)
    section_re = highest("kq,qpc->kpc", fq_re, blocks)
    section_im = highest("kq,qpc->kpc", fq_im, blocks)
    tw_re, tw_im = phase_table(full_q, width_p, full_q * width_p, -1.0)
    turned_re = section_re * tw_re[:, :, None] - section_im * tw_im[:, :, None]
    turned_im = section_re * tw_im[:, :, None] + section_im * tw_re[:, :, None]
    fp_re, fp_im = phase_table(width_p, width_p, width_p, -1.0)
    out_re = highest("jp,kpc->jkc", fp_re, turned_re) - highest("jp,kpc->jkc", fp_im, turned_im)
    out_im = highest("jp,kpc->jkc", fp_re, turned_im) + highest("jp,kpc->jkc", fp_im, turned_re)
    return (out_re, out_im)


def inverse_field(spec_re, spec_im, half_q, width_p):
    full_q = 2 * half_q
    gp_re, gp_im = phase_table(width_p, width_p, width_p, 1.0)
    section_re = highest("mn,nqc->mqc", gp_re, spec_re) - highest("mn,nqc->mqc", gp_im, spec_im)
    section_im = highest("mn,nqc->mqc", gp_re, spec_im) + highest("mn,nqc->mqc", gp_im, spec_re)
    tw_re, tw_im = phase_table(width_p, full_q, full_q * width_p, 1.0)
    turned_re = section_re * tw_re[:, :, None] - section_im * tw_im[:, :, None]
    turned_im = section_re * tw_im[:, :, None] + section_im * tw_re[:, :, None]
    gq_re, gq_im = phase_table(half_q, full_q, full_q, 1.0)
    result = highest("aq,mqc->amc", gq_re, turned_re) - highest("aq,mqc->amc", gq_im, turned_im)
    return result.reshape(half_q * width_p, spec_re.shape[2]) / (full_q * width_p)


def large_section(x, g, taps, kernel, half_q):
    rows = x.shape[0]
    width_p = rows // half_q
    signal, upstream = x.astype(jnp.float32), g.astype(jnp.float32)
    moved = [jnp.pad(signal, ((i, 0), (0, 0)))[:rows] for i in range(3)]
    query, key, value = (
        sum(taps[3 * s + i] * moved[i] for i in range(3)).astype(jnp.bfloat16).astype(jnp.float32)
        for s in range(3)
    )
    p_re, p_im = forward_spectrum(key * value, half_q, width_p)
    a_re, a_im = forward_spectrum(upstream * query, half_q, width_p)
    h_re, h_im = forward_spectrum(kernel, half_q, width_p)
    combined = inverse_field(
        p_re * h_re - p_im * h_im, p_re * h_im + p_im * h_re, half_q, width_p
    )
    backward = inverse_field(
        h_re * a_re + h_im * a_im, h_re * a_im - h_im * a_re, half_q, width_p
    )
    filter_grad = inverse_field(
        p_re * a_re + p_im * a_im, p_re * a_im - p_im * a_re, half_q, width_p
    )
    grads = (upstream * combined, backward * value, backward * key)
    total = jnp.zeros_like(signal)
    for s in range(3):
        grad = grads[s].astype(jnp.bfloat16).astype(jnp.float32)
        for i in range(3):
            total = total + taps[3 * s + i] * jnp.pad(grad, ((0, i), (0, 0)))[i:]
    return total.astype(jnp.bfloat16), filter_grad * (1.0 / math.sqrt(rows))


def shards(section_input, out_grad, conv_filter, short_taps):
    inputs, upstream, kernel = section_input[0], out_grad[0], conv_filter[0]
    devices = lax.axis_size("seq")
    length_dev, model = inputs.shape
    rows, width = kernel.shape
    assert rows == length_dev * devices and model == width * devices
    me = lax.axis_index("seq")
    taps = lax.dynamic_slice_in_dim(short_taps[0].reshape(9, model), me * width, width, axis=1)
    to_columns = lambda block: block.reshape(length_dev, devices, width).transpose(1, 0, 2)
    sent = jnp.stack([to_columns(inputs), to_columns(upstream)], axis=1)
    got = lax.all_to_all(sent, "seq", split_axis=0, concat_axis=0, tiled=True)
    x_cols = got[:, 0].reshape(rows, width)
    g_cols = got[:, 1].reshape(rows, width)
    if rows <= DENSE_ROWS:
        fwd, inv, spec = tables(kernel)
        grad_cols, filter_grad = section(x_cols, g_cols, taps, fwd, inv, spec)
    else:
        grad_cols, filter_grad = large_section(x_cols, g_cols, taps, kernel, devices)
    back = lax.all_to_all(
        grad_cols.reshape(devices, length_dev, width), "seq", split_axis=0, concat_axis=0, tiled=True
    )
    grad_input = back.transpose(1, 0, 2).reshape(length_dev, model)
    count = lax.axis_size("pipe")
    received = lax.ppermute(
        grad_input[None], "pipe", [((i + 1) % count, i) for i in range(count)]
    )
    return received, filter_grad[None]


def solution(mesh):
    return jax.shard_map(
        shards,
        mesh=mesh,
        in_specs=(
            P("pipe", "seq", None),
            P("pipe", "seq", None),
            P("pipe", None, "seq"),
            P("pipe", None, None, None),
        ),
        out_specs=(P("pipe", "seq", None), P("pipe", None, "seq")),
        check_vma=False,
    )
```

time: 425 us -> 110 us (0.26); the launches traced: 420 us -> 109 us
  matrix products: 256 us -> 0 us
  Pallas kernels: 0 us -> 30.8 us
  other arithmetic: 32.5 us -> 1.81 us
  waiting for transfers between devices: 68.1 us -> 38.4 us
  local copies, waits for them, and re-layouts: 33.7 us -> 9.97 us
  starting transfers between devices: 28.8 us -> 8.96 us
  blocking collectives: 0 us -> 18.8 us
    dot_general x36 -> x0, matrix products: 256 us -> none  [highest(): jnp.einsum(pattern, first_op, second_op, precision=lax.Precision.HIGHEST)]
    all_to_all x4 -> x1, waiting for transfers between devices: 56.9 us -> 16.6 us  [shards(): got = lax.all_to_all(sent, 'seq', split_axis=0, concat_axis=0, tiled=True)]
    pallas_call x0 -> x2, Pallas kernels: none -> 30.8 us  [the longest x1 21.9 us: section(): pl.pallas_call(section_kernel, grid=(freq_steps + row_steps,), in_specs=[...]
    all_to_all x0 -> x1, blocking collectives: none -> 18.8 us  [shards(): lax.all_to_all(grad_cols.reshape(devices, length_dev, width), 'seq', spli...]
    all_to_all x4 -> x1, starting transfers between devices: 18.7 us -> 5.3 us  [shards(): got = lax.all_to_all(sent, 'seq', split_axis=0, concat_axis=0, tiled=True)]
    convert_element_type x6 -> x0, other arithmetic: 13 us -> none  [the longest x3 6.32 us: shards(): jnp.concatenate([grad_list[stream_idx], later_rows[stream_idx]], axis=0)]
    all_to_all x4 -> x0, local copies, waits for them, and re-layouts: 11.7 us -> none  [the longest x1 2.94 us: shards(): lax.all_to_all(mixed_cols, 'seq', split_axis=0, concat_axis=1, tiled=True)]
    broadcast_in_dim x1 -> x0, other arithmetic: 10.9 us -> none  [shards(): received = shifted(grad_input[None], 'pipe', -1)]
  transfers between devices with their start and end apart: 9 -> 2, of which waited for: 5 -> 2; matrix products, arithmetic and copies ran while one was open for 19% -> 1% of each run, Pallas kernels for 0% -> 8%
where the time goes in v1:
time: 110 us; the launch traced here: 109 us
  waiting for transfers between devices  38.4 us (35%)
  Pallas kernels  30.8 us (28%)
  blocking collectives  18.8 us (17%)
  local copies, waits for them, and re-layouts  9.97 us (9%)
  starting transfers between devices  8.96 us (8%)
  other arithmetic  1.81 us (2%)
    pallas_call x1, Pallas kernels, section(): pl.pallas_call(section_kernel, grid=(freq_steps + row_steps,), in_specs=[...  21.9 us
    ppermute x1, waiting for transfers between devices, shards(): lax.ppermute(grad_input[None], 'pipe', [((i + 1) % count, i) for i in ran...  21.8 us
    all_to_all x1, blocking collectives, shards(): lax.all_to_all(grad_cols.reshape(devices, length_dev, width), 'seq', spli...  18.8 us
    all_to_all x1, waiting for transfers between devices, shards(): got = lax.all_to_all(sent, 'seq', split_axis=0, concat_axis=0, tiled=True)  16.6 us
    pallas_call x1, Pallas kernels, tables(): pl.pallas_call(table_kernel, grid=(steps,), in_specs=[pl.BlockSpec(by_pla...  8.95 us
    all_to_all x1, starting transfers between devices, shards(): got = lax.all_to_all(sent, 'seq', split_axis=0, concat_axis=0, tiled=True)  5.3 us
    unnamed x7, local copies, waits for them, and re-layouts  3.99 us
    ppermute x1, starting transfers between devices, shards(): lax.ppermute(grad_input[None], 'pipe', [((i + 1) % count, i) for i in ran...  3.66 us
  transfers between devices with their start and end apart: 2, of which 2 were waited for; matrix products, arithmetic and copies ran while one was open for 1% of the time, Pallas kernels for 8%

profile of v1, /device:TPU:0, one launch (start us, length us, event | category | flops | bytes accessed | tf_op | source)
XLA Modules:
  0.0 109.4 jit_solution(12694734857605713311)
XLA Ops:
  0.6 0.0 copy-start
  0.6 1.7 %copy.12 = bf16[1,128,4096]{1,2,0:T(8,128)(2,1)S(1)} copy(bf16[1,128,4096]{2,1,0:T(8,128)(2,1)} %param.6) | data formatting | bytes 2097152 | tf_op args[0]
  2.4 0.0 copy-done
  2.4 1.3 %copy.13 = bf16[1,128,4096]{1,2,0:T(8,128)(2,1)} copy(bf16[1,128,4096]{2,1,0:T(8,128)(2,1)S(1)} %copy-done) | data formatting | bytes 2097152 | tf_op args[1]
  3.7 1.4 %pad_maximum_fusion = bf16[8,2,128,512]{2,3,0,1:T(8,128)(2,1)S(1)} fusion(bf16[8,1,128,512]{2,3,0,1:T(8,128)(2,1)} %bitcast.18, bf16[8,1,128,512]{2,3,0,1:T(8,128)(2,1)S(1)} %bitcast.17), kind=kLoop, calls=%fused_computation | loop fusion | flops 1048576 | bytes 4194304 | tf_op jit(solution)/shard_map/stack | solution.py:320
  5.1 2.6 %copy.14 = bf16[8,2,128,512]{3,2,1,0:T(8,128)(2,1)} copy(bf16[8,2,128,512]{2,3,0,1:T(8,128)(2,1)S(1)} %pad_maximum_fusion) | data formatting | bytes 4194304 | tf_op jit(solution)/shard_map/stack | solution.py:320
  7.7 0.0 copy-start.1
  7.7 5.3 %all-to-all-start = ((bf16[8,2,128,512]{3,2,1,0:T(8,128)(2,1)}), bf16[8,2,128,512]{3,2,1,0:T(8,128)(2,1)S(1)}, u32[]{:S(2)}, u32[]{:S(2)}) async-start(bf16[8,2,128,512]{3,2,1,0:T(8,128)(2,1)} %copy.14), calls=%async_computation | async-start | bytes 4194304 | tf_op jit(solution)/shard_map/all_to_all | solution.py:321
  13.0 0.0 copy-done.1
  13.0 0.4 reduce
  13.4 0.1 reshape_squeeze.19
  13.5 0.6 constant_dynamic-slice_fusion.tap_ref
  14.1 8.9 %tables.1 = (bf16[2048,1024]{1,0:T(8,128)(2,1)}, bf16[1024,2048]{1,0:T(8,128)(2,1)}, f32[2048,512]{1,0:T(8,128)}) custom-call(f32[4,32,1024]{2,1,0:T(8,128)} %constant.16.clone.place_ref, f32[4,32,1024]{2,1,0:T(8,128)} %constant.17.clone.freq_ref, f32[1024,512]{1,0:T(8,128)} %bitcast.22), custom_call_target="tpu_custom_call" | custom-call | flops 2147483648 | bytes 16777216 | tf_op jit(solution)/shard_map/tables/pallas_call | solution.py:84
  23.0 16.6 %all-to-all-done = bf16[8,2,128,512]{3,2,1,0:T(8,128)(2,1)S(1)} async-done(((bf16[8,2,128,512]{3,2,1,0:T(8,128)(2,1)}), bf16[8,2,128,512]{3,2,1,0:T(8,128)(2,1)S(1)}, u32[]{:S(2)}, u32[]{:S(2)}) %all-to-all-start) | async-done | bytes 2097184 | tf_op jit(solution)/shard_map/all_to_all | solution.py:321
  39.6 1.6 %fusion = (bf16[8,1,128,512]{3,2,1,0:T(8,128)(2,1)}, bf16[8,1,128,512]{3,2,1,0:T(8,128)(2,1)}) fusion(bf16[8,2,128,512]{3,2,1,0:T(8,128)(2,1)S(1)} %all-to-all-done), kind=kLoop, calls=%fused_computation.2 | loop fusion | bytes 4194304 | tf_op jit(solution)/shard_map/slice | solution.py:323
  41.2 21.9 %section.1 = (bf16[1024,512]{1,0:T(8,128)(2,1)}, f32[1024,512]{1,0:T(8,128)}) custom-call(bf16[1024,512]{1,0:T(8,128)(2,1)} %bitcast.21, bf16[1024,512]{1,0:T(8,128)(2,1)} %bitcast.20, f32[9,512]{1,0:T(8,128)} %constant_dynamic-slice_fusion.tap_ref, bf16[2048,1024]{1,0:T(8,128)(2,1)} %get-tuple-element.7.fwd_ref, ...), custom_call_target="tpu_custom_call" | custom-call | flops 10737418240 | bytes 18874368 | tf_op jit(solution)/shard_map/section/pallas_call | solution.py:204
  63.1 18.8 %all_to_all.10 = bf16[8,128,512]{2,1,0:T(8,128)(2,1)S(1)} all-to-all(bf16[8,128,512]{2,1,0:T(8,128)(2,1)} %bitcast.19), channel_id=1, replica_groups=mesh['seq'=8,'pipe'=4] {'seq'}, dimensions={0} | all-to-all | bytes 2097152 | tf_op jit(solution)/shard_map/all_to_all | solution.py:329
  81.9 0.6 copy.15
  82.5 0.5 broadcast_in_dim_reshape.3
  83.0 3.7 %collective-permute-start = (bf16[1,128,4096]{2,1,0:T(8,128)(2,1)S(1)}, bf16[1,128,4096]{2,1,0:T(8,128)(2,1)S(1)}, u32[]{:S(2)}, u32[]{:S(2)}) collective-permute-start(bf16[1,128,4096]{2,1,0:T(8,128)(2,1)S(1)} %broadcast_in_dim_reshape.3), channel_id=1, source_target_pairs={{1,0},{2,1},{3,2},{0,3},{5,4},{6,5},{7,6},{4,7},{9,8},{10,9},{11,1... | collective-permute-start | bytes 3145736 | tf_op jit(solution)/shard_map/ppermute | solution.py:334
  86.7 21.8 %collective-permute-done = bf16[1,128,4096]{2,1,0:T(8,128)(2,1)S(1)} collective-permute-done((bf16[1,128,4096]{2,1,0:T(8,128)(2,1)S(1)}, bf16[1,128,4096]{2,1,0:T(8,128)(2,1)S(1)}, u32[]{:S(2)}, u32[]{:S(2)}) %collective-permute-start) | collective-permute-done | bytes 1048608 | tf_op jit(solution)/shard_map/ppermute | solution.py:334
  108.4 1.0 copy.18
Async XLA Ops:
  0.6 1.7 %copy-start = (bf16[1,128,4096]{2,1,0:T(8,128)(2,1)S(1)}, bf16[1,128,4096]{2,1,0:T(8,128)(2,1)}, u32[]{:S(2)}) copy-start(bf16[1,128,4096]{2,1,0:T(8,128)(2,1)} %param.7) | copy-start | bytes 3145732
  7.7 5.3 %copy-start.1 = (f32[1,3,3,4096]{3,0,2,1:T(1,128)S(1)}, f32[1,3,3,4096]{3,0,2,1:T(1,128)}, u32[]{:S(2)}) copy-start(f32[1,3,3,4096]{3,0,2,1:T(1,128)} %param.9) | copy-start | bytes 442372
  7.7 31.9 %all-to-all-start = ((bf16[8,2,128,512]{3,2,1,0:T(8,128)(2,1)}), bf16[8,2,128,512]{3,2,1,0:T(8,128)(2,1)S(1)}, u32[]{:S(2)}, u32[]{:S(2)}) async-start(bf16[8,2,128,512]{3,2,1,0:T(8,128)(2,1)} %copy.14), calls=%async_computation | async-start | bytes 4194304 | tf_op jit(solution)/shard_map/all_to_all | solution.py:321
  83.0 25.4 %collective-permute-start = (bf16[1,128,4096]{2,1,0:T(8,128)(2,1)S(1)}, bf16[1,128,4096]{2,1,0:T(8,128)(2,1)S(1)}, u32[]{:S(2)}, u32[]{:S(2)}) collective-permute-start(bf16[1,128,4096]{2,1,0:T(8,128)(2,1)S(1)} %broadcast_in_dim_reshape.3), channel_id=1, source_target_pairs={{1,0},{2,1},{3,2},{0,3},{5,4},{6,5},{7,6},{4,7},{9,8},{10,9},{11,1... | collective-permute-start | bytes 3145736 | tf_op jit(solution)/shard_map/ppermute | solution.py:334

commit v2 on v1

--- a/solution.py
+++ b/solution.py
@@ -1,3 +1,4 @@
+import functools
 import math
 
 import jax
@@ -112,22 +113,107 @@
 CHUNK = 64
 
 
-def section_kernel(
-    x_ref, g_ref, tap_ref, fwd_ref, inv_ref, spec_ref,
-    out_ref, filt_ref,
-    padded, signals, key_rows, value_rows, mixed, later,
-):
+def in_then_out(moves, held, in_sem, out_sem):
+    arriving = [pltpu.make_async_copy(a, held.at[i], in_sem.at[i]) for i, (a, _) in enumerate(moves)]
+    leaving = [pltpu.make_async_copy(held.at[i], b, out_sem.at[i]) for i, (_, b) in enumerate(moves)]
+    for copy in arriving:
+        copy.start()
+    for first, second in zip(arriving, leaving):
+        first.wait()
+        second.start()
+    for copy in leaving:
+        copy.wait()
+
+
+def pack_kernel(x_ref, g_ref, *refs):
+    pieces, scratch = refs[:-3], refs[-3:]
+    devices = lax.axis_size("seq")
+    width = pieces[0].shape[2]
+    chunks = len(pieces) // devices
+    me = lax.axis_index("seq")
+    moves = []
+    for number, piece in enumerate(pieces):
+        chunk, k = divmod(number, devices)
+        start = pl.multiple_of(((me ^ k) * chunks + chunk) * width, width)
+        for half, ref in enumerate((x_ref, g_ref)):
+            moves.append((ref.at[:, pl.ds(start, width)], piece.at[half]))
+    in_then_out(moves, *scratch)
+
+
+def pack(x, g, devices, chunks):
+    length, model = x.shape
+    width = model // devices // chunks
+    count = devices * chunks
+    anywhere = pl.BlockSpec(memory_space=pl.ANY)
+    pieces = pl.pallas_call(
+        pack_kernel,
+        in_specs=[anywhere] * 2,
+        out_specs=[anywhere] * count,
+        out_shape=[jax.ShapeDtypeStruct((2, length, width), x.dtype)] * count,
+        scratch_shapes=[
+            pltpu.VMEM((2 * count, length, width), x.dtype),
+            pltpu.SemaphoreType.DMA((2 * count,)),
+            pltpu.SemaphoreType.DMA((2 * count,)),
+        ],
+        name="pack",
+    )(x, g)
+    return [pieces[c * devices : (c + 1) * devices] for c in range(chunks)]
+
+
+def unpack_kernel(*refs):
+    pieces, out_ref, scratch = refs[:-4], refs[-4], refs[-3:]
+    devices = lax.axis_size("seq")
+    width = pieces[0].shape[1]
+    chunks = len(pieces) // devices
+    me = lax.axis_index("seq")
+    moves = []
+    for number, piece in enumerate(pieces):
+        chunk, k = divmod(number, devices)
+        start = pl.multiple_of(((me ^ k) * chunks + chunk) * width, width)
+        moves.append((piece, out_ref.at[0, :, pl.ds(start, width)]))
+    in_then_out(moves, *scratch)
+
+
+def unpack(pieces):
+    flat = [piece for chunk in pieces for piece in chunk]
+    length, width = flat[0].shape
+    anywhere = pl.BlockSpec(memory_space=pl.ANY)
+    return pl.pallas_call(
+        unpack_kernel,
+        in_specs=[anywhere] * len(flat),
+        out_specs=anywhere,
+        out_shape=jax.ShapeDtypeStruct((1, length, width * len(flat)), flat[0].dtype),
+        scratch_shapes=[
+            pltpu.VMEM((len(flat), length, width), flat[0].dtype),
+            pltpu.SemaphoreType.DMA((len(flat),)),
+            pltpu.SemaphoreType.DMA((len(flat),)),
+        ],
+        name="unpack",
+    )(*flat)
+
+
+def section_kernel(devices, aliased, *refs):
+    pieces, refs = refs[:devices], refs[devices:]
+    tap_ref, fwd_ref, inv_ref, spec_ref = refs[:4]
+    refs = refs[4 + aliased :]
+    outs, refs = refs[:devices], refs[devices:]
+    filt_ref, padded, upstream, signals, key_rows, value_rows, mixed, later, grad_rows = refs
     step = pl.program_id(0)
-    rows, width = x_ref.shape
+    me = lax.axis_index("seq")
+    length, width = outs[0].shape
+    rows = length * devices
     freq_block = fwd_ref.shape[0] // 2
     row_block = inv_ref.shape[0]
     freq_steps = rows // freq_block
     row_steps = rows // row_block
+    place = lambda k, offset: pl.ds(pl.multiple_of((me ^ k) * length + offset, 8), length)
 
     @pl.when(step == 0)
     def _():
         padded[0:PAD, :] = jnp.zeros((PAD, width), jnp.float32)
-        padded[PAD:, :] = x_ref[...].astype(jnp.float32)
+        for k in range(devices):
+            padded[place(k, PAD), :] = pieces[k][0].astype(jnp.float32)
+            upstream[place(k, 0), :] = pieces[k][1].astype(jnp.float32)
         taps = [tap_ref[i : i + 1, :] for i in range(9)]
 
         @pl.loop(0, rows // CHUNK)
@@ -145,9 +231,7 @@
             key_rows[here, :] = key
             value_rows[here, :] = value
             signals[here, 0:width] = (key * value).astype(jnp.bfloat16)
-            signals[here, width:] = (g_ref[here, :].astype(jnp.float32) * query).astype(
-                jnp.bfloat16
-            )
+            signals[here, width:] = (upstream[here, :] * query).astype(jnp.bfloat16)
 
         later[...] = jnp.zeros(later.shape, jnp.float32)
 
@@ -176,58 +260,65 @@
         filt_ref[...] = result[:, 2 * width :] * (1.0 / math.sqrt(rows))
         low = lambda v: v.astype(jnp.bfloat16).astype(jnp.float32)
         grads = (
-            low(g_ref[here, :].astype(jnp.float32) * combined),
+            low(upstream[here, :] * combined),
             low(backward * value_rows[here, :]),
             low(backward * key_rows[here, :]),
         )
-        shifts = []
-        for i in range(3):
-            shifts.append(
-                tap_ref[i : i + 1, :] * grads[0]
-                + tap_ref[3 + i : 4 + i, :] * grads[1]
-                + tap_ref[6 + i : 7 + i, :] * grads[2]
-            )
+        shifts = [
+            tap_ref[i : i + 1, :] * grads[0]
+            + tap_ref[3 + i : 4 + i, :] * grads[1]
+            + tap_ref[6 + i : 7 + i, :] * grads[2]
+            for i in range(3)
+        ]
         for i in (1, 2):
             later[i - 1, 0:row_block, :] = shifts[i]
         total = shifts[0] + later[0, 1 : 1 + row_block, :] + later[1, 2 : 2 + row_block, :]
-        out_ref[...] = total.astype(jnp.bfloat16)
+        grad_rows[here, :] = total.astype(jnp.bfloat16)
         for i in (1, 2):
             later[i - 1, row_block : row_block + PAD, :] = shifts[i][0:PAD, :]
 
-
-def section(x, g, taps, fwd, inv, spec):
-    rows, width = x.shape
+    @pl.when(step == freq_steps + row_steps - 1)
+    def _():
+        for k in range(devices):
+            outs[k][...] = grad_rows[place(k, 0), :]
+
+
+def section(pieces, taps, fwd, inv, spec, chunk, filt):
+    devices = len(pieces)
+    length, width = pieces[0].shape[1:]
+    rows = devices * length
     freq_steps, row_steps = rows // FREQ_BLOCK, rows // ROW_BLOCK
     forward = lambda step: (jnp.minimum(step, freq_steps - 1), 0)
-    inverse = lambda step: (row_steps - 1 - jnp.maximum(step - freq_steps, 0), 0)
+    backward = lambda step: (row_steps - 1 - jnp.maximum(step - freq_steps, 0), 0)
+    here = lambda index: lambda step: (index(step)[0], chunk)
     once = lambda step: (0, 0)
-    return pl.pallas_call(
-        section_kernel,
+    more = [] if filt is None else [filt]
+    *outs, filt = pl.pallas_call(
+        functools.partial(section_kernel, devices, len(more)),
         grid=(freq_steps + row_steps,),
-        in_specs=[
-            pl.BlockSpec((rows, width), once),
-            pl.BlockSpec((rows, width), once),
-            pl.BlockSpec(taps.shape, once),
+        in_specs=[pl.BlockSpec((2, length, width), lambda step: (0, 0, 0))] * devices
+        + [
+            pl.BlockSpec((taps.shape[0], width), lambda step: (0, chunk)),
             pl.BlockSpec((2 * FREQ_BLOCK, rows), forward),
-            pl.BlockSpec((ROW_BLOCK, 2 * rows), inverse),
-            pl.BlockSpec((2 * FREQ_BLOCK, width), forward),
-        ],
-        out_specs=[
-            pl.BlockSpec((ROW_BLOCK, width), inverse),
-            pl.BlockSpec((ROW_BLOCK, width), inverse),
-        ],
-        out_shape=[
-            jax.ShapeDtypeStruct((rows, width), jnp.bfloat16),
-            jax.ShapeDtypeStruct((rows, width), jnp.float32),
-        ],
+            pl.BlockSpec((ROW_BLOCK, 2 * rows), backward),
+            pl.BlockSpec((2 * FREQ_BLOCK, width), here(forward)),
+        ]
+        + [pl.BlockSpec(memory_space=pl.ANY)] * len(more),
+        out_specs=[pl.BlockSpec((length, width), once)] * devices
+        + [pl.BlockSpec((ROW_BLOCK, width), here(backward))],
+        out_shape=[jax.ShapeDtypeStruct((length, width), jnp.bfloat16)] * devices
+        + [jax.ShapeDtypeStruct((rows, taps.shape[1]), jnp.float32)],
         scratch_shapes=[
             pltpu.VMEM((rows + PAD, width), jnp.float32),
+            pltpu.VMEM((rows, width), jnp.float32),
             pltpu.VMEM((rows, 2 * width), jnp.bfloat16),
             pltpu.VMEM((rows, width), jnp.float32),
             pltpu.VMEM((rows, width), jnp.float32),
             pltpu.VMEM((2 * rows, 3 * width), jnp.bfloat16),
             pltpu.VMEM((2, ROW_BLOCK + PAD, width), jnp.float32),
-        ],
+            pltpu.VMEM((rows, width), jnp.bfloat16),
+        ],
+        input_output_aliases={devices + 4: devices} if more else {},
         compiler_params=pltpu.CompilerParams(vmem_limit_bytes=VMEM_BYTES),
         cost_estimate=pl.CostEstimate(
             flops=20 * rows * rows * width,
@@ -235,7 +326,8 @@
             transcendentals=0,
         ),
         name="section",
-    )(x, g, taps, fwd, inv, spec)
+    )(*pieces, taps, fwd, inv, spec, *more)
+    return outs, filt
 
 
 def phase_table(row_count, col_count, modulus, direction):
@@ -308,33 +400,64 @@
     return total.astype(jnp.bfloat16), filter_grad * (1.0 / math.sqrt(rows))
 
 
+CHUNKS = 1
+
+
+def fast(inputs, upstream, kernel, taps):
+    devices, count = lax.axis_size("seq"), lax.axis_size("pipe")
+    pieces = pack(inputs, upstream, devices, CHUNKS)
+    across = lambda k: [(i, i ^ k) for i in range(devices)]
+    home = lambda k: [
+        (i * count + p, (i ^ k) * count + (p - 1) % count)
+        for i in range(devices)
+        for p in range(count)
+    ]
+    arrived = [
+        [chunk[0]] + [lax.ppermute(chunk[k], "seq", across(k)) for k in range(1, devices)]
+        for chunk in pieces
+    ]
+    fwd, inv, spec = tables(kernel)
+    filter_grad, grads = None, []
+    for chunk in range(CHUNKS):
+        outs, filter_grad = section(arrived[chunk], taps, fwd, inv, spec, chunk, filter_grad)
+        grads.append([lax.ppermute(outs[k], ("seq", "pipe"), home(k)) for k in range(devices)])
+    return unpack(grads), filter_grad[None]
+
+
+def general(inputs, upstream, kernel, taps):
+    devices, count = lax.axis_size("seq"), lax.axis_size("pipe")
+    length_dev, model = inputs.shape
+    rows, width = kernel.shape
+    to_columns = lambda block: block.reshape(length_dev, devices, width).transpose(1, 0, 2)
+    sent = jnp.stack([to_columns(inputs), to_columns(upstream)], axis=1)
+    got = lax.all_to_all(sent, "seq", split_axis=0, concat_axis=0, tiled=True)
+    x_cols, g_cols = got[:, 0].reshape(rows, width), got[:, 1].reshape(rows, width)
+    grad_cols, filter_grad = large_section(x_cols, g_cols, taps, kernel, devices)
+    back = lax.all_to_all(
+        grad_cols.reshape(devices, length_dev, width), "seq", split_axis=0, concat_axis=0, tiled=True
+    )
+    grad_input = back.transpose(1, 0, 2).reshape(length_dev, model)
+    received = lax.ppermute(
+        grad_input[None], "pipe", [((i + 1) % count, i) for i in range(count)]
+    )
+    return received, filter_grad[None]
+
+
 def shards(section_input, out_grad, conv_filter, short_taps):
     inputs, upstream, kernel = section_input[0], out_grad[0], conv_filter[0]
     devices = lax.axis_size("seq")
-    length_dev, model = inputs.shape
+    model = inputs.shape[1]
     rows, width = kernel.shape
-    assert rows == length_dev * devices and model == width * devices
-    me = lax.axis_index("seq")
-    taps = lax.dynamic_slice_in_dim(short_taps[0].reshape(9, model), me * width, width, axis=1)
-    to_columns = lambda block: block.reshape(length_dev, devices, width).transpose(1, 0, 2)
-    sent = jnp.stack([to_columns(inputs), to_columns(upstream)], axis=1)
-    got = lax.all_to_all(sent, "seq", split_axis=0, concat_axis=0, tiled=True)
-    x_cols = got[:, 0].reshape(rows, width)
-    g_cols = got[:, 1].reshape(rows, width)
-    if rows <= DENSE_ROWS:
-        fwd, inv, spec = tables(kernel)
-        grad_cols, filter_grad = section(x_cols, g_cols, taps, fwd, inv, spec)
-    else:
-        grad_cols, filter_grad = large_section(x_cols, g_cols, taps, kernel, devices)
-    back = lax.all_to_all(
-        grad_cols.reshape(devices, length_dev, width), "seq", split_axis=0, concat_axis=0, tiled=True
-    )
-    grad_input = back.transpose(1, 0, 2).reshape(length_dev, model)
-    count = lax.axis_size("pipe")
-    received = lax.ppermute(
-        grad_input[None], "pipe", [((i + 1) % count, i) for i in range(count)]
-    )
-    return received, filter_grad[None]
+    taps = lax.dynamic_slice_in_dim(
+        short_taps[0].reshape(-1, model), lax.axis_index("seq") * width, width, axis=1
+    )
+    dense = (
+        rows <= DENSE_ROWS
+        and rows % FREQ_BLOCK == 0
+        and width % (CHUNKS * 128) == 0
+        and devices & (devices - 1) == 0
+    )
+    return (fast if dense else general)(inputs, upstream, kernel, taps)
 
 
 def solution(mesh):

time: 110 us -> 86.2 us (0.78)
  waiting for transfers between devices: 38.4 us -> 17.7 us
  starting transfers between devices: 8.96 us -> 27.8 us
  blocking collectives: 18.8 us -> 0 us
  local copies, waits for them, and re-layouts: 9.97 us -> 2.19 us
  Pallas kernels: 30.8 us -> 36.2 us
    ppermute x1 -> x15, starting transfers between devices: 3.66 us -> 27.8 us  [the longest x8 18.5 us: fast(): lax.ppermute(outs[k], ('seq', 'pipe'), home(k))]
    all_to_all x1 -> x0, blocking collectives: 18.8 us -> none  [shards(): lax.all_to_all(grad_cols.reshape(devices, length_dev, width), 'seq', spli...]
    all_to_all x1 -> x0, waiting for transfers between devices: 16.6 us -> none  [shards(): got = lax.all_to_all(sent, 'seq', split_axis=0, concat_axis=0, tiled=True)]
    pallas_call x1 -> x3, Pallas kernels: 21.9 us -> 27.3 us  [the longest x1 22.6 us: section(): pl.pallas_call(functools.partial(section_kernel, devices, len(more)), gri...]
    all_to_all x1 -> x0, starting transfers between devices: 5.3 us -> none  [shards(): got = lax.all_to_all(sent, 'seq', split_axis=0, concat_axis=0, tiled=True)]
    ppermute x1 -> x15, waiting for transfers between devices: 21.8 us -> 17.7 us  [the longest x8 9.85 us: fast(): lax.ppermute(outs[k], ('seq', 'pipe'), home(k))]
    another operation x3 -> x1, local copies, waits for them, and re-layouts: 3.2 us -> 0.08 us  [shards(): short_taps[0].reshape(-1, model)]
    unnamed x7 -> x30, local copies, waits for them, and re-layouts: 3.99 us -> 1.51 us
  transfers between devices with their start and end apart: 2 -> 15, of which waited for: 2 -> 6; matrix products, arithmetic and copies ran while one was open for 1% -> 2% of each run, Pallas kernels for 8% -> 10%
where the time goes in v2:
time: 86.2 us; the launch traced here: 86 us
  Pallas kernels  36.2 us (42%)
  starting transfers between devices  27.8 us (32%)
  waiting for transfers between devices  17.7 us (21%)
  local copies, waits for them, and re-layouts  2.19 us (3%)
  other arithmetic  1.31 us (2%)
    pallas_call x1, Pallas kernels, section(): pl.pallas_call(functools.partial(section_kernel, devices, len(more)), gri...  22.6 us
    ppermute x8, starting transfers between devices, fast(): lax.ppermute(outs[k], ('seq', 'pipe'), home(k))  18.5 us
    ppermute x8, waiting for transfers between devices, fast(): lax.ppermute(outs[k], ('seq', 'pipe'), home(k))  9.85 us
    ppermute x7, starting transfers between devices, fast(): lax.ppermute(chunk[k], 'seq', across(k))  9.31 us
    pallas_call x1, Pallas kernels, tables(): pl.pallas_call(table_kernel, grid=(steps,), in_specs=[pl.BlockSpec(by_pla...  8.97 us
    ppermute x7, waiting for transfers between devices, fast(): lax.ppermute(chunk[k], 'seq', across(k))  7.83 us
    pallas_call x1, Pallas kernels, pack(): pl.pallas_call(pack_kernel, in_specs=[anywhere] * 2, out_specs=[anywhere]...  2.59 us
    pallas_call x1, Pallas kernels, unpack(): pl.pallas_call(unpack_kernel, in_specs=[anywhere] * len(flat), out_specs=...  2.08 us
  transfers between devices with their start and end apart: 15, of which 6 were waited for; matrix products, arithmetic and copies ran while one was open for 2% of the time, Pallas kernels for 10%

profile of v2, /device:TPU:0, one launch (start us, length us, event | category | flops | bytes accessed | tf_op | source)
XLA Modules:
  0.0 86.0 jit_solution(3441264709730317961)
XLA Ops:
  0.6 2.6 %pack.1 = (bf16[2,128,512]{2,1,0:T(8,128)(2,1)}, bf16[2,128,512]{2,1,0:T(8,128)(2,1)}, bf16[2,128,512]{2,1,0:T(8,128)(2,1)}, bf16[2,128,512]{2,1,0:T(8,128)(2,1)...) custom-call(bf16[128,4096]{1,0:T(8,128)(2,1)} %bitcast.4, ...), custom_call_target="tpu_custom_call" | custom-call | tf_op jit(solution)/shard_map/pack/pallas_call | solution.py:148
  3.2 0.5 collective-permute-start
  3.7 2.6 %collective-permute-start.1 = (bf16[2,128,512]{2,1,0:T(8,128)(2,1)}, bf16[2,128,512]{2,1,0:T(8,128)(2,1)S(1)}, u32[]{:S(2)}, u32[]{:S(2)}) collective-permute-start(bf16[2,128,512]{2,1,0:T(8,128)(2,1)} %get-tuple-element.24), channel_id=1, source_target_pairs={{0,8},{4,12},{8,0},{12,4},{16,24},{20,28},{24,16},{28,20},{1,9},{5... | collective-permute-start | bytes 786440 | tf_op jit(solution)/shard_map/ppermute | solution.py:416
  6.3 0.1 collective-permute-start.2
  6.4 1.8 %collective-permute-start.3 = (bf16[2,128,512]{2,1,0:T(8,128)(2,1)}, bf16[2,128,512]{2,1,0:T(8,128)(2,1)S(1)}, u32[]{:S(2)}, u32[]{:S(2)}) collective-permute-start(bf16[2,128,512]{2,1,0:T(8,128)(2,1)} %get-tuple-element.26), channel_id=1, source_target_pairs={{0,16},{4,20},{8,24},{12,28},{16,0},{20,4},{24,8},{28,12},{1,17},{... | collective-permute-start | bytes 786440 | tf_op jit(solution)/shard_map/ppermute | solution.py:416
  8.1 0.0 collective-permute-start.4
  8.2 1.3 %reduce = f32[3,3,4096]{2,1,0:T(4,128)S(1)} reduce(f32[1,3,3,4096]{3,0,2,1:T(1,128)} %param.9, f32[]{:T(128)} %constant.22), dimensions={0}, to_apply=%param.9.reduce_sub_computation | reduce | bytes 294916 | tf_op args[3]
  9.5 0.1 reshape_squeeze.3
  9.5 0.0 collective-permute-done.refs_1_
  9.6 0.0 copy-start.8
  9.6 2.7 %collective-permute-start.5 = (bf16[2,128,512]{2,1,0:T(8,128)(2,1)}, bf16[2,128,512]{2,1,0:T(8,128)(2,1)S(1)}, u32[]{:S(2)}, u32[]{:S(2)}) collective-permute-start(bf16[2,128,512]{2,1,0:T(8,128)(2,1)} %get-tuple-element.28), channel_id=1, source_target_pairs={{0,24},{4,28},{8,16},{12,20},{16,8},{20,12},{24,0},{28,4},{1,25},{... | collective-permute-start | bytes 786440 | tf_op jit(solution)/shard_map/ppermute | solution.py:416
  12.2 1.4 %collective-permute-done.1.refs_2_ = bf16[2,128,512]{2,1,0:T(8,128)(2,1)S(1)} collective-permute-done((bf16[2,128,512]{2,1,0:T(8,128)(2,1)}, bf16[2,128,512]{2,1,0:T(8,128)(2,1)S(1)}, u32[]{:S(2)}, u32[]{:S(2)}) %collective-permute-start.1) | collective-permute-done | bytes 262176 | tf_op jit(solution)/shard_map/ppermute | solution.py:416
  13.7 0.0 copy-start.9
  13.7 1.7 %collective-permute-start.6 = (bf16[2,128,512]{2,1,0:T(8,128)(2,1)}, bf16[2,128,512]{2,1,0:T(8,128)(2,1)S(1)}, u32[]{:S(2)}, u32[]{:S(2)}) collective-permute-start(bf16[2,128,512]{2,1,0:T(8,128)(2,1)} %get-tuple-element.29), channel_id=1, source_target_pairs={{0,28},{4,24},{8,20},{12,16},{16,12},{20,8},{24,4},{28,0},{1,29},{... | collective-permute-start | bytes 786440 | tf_op jit(solution)/shard_map/ppermute | solution.py:416
  15.4 0.6 constant_dynamic-slice_fusion.refs_8_
  16.0 9.0 %tables.1 = (bf16[2048,1024]{1,0:T(8,128)(2,1)}, bf16[1024,2048]{1,0:T(8,128)(2,1)}, f32[2048,512]{1,0:T(8,128)}) custom-call(f32[4,32,1024]{2,1,0:T(8,128)} %constant.16.clone.place_ref, f32[4,32,1024]{2,1,0:T(8,128)} %constant.17.clone.freq_ref, f32[1024,512]{1,0:T(8,128)} %bitcast.6), custom_call_target="tpu_custom_call" | custom-call | flops 2147483648 | bytes 16777216 | tf_op jit(solution)/shard_map/tables/pallas_call | solution.py:85
  25.0 0.0 collective-permute-done.2.refs_3_
  25.0 0.0 copy-start.10
  25.0 0.0 collective-permute-done.3.refs_4_
  25.0 0.0 copy-start.11
  25.0 6.4 %collective-permute-done.4.refs_5_ = bf16[2,128,512]{2,1,0:T(8,128)(2,1)S(1)} collective-permute-done((bf16[2,128,512]{2,1,0:T(8,128)(2,1)}, bf16[2,128,512]{2,1,0:T(8,128)(2,1)S(1)}, u32[]{:S(2)}, u32[]{:S(2)}) %collective-permute-start.4) | collective-permute-done | bytes 262176 | tf_op jit(solution)/shard_map/ppermute | solution.py:416
  31.4 0.0 collective-permute-done.5.refs_6_
  31.4 0.0 copy-start.13
  31.4 0.0 collective-permute-done.6.refs_7_
  31.4 0.0 copy-start.14
  31.4 0.0 copy-done.8
  31.4 0.0 copy-done.9
  31.4 0.0 copy-done.10
  31.4 0.0 copy-done.11
  31.4 0.6 copy-done.12
  32.1 0.1 copy-done.13
  32.2 0.1 copy-done.14
  32.3 22.6 %section.1 = (bf16[128,512]{1,0:T(8,128)(2,1)}, bf16[128,512]{1,0:T(8,128)(2,1)}, bf16[128,512]{1,0:T(8,128)(2,1)}, bf16[128,512]{1,0:T(8,128)(2,1)}, bf16[128,5...) custom-call(bf16[2,128,512]{2,1,0:T(8,128)(2,1)} %get-tuple-element., ...), custom_call_target="tpu_custom_call" | custom-call | flops 10737418240 | bytes 18874368 | tf_op jit(solution)/shard_map/section/pallas_call | solution.py:296
  54.9 4.0 %collective-permute-start.7 = (bf16[128,512]{1,0:T(8,128)(2,1)}, bf16[128,512]{1,0:T(8,128)(2,1)S(1)}, u32[]{:S(2)}, u32[]{:S(2)}) collective-permute-start(bf16[128,512]{1,0:T(8,128)(2,1)} %get-tuple-element.33), channel_id=1, source_target_pairs={{0,3},{1,0},{2,1},{3,2},{4,7},{5,4},{6,5},{7,6},{8,11},{9,8},{10,9... | collective-permute-start | bytes 393224 | tf_op jit(solution)/shard_map/ppermute | solution.py:423
  58.8 0.2 collective-permute-start.8
  59.0 1.4 %collective-permute-start.9 = (bf16[128,512]{1,0:T(8,128)(2,1)}, bf16[128,512]{1,0:T(8,128)(2,1)S(1)}, u32[]{:S(2)}, u32[]{:S(2)}) collective-permute-start(bf16[128,512]{1,0:T(8,128)(2,1)} %get-tuple-element.35), channel_id=1, source_target_pairs={{0,11},{1,8},{2,9},{3,10},{4,15},{5,12},{6,13},{7,14},{8,3},{9,0},... | collective-permute-start | bytes 393224 | tf_op jit(solution)/shard_map/ppermute | solution.py:423
  60.4 0.0 collective-permute-start.10
  60.4 4.7 %collective-permute-start.11 = (bf16[128,512]{1,0:T(8,128)(2,1)}, bf16[128,512]{1,0:T(8,128)(2,1)S(1)}, u32[]{:S(2)}, u32[]{:S(2)}) collective-permute-start(bf16[128,512]{1,0:T(8,128)(2,1)} %get-tuple-element.37), channel_id=1, source_target_pairs={{0,19},{1,16},{2,17},{3,18},{4,23},{5,20},{6,21},{7,22},{8,27},{9,... | collective-permute-start | bytes 393224 | tf_op jit(solution)/shard_map/ppermute | solution.py:423
  65.0 0.0 collective-permute-done.7.refs_0_
  65.0 0.0 copy-start
  65.0 1.8 %collective-permute-start.12 = (bf16[128,512]{1,0:T(8,128)(2,1)}, bf16[128,512]{1,0:T(8,128)(2,1)S(1)}, u32[]{:S(2)}, u32[]{:S(2)}) collective-permute-start(bf16[128,512]{1,0:T(8,128)(2,1)} %get-tuple-element.38), channel_id=1, source_target_pairs={{0,23},{1,20},{2,21},{3,22},{4,19},{5,16},{6,17},{7,18},{8,31},{9,... | collective-permute-start | bytes 393224 | tf_op jit(solution)/shard_map/ppermute | solution.py:423
  66.8 0.0 collective-permute-done.8.refs_1_
  66.8 0.0 copy-start.1
  66.8 4.0 %collective-permute-start.13 = (bf16[128,512]{1,0:T(8,128)(2,1)}, bf16[128,512]{1,0:T(8,128)(2,1)S(1)}, u32[]{:S(2)}, u32[]{:S(2)}) collective-permute-start(bf16[128,512]{1,0:T(8,128)(2,1)} %get-tuple-element.39), channel_id=1, source_target_pairs={{0,27},{1,24},{2,25},{3,26},{4,31},{5,28},{6,29},{7,30},{8,19},{9,... | collective-permute-start | bytes 393224 | tf_op jit(solution)/shard_map/ppermute | solution.py:423
  70.8 0.0 collective-permute-done.9.refs_2_
  70.8 0.0 copy-start.2
  70.8 2.5 %collective-permute-start.14 = (bf16[128,512]{1,0:T(8,128)(2,1)}, bf16[128,512]{1,0:T(8,128)(2,1)S(1)}, u32[]{:S(2)}, u32[]{:S(2)}) collective-permute-start(bf16[128,512]{1,0:T(8,128)(2,1)} %get-tuple-element.40), channel_id=1, source_target_pairs={{0,31},{1,28},{2,29},{3,30},{4,27},{5,24},{6,25},{7,26},{8,23},{9,... | collective-permute-start | bytes 393224 | tf_op jit(solution)/shard_map/ppermute | solution.py:423
  73.3 0.0 collective-permute-done.10.refs_3_
  73.3 0.0 copy-start.3
  73.3 1.2 %collective-permute-done.11.refs_4_ = bf16[128,512]{1,0:T(8,128)(2,1)S(1)} collective-permute-done((bf16[128,512]{1,0:T(8,128)(2,1)}, bf16[128,512]{1,0:T(8,128)(2,1)S(1)}, u32[]{:S(2)}, u32[]{:S(2)}) %collective-permute-start.11) | collective-permute-done | bytes 131104 | tf_op jit(solution)/shard_map/ppermute | solution.py:423
  74.5 0.0 copy-start.4
  74.5 2.5 %collective-permute-done.12.refs_5_ = bf16[128,512]{1,0:T(8,128)(2,1)S(1)} collective-permute-done((bf16[128,512]{1,0:T(8,128)(2,1)}, bf16[128,512]{1,0:T(8,128)(2,1)S(1)}, u32[]{:S(2)}, u32[]{:S(2)}) %collective-permute-start.12) | collective-permute-done | bytes 131104 | tf_op jit(solution)/shard_map/ppermute | solution.py:423
  77.0 4.0 %collective-permute-done.13.refs_6_ = bf16[128,512]{1,0:T(8,128)(2,1)S(1)} collective-permute-done((bf16[128,512]{1,0:T(8,128)(2,1)}, bf16[128,512]{1,0:T(8,128)(2,1)S(1)}, u32[]{:S(2)}, u32[]{:S(2)}) %collective-permute-start.13) | collective-permute-done | bytes 131104 | tf_op jit(solution)/shard_map/ppermute | solution.py:423
  81.0 2.2 %collective-permute-done.14.refs_7_ = bf16[128,512]{1,0:T(8,128)(2,1)S(1)} collective-permute-done((bf16[128,512]{1,0:T(8,128)(2,1)}, bf16[128,512]{1,0:T(8,128)(2,1)S(1)}, u32[]{:S(2)}, u32[]{:S(2)}) %collective-permute-start.14) | collective-permute-done | bytes 131104 | tf_op jit(solution)/shard_map/ppermute | solution.py:423
  83.2 0.0 copy-done
  83.2 0.0 copy-done.1
  83.2 0.0 copy-done.2
  83.2 0.0 copy-done.3
  83.2 0.0 copy-done.4
  83.2 0.0 copy-done.5
  83.2 0.0 copy-done.6
  83.2 0.0 copy-start.7
  83.2 0.7 copy-done.7
  83.9 2.1 %unpack.1 = bf16[1,128,4096]{2,1,0:T(8,128)(2,1)} custom-call(bf16[128,512]{1,0:T(8,128)(2,1)} %copy-done, bf16[128,512]{1,0:T(8,128)(2,1)} %copy-done.1, bf16[128,512]{1,0:T(8,128)(2,1)} %copy-done.2, bf16[128,512]{1,0:T(8,128)(2,1)} %copy-done.3, bf16[128,512]{1,0:T(8,128)(2,1)} %copy-done.4, bf16[128,512]{1,0:T(8,128)(2,1)} %copy-done.5, ...), custom_call_target="tpu_custom_call" | custom-call | tf_op jit(solution)/shard_map/unpack/pallas_call | solution.py:181
  (3 shorter events, 0.0 us)
Async XLA Ops:
  3.2 6.3 %collective-permute-start = (bf16[2,128,512]{2,1,0:T(8,128)(2,1)}, bf16[2,128,512]{2,1,0:T(8,128)(2,1)S(1)}, u32[]{:S(2)}, u32[]{:S(2)}) collective-permute-start(bf16[2,128,512]{2,1,0:T(8,128)(2,1)} %get-tuple-element.23), channel_id=1, source_target_pairs={{0,4},{4,0},{8,12},{12,8},{16,20},{20,16},{24,28},{28,24},{1,5},{5... | collective-permute-start | bytes 786440 | tf_op jit(solution)/shard_map/ppermute | solution.py:416
  3.7 9.9 %collective-permute-start.1 = (bf16[2,128,512]{2,1,0:T(8,128)(2,1)}, bf16[2,128,512]{2,1,0:T(8,128)(2,1)S(1)}, u32[]{:S(2)}, u32[]{:S(2)}) collective-permute-start(bf16[2,128,512]{2,1,0:T(8,128)(2,1)} %get-tuple-element.24), channel_id=1, source_target_pairs={{0,8},{4,12},{8,0},{12,4},{16,24},{20,28},{24,16},{28,20},{1,9},{5... | collective-permute-start | bytes 786440 | tf_op jit(solution)/shard_map/ppermute | solution.py:416
  6.3 18.7 %collective-permute-start.2 = (bf16[2,128,512]{2,1,0:T(8,128)(2,1)}, bf16[2,128,512]{2,1,0:T(8,128)(2,1)S(1)}, u32[]{:S(2)}, u32[]{:S(2)}) collective-permute-start(bf16[2,128,512]{2,1,0:T(8,128)(2,1)} %get-tuple-element.25), channel_id=1, source_target_pairs={{0,12},{4,8},{8,4},{12,0},{16,28},{20,24},{24,20},{28,16},{1,13},{... | collective-permute-start | bytes 786440 | tf_op jit(solution)/shard_map/ppermute | solution.py:416
  6.4 18.6 %collective-permute-start.3 = (bf16[2,128,512]{2,1,0:T(8,128)(2,1)}, bf16[2,128,512]{2,1,0:T(8,128)(2,1)S(1)}, u32[]{:S(2)}, u32[]{:S(2)}) collective-permute-start(bf16[2,128,512]{2,1,0:T(8,128)(2,1)} %get-tuple-element.26), channel_id=1, source_target_pairs={{0,16},{4,20},{8,24},{12,28},{16,0},{20,4},{24,8},{28,12},{1,17},{... | collective-permute-start | bytes 786440 | tf_op jit(solution)/shard_map/ppermute | solution.py:416
  8.1 23.2 %collective-permute-start.4 = (bf16[2,128,512]{2,1,0:T(8,128)(2,1)}, bf16[2,128,512]{2,1,0:T(8,128)(2,1)S(1)}, u32[]{:S(2)}, u32[]{:S(2)}) collective-permute-start(bf16[2,128,512]{2,1,0:T(8,128)(2,1)} %get-tuple-element.27), channel_id=1, source_target_pairs={{0,20},{4,16},{8,28},{12,24},{16,4},{20,0},{24,12},{28,8},{1,21},{... | collective-permute-start | bytes 786440 | tf_op jit(solution)/shard_map/ppermute | solution.py:416
  9.6 21.8 %copy-start.8 = (bf16[2,128,512]{2,1,0:T(8,128)(2,1)}, bf16[2,128,512]{2,1,0:T(8,128)(2,1)S(1)}, u32[]{:S(2)}) copy-start(bf16[2,128,512]{2,1,0:T(8,128)(2,1)S(1)} %collective-permute-done.refs_1_) | copy-start | bytes 786436
  9.6 21.8 %collective-permute-start.5 = (bf16[2,128,512]{2,1,0:T(8,128)(2,1)}, bf16[2,128,512]{2,1,0:T(8,128)(2,1)S(1)}, u32[]{:S(2)}, u32[]{:S(2)}) collective-permute-start(bf16[2,128,512]{2,1,0:T(8,128)(2,1)} %get-tuple-element.28), channel_id=1, source_target_pairs={{0,24},{4,28},{8,16},{12,20},{16,8},{20,12},{24,0},{28,4},{1,25},{... | collective-permute-start | bytes 786440 | tf_op jit(solution)/shard_map/ppermute | solution.py:416
  13.7 17.7 %copy-start.9 = (bf16[2,128,512]{2,1,0:T(8,128)(2,1)}, bf16[2,128,512]{2,1,0:T(8,128)(2,1)S(1)}, u32[]{:S(2)}) copy-start(bf16[2,128,512]{2,1,0:T(8,128)(2,1)S(1)} %collective-permute-done.1.refs_2_) | copy-start | bytes 786436
  13.7 17.7 %collective-permute-start.6 = (bf16[2,128,512]{2,1,0:T(8,128)(2,1)}, bf16[2,128,512]{2,1,0:T(8,128)(2,1)S(1)}, u32[]{:S(2)}, u32[]{:S(2)}) collective-permute-start(bf16[2,128,512]{2,1,0:T(8,128)(2,1)} %get-tuple-element.29), channel_id=1, source_target_pairs={{0,28},{4,24},{8,20},{12,16},{16,12},{20,8},{24,4},{28,0},{1,29},{... | collective-permute-start | bytes 786440 | tf_op jit(solution)/shard_map/ppermute | solution.py:416
  25.0 6.4 %copy-start.10 = (bf16[2,128,512]{2,1,0:T(8,128)(2,1)}, bf16[2,128,512]{2,1,0:T(8,128)(2,1)S(1)}, u32[]{:S(2)}) copy-start(bf16[2,128,512]{2,1,0:T(8,128)(2,1)S(1)} %collective-permute-done.2.refs_3_) | copy-start | bytes 786436
  25.0 6.4 %copy-start.11 = (bf16[2,128,512]{2,1,0:T(8,128)(2,1)}, bf16[2,128,512]{2,1,0:T(8,128)(2,1)S(1)}, u32[]{:S(2)}) copy-start(bf16[2,128,512]{2,1,0:T(8,128)(2,1)S(1)} %collective-permute-done.3.refs_4_) | copy-start | bytes 786436
  31.4 0.7 copy-start.12
  31.4 0.8 copy-start.13
  31.4 0.9 %copy-start.14 = (bf16[2,128,512]{2,1,0:T(8,128)(2,1)}, bf16[2,128,512]{2,1,0:T(8,128)(2,1)S(1)}, u32[]{:S(2)}) copy-start(bf16[2,128,512]{2,1,0:T(8,128)(2,1)S(1)} %collective-permute-done.6.refs_7_) | copy-start | bytes 786436
  54.9 10.2 %collective-permute-start.7 = (bf16[128,512]{1,0:T(8,128)(2,1)}, bf16[128,512]{1,0:T(8,128)(2,1)S(1)}, u32[]{:S(2)}, u32[]{:S(2)}) collective-permute-start(bf16[128,512]{1,0:T(8,128)(2,1)} %get-tuple-element.33), channel_id=1, source_target_pairs={{0,3},{1,0},{2,1},{3,2},{4,7},{5,4},{6,5},{7,6},{8,11},{9,8},{10,9... | collective-permute-start | bytes 393224 | tf_op jit(solution)/shard_map/ppermute | solution.py:423
  58.8 8.0 %collective-permute-start.8 = (bf16[128,512]{1,0:T(8,128)(2,1)}, bf16[128,512]{1,0:T(8,128)(2,1)S(1)}, u32[]{:S(2)}, u32[]{:S(2)}) collective-permute-start(bf16[128,512]{1,0:T(8,128)(2,1)} %get-tuple-element.34), channel_id=1, source_target_pairs={{0,7},{1,4},{2,5},{3,6},{4,3},{5,0},{6,1},{7,2},{8,15},{9,12},{10,... | collective-permute-start | bytes 393224 | tf_op jit(solution)/shard_map/ppermute | solution.py:423
  59.0 11.8 %collective-permute-start.9 = (bf16[128,512]{1,0:T(8,128)(2,1)}, bf16[128,512]{1,0:T(8,128)(2,1)S(1)}, u32[]{:S(2)}, u32[]{:S(2)}) collective-permute-start(bf16[128,512]{1,0:T(8,128)(2,1)} %get-tuple-element.35), channel_id=1, source_target_pairs={{0,11},{1,8},{2,9},{3,10},{4,15},{5,12},{6,13},{7,14},{8,3},{9,0},... | collective-permute-start | bytes 393224 | tf_op jit(solution)/shard_map/ppermute | solution.py:423
  60.4 13.0 %collective-permute-start.10 = (bf16[128,512]{1,0:T(8,128)(2,1)}, bf16[128,512]{1,0:T(8,128)(2,1)S(1)}, u32[]{:S(2)}, u32[]{:S(2)}) collective-permute-start(bf16[128,512]{1,0:T(8,128)(2,1)} %get-tuple-element.36), channel_id=1, source_target_pairs={{0,15},{1,12},{2,13},{3,14},{4,11},{5,8},{6,9},{7,10},{8,7},{9,4},... | collective-permute-start | bytes 393224 | tf_op jit(solution)/shard_map/ppermute | solution.py:423
  60.4 14.1 %collective-permute-start.11 = (bf16[128,512]{1,0:T(8,128)(2,1)}, bf16[128,512]{1,0:T(8,128)(2,1)S(1)}, u32[]{:S(2)}, u32[]{:S(2)}) collective-permute-start(bf16[128,512]{1,0:T(8,128)(2,1)} %get-tuple-element.37), channel_id=1, source_target_pairs={{0,19},{1,16},{2,17},{3,18},{4,23},{5,20},{6,21},{7,22},{8,27},{9,... | collective-permute-start | bytes 393224 | tf_op jit(solution)/shard_map/ppermute | solution.py:423
  65.0 18.2 %copy-start = (bf16[128,512]{1,0:T(8,128)(2,1)}, bf16[128,512]{1,0:T(8,128)(2,1)S(1)}, u32[]{:S(2)}) copy-start(bf16[128,512]{1,0:T(8,128)(2,1)S(1)} %collective-permute-done.7.refs_0_) | copy-start | bytes 393220
  65.0 12.0 %collective-permute-start.12 = (bf16[128,512]{1,0:T(8,128)(2,1)}, bf16[128,512]{1,0:T(8,128)(2,1)S(1)}, u32[]{:S(2)}, u32[]{:S(2)}) collective-permute-start(bf16[128,512]{1,0:T(8,128)(2,1)} %get-tuple-element.38), channel_id=1, source_target_pairs={{0,23},{1,20},{2,21},{3,22},{4,19},{5,16},{6,17},{7,18},{8,31},{9,... | collective-permute-start | bytes 393224 | tf_op jit(solution)/shard_map/ppermute | solution.py:423
  66.8 16.4 %copy-start.1 = (bf16[128,512]{1,0:T(8,128)(2,1)}, bf16[128,512]{1,0:T(8,128)(2,1)S(1)}, u32[]{:S(2)}) copy-start(bf16[128,512]{1,0:T(8,128)(2,1)S(1)} %collective-permute-done.8.refs_1_) | copy-start | bytes 393220
  66.8 14.2 %collective-permute-start.13 = (bf16[128,512]{1,0:T(8,128)(2,1)}, bf16[128,512]{1,0:T(8,128)(2,1)S(1)}, u32[]{:S(2)}, u32[]{:S(2)}) collective-permute-start(bf16[128,512]{1,0:T(8,128)(2,1)} %get-tuple-element.39), channel_id=1, source_target_pairs={{0,27},{1,24},{2,25},{3,26},{4,31},{5,28},{6,29},{7,30},{8,19},{9,... | collective-permute-start | bytes 393224 | tf_op jit(solution)/shard_map/ppermute | solution.py:423
  70.8 12.4 %copy-start.2 = (bf16[128,512]{1,0:T(8,128)(2,1)}, bf16[128,512]{1,0:T(8,128)(2,1)S(1)}, u32[]{:S(2)}) copy-start(bf16[128,512]{1,0:T(8,128)(2,1)S(1)} %collective-permute-done.9.refs_2_) | copy-start | bytes 393220
  70.8 12.4 %collective-permute-start.14 = (bf16[128,512]{1,0:T(8,128)(2,1)}, bf16[128,512]{1,0:T(8,128)(2,1)S(1)}, u32[]{:S(2)}, u32[]{:S(2)}) collective-permute-start(bf16[128,512]{1,0:T(8,128)(2,1)} %get-tuple-element.40), channel_id=1, source_target_pairs={{0,31},{1,28},{2,29},{3,30},{4,27},{5,24},{6,25},{7,26},{8,23},{9,... | collective-permute-start | bytes 393224 | tf_op jit(solution)/shard_map/ppermute | solution.py:423
  73.3 9.9 %copy-start.3 = (bf16[128,512]{1,0:T(8,128)(2,1)}, bf16[128,512]{1,0:T(8,128)(2,1)S(1)}, u32[]{:S(2)}) copy-start(bf16[128,512]{1,0:T(8,128)(2,1)S(1)} %collective-permute-done.10.refs_3_) | copy-start | bytes 393220
  74.5 8.7 %copy-start.4 = (bf16[128,512]{1,0:T(8,128)(2,1)}, bf16[128,512]{1,0:T(8,128)(2,1)S(1)}, u32[]{:S(2)}) copy-start(bf16[128,512]{1,0:T(8,128)(2,1)S(1)} %collective-permute-done.11.refs_4_) | copy-start | bytes 393220
  77.0 6.2 %copy-start.5 = (bf16[128,512]{1,0:T(8,128)(2,1)}, bf16[128,512]{1,0:T(8,128)(2,1)S(1)}, u32[]{:S(2)}) copy-start(bf16[128,512]{1,0:T(8,128)(2,1)S(1)} %collective-permute-done.12.refs_5_) | copy-start | bytes 393220
  81.0 2.2 %copy-start.6 = (bf16[128,512]{1,0:T(8,128)(2,1)}, bf16[128,512]{1,0:T(8,128)(2,1)S(1)}, u32[]{:S(2)}) copy-start(bf16[128,512]{1,0:T(8,128)(2,1)S(1)} %collective-permute-done.13.refs_6_) | copy-start | bytes 393220
  83.2 0.7 copy-start.7

commit v3 on v0

v3 whole, which is shorter than its diff:
```python
import functools
import math

import jax
import jax.numpy as jnp
import numpy as np
from jax import lax
from jax.experimental import pallas as pl
from jax.experimental.pallas import tpu as pltpu
from jax.sharding import PartitionSpec as P

WHOLE_IN = (False, False)
WHOLE_OUT = (True, False)
CHUNKS = len(WHOLE_IN)
PAD = 8
TILE = 16
LAST_TILE = 64
DENSE_ROWS = 1024
SPECTRUM_VMEM = 12 * 1024 * 1024
SECTION_VMEM = 28 * 1024 * 1024
COS = [math.cos(math.pi / 8 * j) for j in range(4)]
SIN = [math.sin(math.pi / 8 * j) for j in range(4)]


def quarter_tables(rows):
    quarter = rows // 4
    freqs = 16 * np.arange(quarter)[None, :, None] + 4 * np.arange(4)[:, None, None] + 1
    angles = 2.0 * np.pi / (4 * rows) * (freqs * np.arange(quarter) % (4 * rows))
    real, imag = np.cos(angles), -np.sin(angles)
    fwd = np.concatenate(
        [np.concatenate([real, -imag], axis=2), np.concatenate([imag, real], axis=2)], axis=1
    )
    inv = np.swapaxes(fwd, 1, 2) / rows
    return jnp.asarray(fwd.astype(jnp.bfloat16)), jnp.asarray(inv.astype(jnp.bfloat16))


def split(x0, x1, x2, x3):
    even, turn = x0 + COS[2] * x2, SIN[2] * x2
    odd = x0 - COS[2] * x2
    sum_re, sum_im = COS[1] * x1 + COS[3] * x3, SIN[1] * x1 + SIN[3] * x3
    dif_re, dif_im = COS[1] * x1 - COS[3] * x3, SIN[1] * x1 - SIN[3] * x3
    return (
        (even + sum_re, -turn - sum_im),
        (odd - dif_im, turn - dif_re),
        (even - sum_re, sum_im - turn),
        (odd + dif_im, turn + dif_re),
    )


def joined(v0, v1, v2, v3):
    a_re, a_im, b_re, b_im = v0[0] + v2[0], v0[1] + v2[1], v1[0] + v3[0], v1[1] + v3[1]
    c_re, c_im, d_re, d_im = v0[0] - v2[0], v0[1] - v2[1], v1[0] - v3[0], v1[1] - v3[1]
    return (
        a_re + b_re,
        COS[1] * (c_re - d_im) - SIN[1] * (c_im + d_re),
        COS[2] * (a_re - b_re) - SIN[2] * (a_im - b_im),
        COS[3] * (c_re + d_im) - SIN[3] * (c_im - d_re),
    )


def by_target(refs, devices, whole):
    me, refs = lax.axis_index("seq"), list(refs)
    pairs = []
    for together in whole:
        if together:
            ref = refs.pop(0)
            pairs.append([(d, ref.at[d]) for d in range(devices)])
        else:
            pairs.append([(me ^ k, refs.pop(0)) for k in range(devices)])
    return pairs


def pack_kernel(whole, x_ref, g_ref, *refs):
    pieces, sem = refs[:-1], refs[-1]
    devices = lax.axis_size("seq")
    width = pieces[0].shape[-1]
    copies = []
    for chunk, pairs in enumerate(by_target(pieces, devices, whole)):
        for number, (device, piece) in enumerate(pairs):
            start = pl.multiple_of((device * len(whole) + chunk) * width, width)
            for half, ref in enumerate((x_ref, g_ref)):
                copies.append(
                    pltpu.make_async_copy(
                        ref.at[:, pl.ds(start, width)],
                        piece.at[half],
                        sem.at[chunk * devices + number, half],
                    )
                )
    for copy in copies:
        copy.start()
    for copy in copies:
        copy.wait()


def pack(x, g, devices, whole):
    length, model = x.shape
    width = model // devices // len(whole)
    shapes = []
    for together in whole:
        shapes += [(devices, 2, length, width)] if together else [(2, length, width)] * devices
    pieces = pl.pallas_call(
        functools.partial(pack_kernel, whole),
        in_specs=[pl.BlockSpec(memory_space=pl.ANY)] * 2,
        out_specs=[pl.BlockSpec(memory_space=pltpu.VMEM)] * len(shapes),
        out_shape=[jax.ShapeDtypeStruct(shape, x.dtype) for shape in shapes],
        scratch_shapes=[pltpu.SemaphoreType.DMA((devices * len(whole), 2))],
        compiler_params=pltpu.CompilerParams(vmem_limit_bytes=8 * 1024 * 1024),
        name="pack",
    )(x, g)
    chunks, pieces = [], list(pieces)
    for together in whole:
        taken = 1 if together else devices
        chunks.append(pieces[:taken])
        pieces = pieces[taken:]
    return chunks


def unpack_kernel(whole, *refs):
    pieces, out_ref, sem = refs[:-2], refs[-2], refs[-1]
    devices = lax.axis_size("seq")
    width = pieces[0].shape[-1]
    copies = []
    for chunk, pairs in enumerate(by_target(pieces, devices, whole)):
        for number, (device, piece) in enumerate(pairs):
            start = pl.multiple_of((device * len(whole) + chunk) * width, width)
            copies.append(
                pltpu.make_async_copy(
                    piece,
                    out_ref.at[0, :, pl.ds(start, width)],
                    sem.at[chunk * devices + number],
                )
            )
    for copy in copies:
        copy.start()
    for copy in copies:
        copy.wait()


def unpack(chunks, devices, whole):
    flat = [piece for chunk in chunks for piece in chunk]
    length, width = flat[0].shape[-2:]
    count = devices * len(whole)
    return pl.pallas_call(
        functools.partial(unpack_kernel, whole),
        in_specs=[pl.BlockSpec(memory_space=pltpu.VMEM)] * len(flat),
        out_specs=pl.BlockSpec(memory_space=pl.ANY),
        out_shape=jax.ShapeDtypeStruct((1, length, width * count), flat[0].dtype),
        scratch_shapes=[pltpu.SemaphoreType.DMA((count,))],
        compiler_params=pltpu.CompilerParams(vmem_limit_bytes=8 * 1024 * 1024),
        name="unpack",
    )(*flat)


def spectrum_kernel(kernel_ref, fwd_ref, spec_ref, turned):
    rows = kernel_ref.shape[0]
    quarter = rows // 4

    @pl.loop(0, quarter // TILE)
    def _(step):
        start = pl.multiple_of(step * TILE, TILE)
        parts = split(*(kernel_ref[pl.ds(start + j * quarter, TILE), :] for j in range(4)))
        for j, (real, imag) in enumerate(parts):
            turned[j, pl.ds(start, TILE), :] = real.astype(jnp.bfloat16)
            turned[j, pl.ds(start + quarter, TILE), :] = imag.astype(jnp.bfloat16)

    for j in range(4):
        spec_ref[j] = jnp.dot(fwd_ref[j], turned[j], preferred_element_type=jnp.float32)


def spectrum(kernel, fwd):
    rows, width = kernel.shape
    near = pl.BlockSpec(memory_space=pltpu.VMEM)
    return pl.pallas_call(
        spectrum_kernel,
        in_specs=[near] * 2,
        out_specs=near,
        out_shape=jax.ShapeDtypeStruct((4, rows // 2, width), jnp.float32),
        scratch_shapes=[pltpu.VMEM((4, rows // 2, width), jnp.bfloat16)],
        compiler_params=pltpu.CompilerParams(vmem_limit_bytes=SPECTRUM_VMEM),
        cost_estimate=pl.CostEstimate(
            flops=2 * rows * rows * width, bytes_accessed=14 * rows * width, transcendentals=0
        ),
        name="spectrum",
    )(kernel, fwd)


def section_kernel(devices, chunk, aliased, whole_in, whole_out, *refs):
    taken = 1 if whole_in else devices
    (pieces,) = by_target(refs[:taken], devices, [whole_in])
    refs = refs[taken:]
    tap_ref, fwd_ref, inv_ref, spec_ref = refs[:4]
    refs = refs[4 + aliased :]
    out_ref, filt_ref, padded, upstream, key_rows, value_rows, turned, mixed, back = refs[:9]
    shifted_rows, filt_rows, grad_rows, tap_rows, filt_sem, tap_sem = refs[9:]
    me = lax.axis_index("seq")
    length, width = pieces[0][1].shape[1:]
    rows = length * devices
    quarter = rows // 4
    columns = slice(chunk * width, (chunk + 1) * width)
    place = lambda device, offset: pl.ds(pl.multiple_of(device * length + offset, 8), length)
    low = lambda v: v.astype(jnp.bfloat16).astype(jnp.float32)

    start = pl.multiple_of((me * (spec_ref.shape[2] // width) + chunk) * width, width)
    fetch = pltpu.make_async_copy(tap_ref.at[0, :, :, pl.ds(start, width)], tap_rows, tap_sem)
    fetch.start()
    padded[0:PAD, :] = jnp.zeros((PAD, width), jnp.float32)
    for device, piece in pieces:
        padded[place(device, PAD), :] = piece[0].astype(jnp.float32)
        upstream[place(device, 0), :] = piece[1].astype(jnp.float32)
    fetch.wait()
    taps = [tap_rows[s, i : i + 1, :] for s in range(3) for i in range(3)]

    @pl.loop(0, quarter // TILE)
    def _(step):
        begin = pl.multiple_of(step * TILE, TILE)
        products, adjoints = [], []
        for j in range(4):
            here = pl.ds(begin + j * quarter, TILE)
            window = padded[pl.ds(begin + j * quarter, TILE + PAD), :]
            moved = [window[PAD - i : PAD - i + TILE, :] for i in range(3)]
            query, key, value = (
                low(sum(taps[3 * s + i] * moved[i] for i in range(3))) for s in range(3)
            )
            key_rows[here, :] = key
            value_rows[here, :] = value
            products.append(key * value)
            adjoints.append(upstream[here, :] * query)
        for half, signals in enumerate((products, adjoints)):
            into = slice(half * width, (half + 1) * width)
            for j, (real, imag) in enumerate(split(*signals)):
                turned[j, pl.ds(begin, TILE), into] = real.astype(jnp.bfloat16)
                turned[j, pl.ds(begin + quarter, TILE), into] = imag.astype(jnp.bfloat16)

    for j in range(4):
        both = jnp.dot(fwd_ref[j], turned[j], preferred_element_type=jnp.float32)
        p_re, p_im = both[:quarter, :width], both[quarter:, :width]
        a_re, a_im = both[:quarter, width:], both[quarter:, width:]
        h_re, h_im = spec_ref[j, :quarter, columns], spec_ref[j, quarter:, columns]
        for number, (real, imag) in enumerate(
            (
                (p_re * h_re - p_im * h_im, p_re * h_im + p_im * h_re),
                (h_re * a_re + h_im * a_im, h_re * a_im - h_im * a_re),
                (p_re * a_re + p_im * a_im, p_re * a_im - p_im * a_re),
            )
        ):
            into = slice(number * width, (number + 1) * width)
            mixed[j, :quarter, into] = real.astype(jnp.bfloat16)
            mixed[j, quarter:, into] = imag.astype(jnp.bfloat16)
        back[j] = jnp.dot(inv_ref[j], mixed[j], preferred_element_type=jnp.float32)

    @pl.loop(0, quarter // TILE)
    def _(step):
        begin = pl.multiple_of(step * TILE, TILE)
        real, imag = pl.ds(begin, TILE), pl.ds(begin + quarter, TILE)
        results = []
        for number in range(3):
            part = slice(number * width, (number + 1) * width)
            results.append(joined(*((back[j, real, part], back[j, imag, part]) for j in range(4))))
        for j, (combined, backward, filt) in enumerate(zip(*results)):
            here = pl.ds(begin + j * quarter, TILE)
            filt_rows[here, :] = filt * (1.0 / math.sqrt(rows))
            pltpu.make_async_copy(
                filt_rows.at[here, :], filt_ref.at[here, columns], filt_sem
            ).start()
            grads = (
                low(upstream[here, :] * combined),
                low(backward * value_rows[here, :]),
                low(backward * key_rows[here, :]),
            )
            for i in range(3):
                shifted_rows[i, here, :] = sum(taps[3 * s + i] * grads[s] for s in range(3))

    shifted_rows[:, rows:, :] = jnp.zeros((3, PAD, width), jnp.float32)

    @pl.loop(0, rows // LAST_TILE)
    def _(step):
        begin = pl.multiple_of(step * LAST_TILE, LAST_TILE)
        windows = [shifted_rows[i, pl.ds(begin, LAST_TILE + PAD), :] for i in range(3)]
        total = sum(windows[i][i : i + LAST_TILE, :] for i in range(3))
        grad_rows[pl.ds(begin, LAST_TILE), :] = total.astype(jnp.bfloat16)

    for k in range(devices):
        out_ref[k] = grad_rows[place(k if whole_out else me ^ k, 0), :]
    pltpu.make_async_copy(filt_rows, filt_ref.at[:, columns], filt_sem).wait()


def section(pieces, taps, fwd, inv, spec, chunk, filt, devices, whole_in, whole_out):
    length, width = pieces[0].shape[-2:]
    rows = devices * length
    near = pl.BlockSpec(memory_space=pltpu.VMEM)
    far = pl.BlockSpec(memory_space=pl.ANY)
    more = [] if filt is None else [filt]
    vmem = lambda *shape: pltpu.VMEM(shape, jnp.float32)
    return pl.pallas_call(
        functools.partial(section_kernel, devices, chunk, len(more), whole_in, whole_out),
        in_specs=[near] * len(pieces) + [far] + [near] * 3 + [far] * len(more),
        out_specs=[near, far],
        out_shape=[
            jax.ShapeDtypeStruct((devices, length, width), jnp.bfloat16),
            jax.ShapeDtypeStruct((rows, spec.shape[2]), jnp.float32),
        ],
        scratch_shapes=[
            vmem(rows + PAD, width),
            vmem(rows, width),
            vmem(rows, width),
            vmem(rows, width),
            pltpu.VMEM((4, rows // 2, 2 * width), jnp.bfloat16),
            pltpu.VMEM((4, rows // 2, 3 * width), jnp.bfloat16),
            vmem(4, rows // 2, 3 * width),
            vmem(3, rows + PAD, width),
            vmem(rows, width),
            pltpu.VMEM((rows, width), jnp.bfloat16),
            vmem(*taps.shape[1:3], width),
            pltpu.SemaphoreType.DMA,
            pltpu.SemaphoreType.DMA,
        ],
        input_output_aliases={len(pieces) + 4: 1} if more else {},
        compiler_params=pltpu.CompilerParams(vmem_limit_bytes=SECTION_VMEM),
        cost_estimate=pl.CostEstimate(
            flops=10 * rows * rows * width, bytes_accessed=30 * rows * width, transcendentals=0
        ),
        name="section",
    )(*pieces, taps, fwd, inv, spec, *more)


def phase_table(row_count, col_count, modulus, direction):
    row_ids = lax.broadcasted_iota(jnp.int32, (row_count, col_count), 0)
    col_ids = lax.broadcasted_iota(jnp.int32, (row_count, col_count), 1)
    residue = row_ids * col_ids % modulus
    angles = direction * 2.0 * math.pi / modulus * residue.astype(jnp.float32)
    return (jnp.cos(angles), jnp.sin(angles))


def highest(pattern, first_op, second_op):
    return jnp.einsum(pattern, first_op, second_op, precision=lax.Precision.HIGHEST)


def forward_spectrum(signal, half_q, width_p):
    full_q = 2 * half_q
    blocks = signal.reshape(half_q, width_p, signal.shape[1])
    fq_re, fq_im = phase_table(full_q, half_q, full_q, -1.0)
    section_re = highest("kq,qpc->kpc", fq_re, blocks)
    section_im = highest("kq,qpc->kpc", fq_im, blocks)
    tw_re, tw_im = phase_table(full_q, width_p, full_q * width_p, -1.0)
    turned_re = section_re * tw_re[:, :, None] - section_im * tw_im[:, :, None]
    turned_im = section_re * tw_im[:, :, None] + section_im * tw_re[:, :, None]
    fp_re, fp_im = phase_table(width_p, width_p, width_p, -1.0)
    out_re = highest("jp,kpc->jkc", fp_re, turned_re) - highest("jp,kpc->jkc", fp_im, turned_im)
    out_im = highest("jp,kpc->jkc", fp_re, turned_im) + highest("jp,kpc->jkc", fp_im, turned_re)
    return (out_re, out_im)


def inverse_field(spec_re, spec_im, half_q, width_p):
    full_q = 2 * half_q
    gp_re, gp_im = phase_table(width_p, width_p, width_p, 1.0)
    section_re = highest("mn,nqc->mqc", gp_re, spec_re) - highest("mn,nqc->mqc", gp_im, spec_im)
    section_im = highest("mn,nqc->mqc", gp_re, spec_im) + highest("mn,nqc->mqc", gp_im, spec_re)
    tw_re, tw_im = phase_table(width_p, full_q, full_q * width_p, 1.0)
    turned_re = section_re * tw_re[:, :, None] - section_im * tw_im[:, :, None]
    turned_im = section_re * tw_im[:, :, None] + section_im * tw_re[:, :, None]
    gq_re, gq_im = phase_table(half_q, full_q, full_q, 1.0)
    result = highest("aq,mqc->amc", gq_re, turned_re) - highest("aq,mqc->amc", gq_im, turned_im)
    return result.reshape(half_q * width_p, spec_re.shape[2]) / (full_q * width_p)


def large_section(x, g, taps, kernel, half_q):
    rows = x.shape[0]
    width_p = rows // half_q
    signal, upstream = x.astype(jnp.float32), g.astype(jnp.float32)
    moved = [jnp.pad(signal, ((i, 0), (0, 0)))[:rows] for i in range(3)]
    query, key, value = (
        sum(taps[3 * s + i] * moved[i] for i in range(3)).astype(jnp.bfloat16).astype(jnp.float32)
        for s in range(3)
    )
    p_re, p_im = forward_spectrum(key * value, half_q, width_p)
    a_re, a_im = forward_spectrum(upstream * query, half_q, width_p)
    h_re, h_im = forward_spectrum(kernel, half_q, width_p)
    combined = inverse_field(
        p_re * h_re - p_im * h_im, p_re * h_im + p_im * h_re, half_q, width_p
    )
    backward = inverse_field(
        h_re * a_re + h_im * a_im, h_re * a_im - h_im * a_re, half_q, width_p
    )
    filter_grad = inverse_field(
        p_re * a_re + p_im * a_im, p_re * a_im - p_im * a_re, half_q, width_p
    )
    grads = (upstream * combined, backward * value, backward * key)
    total = jnp.zeros_like(signal)
    for s in range(3):
        grad = grads[s].astype(jnp.bfloat16).astype(jnp.float32)
        for i in range(3):
            total = total + taps[3 * s + i] * jnp.pad(grad, ((0, i), (0, 0)))[i:]
    return total.astype(jnp.bfloat16), filter_grad * (1.0 / math.sqrt(rows))


def exchanged(chunk, devices, whole):
    if whole:
        return [lax.all_to_all(chunk[0], "seq", split_axis=0, concat_axis=0, tiled=True)]
    pairs = lambda k: [(i, i ^ k) for i in range(devices)]
    return [chunk[0]] + [lax.ppermute(chunk[k], "seq", pairs(k)) for k in range(1, devices)]


def fast(inputs, upstream, kernel, taps):
    devices, count = lax.axis_size("seq"), lax.axis_size("pipe")
    before = [(p, (p - 1) % count) for p in range(count)]
    arrived = [
        exchanged(chunk, devices, whole)
        for chunk, whole in zip(pack(inputs, upstream, devices, WHOLE_IN), WHOLE_IN)
    ]
    fwd, inv = quarter_tables(kernel.shape[0])
    spec = spectrum(kernel, fwd)
    filter_grad, home = None, []
    for chunk in range(CHUNKS):
        whole = WHOLE_OUT[chunk]
        grad, filter_grad = section(
            arrived[chunk], taps, fwd, inv, spec, chunk, filter_grad,
            devices, WHOLE_IN[chunk], whole,
        )
        grad = lax.ppermute(grad, "pipe", before)
        home.append(
            exchanged([grad] if whole else [grad[k] for k in range(devices)], devices, whole)
        )
    return unpack(home, devices, WHOLE_OUT), filter_grad[None]


def general(inputs, upstream, kernel, taps):
    devices, count = lax.axis_size("seq"), lax.axis_size("pipe")
    length_dev, model = inputs.shape
    rows, width = kernel.shape
    to_columns = lambda block: block.reshape(length_dev, devices, width).transpose(1, 0, 2)
    sent = jnp.stack([to_columns(inputs), to_columns(upstream)], axis=1)
    got = lax.all_to_all(sent, "seq", split_axis=0, concat_axis=0, tiled=True)
    x_cols, g_cols = got[:, 0].reshape(rows, width), got[:, 1].reshape(rows, width)
    grad_cols, filter_grad = large_section(x_cols, g_cols, taps, kernel, devices)
    back = lax.all_to_all(
        grad_cols.reshape(devices, length_dev, width), "seq", split_axis=0, concat_axis=0, tiled=True
    )
    grad_input = back.transpose(1, 0, 2).reshape(length_dev, model)
    received = lax.ppermute(
        grad_input[None], "pipe", [((i + 1) % count, i) for i in range(count)]
    )
    return received, filter_grad[None]


def shards(section_input, out_grad, conv_filter, short_taps):
    inputs, upstream, kernel = section_input[0], out_grad[0], conv_filter[0]
    devices = lax.axis_size("seq")
    model = inputs.shape[1]
    rows, width = kernel.shape
    dense = (
        rows <= DENSE_ROWS
        and rows % 256 == 0
        and width % (CHUNKS * 128) == 0
        and devices & (devices - 1) == 0
    )
    if dense:
        return fast(inputs, upstream, kernel, short_taps)
    taps = lax.dynamic_slice_in_dim(
        short_taps[0].reshape(-1, model), lax.axis_index("seq") * width, width, axis=1
    )
    return general(inputs, upstream, kernel, taps)


def solution(mesh):
    return jax.shard_map(
        shards,
        mesh=mesh,
        in_specs=(
            P("pipe", "seq", None),
            P("pipe", "seq", None),
            P("pipe", None, "seq"),
            P("pipe", None, None, None),
        ),
        out_specs=(P("pipe", "seq", None), P("pipe", None, "seq")),
        check_vma=False,
    )
```

time: 425 us -> 73.5 us (0.17); the launches traced: 420 us -> 73.2 us
  matrix products: 256 us -> 0 us
  waiting for transfers between devices: 68.1 us -> 15.6 us
  other arithmetic: 32.5 us -> 0 us
  local copies, waits for them, and re-layouts: 33.7 us -> 5.23 us
  Pallas kernels: 0 us -> 19.9 us
    dot_general x36 -> x0, matrix products: 256 us -> none  [highest(): jnp.einsum(pattern, first_op, second_op, precision=lax.Precision.HIGHEST)]
    all_to_all x4 -> x1, waiting for transfers between devices: 56.9 us -> 0.01 us  [exchanged(): lax.all_to_all(chunk[0], 'seq', split_axis=0, concat_axis=0, tiled=True)]
    pallas_call x0 -> x5, Pallas kernels: none -> 19.9 us  [the longest x2 16.2 us: section(): pl.pallas_call(functools.partial(section_kernel, devices, chunk, len(more...]
    ppermute x5 -> x23, starting transfers between devices: 10.1 us -> 28.3 us  [the longest x21 24.2 us: exchanged(): lax.ppermute(chunk[k], 'seq', pairs(k))]
    all_to_all x4 -> x1, starting transfers between devices: 18.7 us -> 3.49 us  [exchanged(): lax.all_to_all(chunk[0], 'seq', split_axis=0, concat_axis=0, tiled=True)]
    convert_element_type x6 -> x0, other arithmetic: 13 us -> none  [the longest x3 6.32 us: shards(): jnp.concatenate([grad_list[stream_idx], later_rows[stream_idx]], axis=0)]
    all_to_all x4 -> x0, local copies, waits for them, and re-layouts: 11.7 us -> none  [the longest x1 2.94 us: shards(): lax.all_to_all(mixed_cols, 'seq', split_axis=0, concat_axis=1, tiled=True)]
    broadcast_in_dim x1 -> x0, other arithmetic: 10.9 us -> none  [shards(): received = shifted(grad_input[None], 'pipe', -1)]
  transfers between devices with their start and end apart: 9 -> 24, of which waited for: 5 -> 8; matrix products, arithmetic and copies ran while one was open for 19% -> 1% of each run, Pallas kernels for 0% -> 25%
where the time goes in v3:
time: 73.5 us; the launch traced here: 73.2 us
  starting transfers between devices  31.8 us (43%)
  Pallas kernels  19.9 us (27%)
  waiting for transfers between devices  15.6 us (21%)
  local copies, waits for them, and re-layouts  5.23 us (7%)
  between operations  0.76 us (1%)
    ppermute x21, starting transfers between devices, exchanged(): lax.ppermute(chunk[k], 'seq', pairs(k))  24.2 us
    pallas_call x2, Pallas kernels, section(): pl.pallas_call(functools.partial(section_kernel, devices, chunk, len(more...  16.2 us
    ppermute x2, waiting for transfers between devices, fast(): grad = lax.ppermute(grad, 'pipe', before)  10.7 us
    unnamed x11, local copies, waits for them, and re-layouts  5.2 us
    ppermute x21, waiting for transfers between devices, exchanged(): lax.ppermute(chunk[k], 'seq', pairs(k))  4.9 us
    ppermute x2, starting transfers between devices, fast(): grad = lax.ppermute(grad, 'pipe', before)  4.16 us
    all_to_all x1, starting transfers between devices, exchanged(): lax.all_to_all(chunk[0], 'seq', split_axis=0, concat_axis=0, tiled=True)  3.49 us
    pallas_call x1, Pallas kernels, spectrum(): pl.pallas_call(spectrum_kernel, in_specs=[near] * 2, out_specs=near, out_...  1.83 us
  transfers between devices with their start and end apart: 24, of which 8 were waited for; matrix products, arithmetic and copies ran while one was open for 1% of the time, Pallas kernels for 25%

profile of v3, /device:TPU:0, one launch (start us, length us, event | category | flops | bytes accessed | tf_op | source)
XLA Modules:
  0.0 73.2 jit_solution(18079799246552236306)
XLA Ops:
  0.6 0.0 copy-start
  0.6 0.0 copy-start.3
  0.7 1.4 %copy-done.3 = bf16[1,128,4096]{2,1,0:T(8,128)(2,1)S(1)} copy-done((bf16[1,128,4096]{2,1,0:T(8,128)(2,1)S(1)}, bf16[1,128,4096]{2,1,0:T(8,128)(2,1)}, u32[]{:S(2)}) %copy-start.3) | copy-done | bytes 1048600
  2.0 0.0 copy-start.4
  2.0 1.2 %copy-done.4 = bf16[1,128,4096]{2,1,0:T(8,128)(2,1)S(1)} copy-done((bf16[1,128,4096]{2,1,0:T(8,128)(2,1)S(1)}, bf16[1,128,4096]{2,1,0:T(8,128)(2,1)}, u32[]{:S(2)}) %copy-start.4) | copy-done | bytes 1048600
  3.2 0.7 pack.1
  4.0 0.5 collective-permute-start
  4.5 2.6 %collective-permute-start.1 = (bf16[2,128,256]{2,1,0:T(8,128)(2,1)S(1)}, bf16[2,128,256]{2,1,0:T(8,128)(2,1)S(1)}, u32[]{:S(2)}, u32[]{:S(2)}) collective-permute-start(bf16[2,128,256]{2,1,0:T(8,128)(2,1)S(1)} %get-tuple-element.24), channel_id=1, source_target_pairs={{0,8},{4,12},{8,0},{12,4},{16,24},{20,28},{24,16},{28,20},{1,9},{5... | collective-permute-start | bytes 393224 | tf_op jit(solution)/shard_map/ppermute | solution.py:400
  7.1 0.1 collective-permute-start.2
  7.1 1.8 %collective-permute-start.3 = (bf16[2,128,256]{2,1,0:T(8,128)(2,1)S(1)}, bf16[2,128,256]{2,1,0:T(8,128)(2,1)S(1)}, u32[]{:S(2)}, u32[]{:S(2)}) collective-permute-start(bf16[2,128,256]{2,1,0:T(8,128)(2,1)S(1)} %get-tuple-element.26), channel_id=1, source_target_pairs={{0,16},{4,20},{8,24},{12,28},{16,0},{20,4},{24,8},{28,12},{1,17},{... | collective-permute-start | bytes 393224 | tf_op jit(solution)/shard_map/ppermute | solution.py:400
  8.9 0.0 collective-permute-start.4
  8.9 0.0 collective-permute-done.refs_1_
  8.9 2.6 %collective-permute-start.5 = (bf16[2,128,256]{2,1,0:T(8,128)(2,1)S(1)}, bf16[2,128,256]{2,1,0:T(8,128)(2,1)S(1)}, u32[]{:S(2)}, u32[]{:S(2)}) collective-permute-start(bf16[2,128,256]{2,1,0:T(8,128)(2,1)S(1)} %get-tuple-element.28), channel_id=1, source_target_pairs={{0,24},{4,28},{8,16},{12,20},{16,8},{20,12},{24,0},{28,4},{1,25},{... | collective-permute-start | bytes 393224 | tf_op jit(solution)/shard_map/ppermute | solution.py:400
  11.5 0.0 collective-permute-done.1.refs_2_
  11.5 1.6 %collective-permute-start.6 = (bf16[2,128,256]{2,1,0:T(8,128)(2,1)S(1)}, bf16[2,128,256]{2,1,0:T(8,128)(2,1)S(1)}, u32[]{:S(2)}, u32[]{:S(2)}) collective-permute-start(bf16[2,128,256]{2,1,0:T(8,128)(2,1)S(1)} %get-tuple-element.29), channel_id=1, source_target_pairs={{0,28},{4,24},{8,20},{12,16},{16,12},{20,8},{24,4},{28,0},{1,29},{... | collective-permute-start | bytes 393224 | tf_op jit(solution)/shard_map/ppermute | solution.py:400
  13.1 0.6 collective-permute-done.2.refs_3_
  13.7 0.7 %collective-permute-start.8 = (bf16[2,128,256]{2,1,0:T(8,128)(2,1)S(1)}, bf16[2,128,256]{2,1,0:T(8,128)(2,1)S(1)}, u32[]{:S(2)}, u32[]{:S(2)}) collective-permute-start(bf16[2,128,256]{2,1,0:T(8,128)(2,1)S(1)} %get-tuple-element.32), channel_id=1, source_target_pairs={{0,4},{4,0},{8,12},{12,8},{16,20},{20,16},{24,28},{28,24},{1,5},{5... | collective-permute-start | bytes 393224 | tf_op jit(solution)/shard_map/ppermute | solution.py:400
  14.4 0.0 collective-permute-done.3.refs_4_
  14.4 1.8 %collective-permute-start.9 = (bf16[2,128,256]{2,1,0:T(8,128)(2,1)S(1)}, bf16[2,128,256]{2,1,0:T(8,128)(2,1)S(1)}, u32[]{:S(2)}, u32[]{:S(2)}) collective-permute-start(bf16[2,128,256]{2,1,0:T(8,128)(2,1)S(1)} %get-tuple-element.33), channel_id=1, source_target_pairs={{0,8},{4,12},{8,0},{12,4},{16,24},{20,28},{24,16},{28,20},{1,9},{5... | collective-permute-start | bytes 393224 | tf_op jit(solution)/shard_map/ppermute | solution.py:400
  16.3 1.0 %copy.9.refs_8_ = f32[1,3,3,4096]{3,2,1,0:T(4,128)S(1)} copy(f32[1,3,3,4096]{3,0,2,1:T(1,128)} %param.9) | data formatting | bytes 294912 | tf_op args[3]
  17.3 0.0 copy-done
  17.3 0.0 copy-start.1
  17.3 1.6 %copy-done.1 = f32[1,1024,512]{2,1,0:T(8,128)S(1)} copy-done((f32[1,1024,512]{2,1,0:T(8,128)S(1)}, f32[1,1024,512]{2,1,0:T(8,128)}, u32[]{:S(2)}) %copy-start.1) | copy-done | bytes 2097176
  18.9 0.0 copy-start.2
  18.9 1.8 %spectrum.1.refs_11_ = f32[4,512,512]{2,1,0:T(8,128)S(1)} custom-call(f32[1024,512]{1,0:T(8,128)S(1)} %bitcast.20, bf16[4,512,512]{2,1,0:T(8,128)(2,1)S(1)} %copy-done), custom_call_target="tpu_custom_call" | custom-call | flops 1073741824 | bytes 7340032 | tf_op jit(solution)/shard_map/spectrum/pallas_call | solution.py:173
  20.7 0.0 collective-permute-done.4.refs_5_
  20.7 2.0 %collective-permute-start.10 = (bf16[2,128,256]{2,1,0:T(8,128)(2,1)S(1)}, bf16[2,128,256]{2,1,0:T(8,128)(2,1)S(1)}, u32[]{:S(2)}, u32[]{:S(2)}) collective-permute-start(bf16[2,128,256]{2,1,0:T(8,128)(2,1)S(1)} %get-tuple-element.34), channel_id=1, source_target_pairs={{0,12},{4,8},{8,4},{12,0},{16,28},{20,24},{24,20},{28,16},{1,13},{... | collective-permute-start | bytes 393224 | tf_op jit(solution)/shard_map/ppermute | solution.py:400
  22.7 0.0 collective-permute-done.5.refs_6_
  22.8 1.5 %collective-permute-start.11 = (bf16[2,128,256]{2,1,0:T(8,128)(2,1)S(1)}, bf16[2,128,256]{2,1,0:T(8,128)(2,1)S(1)}, u32[]{:S(2)}, u32[]{:S(2)}) collective-permute-start(bf16[2,128,256]{2,1,0:T(8,128)(2,1)S(1)} %get-tuple-element.35), channel_id=1, source_target_pairs={{0,16},{4,20},{8,24},{12,28},{16,0},{20,4},{24,8},{28,12},{1,17},{... | collective-permute-start | bytes 393224 | tf_op jit(solution)/shard_map/ppermute | solution.py:400
  24.3 0.0 collective-permute-done.6.refs_7_
  24.3 0.0 collective-permute-start.12
  24.3 0.0 collective-permute-done.8.refs_1_
  24.3 1.2 %collective-permute-start.13 = (bf16[2,128,256]{2,1,0:T(8,128)(2,1)S(1)}, bf16[2,128,256]{2,1,0:T(8,128)(2,1)S(1)}, u32[]{:S(2)}, u32[]{:S(2)}) collective-permute-start(bf16[2,128,256]{2,1,0:T(8,128)(2,1)S(1)} %get-tuple-element.37), channel_id=1, source_target_pairs={{0,24},{4,28},{8,16},{12,20},{16,8},{20,12},{24,0},{28,4},{1,25},{... | collective-permute-start | bytes 393224 | tf_op jit(solution)/shard_map/ppermute | solution.py:400
  25.5 0.0 collective-permute-done.9.refs_2_
  25.5 1.7 %collective-permute-start.14 = (bf16[2,128,256]{2,1,0:T(8,128)(2,1)S(1)}, bf16[2,128,256]{2,1,0:T(8,128)(2,1)S(1)}, u32[]{:S(2)}, u32[]{:S(2)}) collective-permute-start(bf16[2,128,256]{2,1,0:T(8,128)(2,1)S(1)} %get-tuple-element.38), channel_id=1, source_target_pairs={{0,28},{4,24},{8,20},{12,16},{16,12},{20,8},{24,4},{28,0},{1,29},{... | collective-permute-start | bytes 393224 | tf_op jit(solution)/shard_map/ppermute | solution.py:400
  27.2 0.0 copy-done.2
  27.2 8.1 %section.2 = (bf16[8,128,256]{2,1,0:T(8,128)(2,1)S(1)}, f32[1024,512]{1,0:T(8,128)}) custom-call(bf16[2,128,256]{2,1,0:T(8,128)(2,1)S(1)} %get-tuple-element.22.refs_0_, bf16[2,128,256]{2,1,0:T(8,128)(2,1)S(1)} %collective-permute-done.refs_1_, bf16[2,128,256]{2,1,0:T(8,128)(2,1)S(1)} %collective-permute-done.1.refs_2_, ...), custom_call_target="tpu_custom_call" | custom-call | flops 2684354560 | bytes 7864320 | tf_op jit(solution)/shard_map/section/pallas_call | solution.py:294
  35.3 0.0 collective-permute-done.10.refs_3_
  35.3 3.7 %collective-permute-start.7 = (bf16[8,128,256]{2,1,0:T(8,128)(2,1)S(1)}, bf16[8,128,256]{2,1,0:T(8,128)(2,1)}, u32[]{:S(2)}, u32[]{:S(2)}) collective-permute-start(bf16[8,128,256]{2,1,0:T(8,128)(2,1)S(1)} %get-tuple-element.30), channel_id=1, source_target_pairs={{0,3},{1,0},{2,1},{3,2},{4,7},{5,4},{6,5},{7,6},{8,11},{9,8},{10,9... | collective-permute-start | bytes 1572872 | tf_op jit(solution)/shard_map/ppermute | solution.py:419
  38.9 0.0 collective-permute-done.11.refs_4_
  38.9 0.0 collective-permute-done.12.refs_5_
  38.9 0.0 collective-permute-done.13.refs_6_
  38.9 0.0 collective-permute-done.14.refs_7_
  38.9 8.1 %section.3 = (bf16[8,128,256]{2,1,0:T(8,128)(2,1)S(1)}, f32[1024,512]{1,0:T(8,128)}) custom-call(bf16[2,128,256]{2,1,0:T(8,128)(2,1)S(1)} %get-tuple-element.31.refs_0_, bf16[2,128,256]{2,1,0:T(8,128)(2,1)S(1)} %collective-permute-done.8.refs_1_, bf16[2,128,256]{2,1,0:T(8,128)(2,1)S(1)} %collective-permute-done.9.refs_2_, ...), custom_call_target="tpu_custom_call", output_to_operand_aliasing={{1}: (12, {})} | custom-call | flops 2684354560 | bytes 7864320 | tf_op jit(solution)/shard_map/section/pallas_call | solution.py:294
  47.1 0.5 collective-permute-start.15
  47.6 3.6 %collective-permute-done.7 = bf16[8,128,256]{2,1,0:T(8,128)(2,1)} collective-permute-done((bf16[8,128,256]{2,1,0:T(8,128)(2,1)S(1)}, bf16[8,128,256]{2,1,0:T(8,128)(2,1)}, u32[]{:S(2)}, u32[]{:S(2)}) %collective-permute-start.7) | collective-permute-done | bytes 524320 | tf_op jit(solution)/shard_map/ppermute | solution.py:419
  51.2 3.5 %all-to-all-start = ((bf16[8,128,256]{2,1,0:T(8,128)(2,1)}), bf16[8,128,256]{2,1,0:T(8,128)(2,1)S(1)}, u32[]{:S(2)}, u32[]{:S(2)}) async-start(bf16[8,128,256]{2,1,0:T(8,128)(2,1)} %collective-permute-done.7), calls=%async_computation | async-start | bytes 1048576 | tf_op jit(solution)/shard_map/all_to_all | solution.py:398
  54.7 7.0 %collective-permute-done.15 = bf16[8,128,256]{2,1,0:T(8,128)(2,1)S(1)} collective-permute-done((bf16[8,128,256]{2,1,0:T(8,128)(2,1)S(1)}, bf16[8,128,256]{2,1,0:T(8,128)(2,1)S(1)}, u32[]{:S(2)}, u32[]{:S(2)}) %collective-permute-start.15) | collective-permute-done | bytes 524320 | tf_op jit(solution)/shard_map/ppermute | solution.py:419
  61.8 0.1 collective-permute-start.16
  61.9 0.6 collective-permute-start.17
  62.5 1.3 %collective-permute-start.18 = (bf16[128,256]{1,0:T(8,128)(2,1)S(1)}, bf16[128,256]{1,0:T(8,128)(2,1)S(1)}, u32[]{:S(2)}, u32[]{:S(2)}) collective-permute-start(bf16[128,256]{1,0:T(8,128)(2,1)S(1)} %get-tuple-element.46), channel_id=1, source_target_pairs={{0,12},{4,8},{8,4},{12,0},{16,28},{20,24},{24,20},{28,16},{1,13},{... | collective-permute-start | bytes 196616 | tf_op jit(solution)/shard_map/ppermute | solution.py:400
  63.7 1.1 %collective-permute-start.19 = (bf16[128,256]{1,0:T(8,128)(2,1)S(1)}, bf16[128,256]{1,0:T(8,128)(2,1)S(1)}, u32[]{:S(2)}, u32[]{:S(2)}) collective-permute-start(bf16[128,256]{1,0:T(8,128)(2,1)S(1)} %get-tuple-element.45), channel_id=1, source_target_pairs={{0,16},{4,20},{8,24},{12,28},{16,0},{20,4},{24,8},{28,12},{1,17},{... | collective-permute-start | bytes 196616 | tf_op jit(solution)/shard_map/ppermute | solution.py:400
  64.8 0.6 collective-permute-start.20
  65.4 0.0 collective-permute-done.16.refs_2_
  65.4 1.1 %collective-permute-start.21 = (bf16[128,256]{1,0:T(8,128)(2,1)S(1)}, bf16[128,256]{1,0:T(8,128)(2,1)S(1)}, u32[]{:S(2)}, u32[]{:S(2)}) collective-permute-start(bf16[128,256]{1,0:T(8,128)(2,1)S(1)} %get-tuple-element.43), channel_id=1, source_target_pairs={{0,24},{4,28},{8,16},{12,20},{16,8},{20,12},{24,0},{28,4},{1,25},{... | collective-permute-start | bytes 196616 | tf_op jit(solution)/shard_map/ppermute | solution.py:400
  66.5 0.3 collective-permute-done.17.refs_3_
  66.8 1.3 %collective-permute-start.22 = (bf16[128,256]{1,0:T(8,128)(2,1)S(1)}, bf16[128,256]{1,0:T(8,128)(2,1)S(1)}, u32[]{:S(2)}, u32[]{:S(2)}) collective-permute-start(bf16[128,256]{1,0:T(8,128)(2,1)S(1)} %get-tuple-element.42), channel_id=1, source_target_pairs={{0,28},{4,24},{8,20},{12,16},{16,12},{20,8},{24,4},{28,0},{1,29},{... | collective-permute-start | bytes 196616 | tf_op jit(solution)/shard_map/ppermute | solution.py:400
  68.1 0.0 collective-permute-done.18.refs_4_
  68.1 0.3 collective-permute-done.19.refs_5_
  68.4 0.8 %collective-permute-done.20.refs_6_ = bf16[128,256]{1,0:T(8,128)(2,1)S(1)} collective-permute-done((bf16[128,256]{1,0:T(8,128)(2,1)S(1)}, bf16[128,256]{1,0:T(8,128)(2,1)S(1)}, u32[]{:S(2)}, u32[]{:S(2)}) %collective-permute-start.20) | collective-permute-done | bytes 65568 | tf_op jit(solution)/shard_map/ppermute | solution.py:400
  69.2 1.8 %collective-permute-done.21.refs_7_ = bf16[128,256]{1,0:T(8,128)(2,1)S(1)} collective-permute-done((bf16[128,256]{1,0:T(8,128)(2,1)S(1)}, bf16[128,256]{1,0:T(8,128)(2,1)S(1)}, u32[]{:S(2)}, u32[]{:S(2)}) %collective-permute-start.21) | collective-permute-done | bytes 65568 | tf_op jit(solution)/shard_map/ppermute | solution.py:400
  71.0 1.1 %collective-permute-done.22.refs_8_ = bf16[128,256]{1,0:T(8,128)(2,1)S(1)} collective-permute-done((bf16[128,256]{1,0:T(8,128)(2,1)S(1)}, bf16[128,256]{1,0:T(8,128)(2,1)S(1)}, u32[]{:S(2)}, u32[]{:S(2)}) %collective-permute-start.22) | collective-permute-done | bytes 65568 | tf_op jit(solution)/shard_map/ppermute | solution.py:400
  72.1 0.0 all-to-all-done.refs_0_
  72.1 1.1 %unpack.1 = bf16[1,128,4096]{2,1,0:T(8,128)(2,1)} custom-call(bf16[8,128,256]{2,1,0:T(8,128)(2,1)S(1)} %all-to-all-done.refs_0_, bf16[128,256]{1,0:T(8,128)(2,1)S(1)} %get-tuple-element.49.refs_1_, bf16[128,256]{1,0:T(8,128)(2,1)S(1)} %collective-permute-done.16.refs_2_, bf16[128,256]{1,0:T(8,128)(2,1)S(1)} %collective-permute-done.17.refs_3_, ...), custom_call_target="tpu_custom_call" | custom-call | tf_op jit(solution)/shard_map/unpack/pallas_call | solution.py:143
  (1 shorter events, 0.0 us)
Async XLA Ops:
  0.6 16.7 %copy-start = (bf16[4,512,512]{2,1,0:T(8,128)(2,1)S(1)}, bf16[4,512,512]{2,1,0:T(8,128)(2,1)}, u32[]{:S(2)}) copy-start(bf16[4,512,512]{2,1,0:T(8,128)(2,1)} %constant.4.clone.fwd_ref.refs_9_) | copy-start | bytes 6291460
  0.6 1.4 %copy-start.3 = (bf16[1,128,4096]{2,1,0:T(8,128)(2,1)S(1)}, bf16[1,128,4096]{2,1,0:T(8,128)(2,1)}, u32[]{:S(2)}) copy-start(bf16[1,128,4096]{2,1,0:T(8,128)(2,1)} %param.6) | copy-start | bytes 3145732
  2.0 1.2 %copy-start.4 = (bf16[1,128,4096]{2,1,0:T(8,128)(2,1)S(1)}, bf16[1,128,4096]{2,1,0:T(8,128)(2,1)}, u32[]{:S(2)}) copy-start(bf16[1,128,4096]{2,1,0:T(8,128)(2,1)} %param.7) | copy-start | bytes 3145732
  4.0 4.9 %collective-permute-start = (bf16[2,128,256]{2,1,0:T(8,128)(2,1)S(1)}, bf16[2,128,256]{2,1,0:T(8,128)(2,1)S(1)}, u32[]{:S(2)}, u32[]{:S(2)}) collective-permute-start(bf16[2,128,256]{2,1,0:T(8,128)(2,1)S(1)} %get-tuple-element.23), channel_id=1, source_target_pairs={{0,4},{4,0},{8,12},{12,8},{16,20},{20,16},{24,28},{28,24},{1,5},{5... | collective-permute-start | bytes 393224 | tf_op jit(solution)/shard_map/ppermute | solution.py:400
  4.5 7.0 %collective-permute-start.1 = (bf16[2,128,256]{2,1,0:T(8,128)(2,1)S(1)}, bf16[2,128,256]{2,1,0:T(8,128)(2,1)S(1)}, u32[]{:S(2)}, u32[]{:S(2)}) collective-permute-start(bf16[2,128,256]{2,1,0:T(8,128)(2,1)S(1)} %get-tuple-element.24), channel_id=1, source_target_pairs={{0,8},{4,12},{8,0},{12,4},{16,24},{20,28},{24,16},{28,20},{1,9},{5... | collective-permute-start | bytes 393224 | tf_op jit(solution)/shard_map/ppermute | solution.py:400
  7.1 6.6 %collective-permute-start.2 = (bf16[2,128,256]{2,1,0:T(8,128)(2,1)S(1)}, bf16[2,128,256]{2,1,0:T(8,128)(2,1)S(1)}, u32[]{:S(2)}, u32[]{:S(2)}) collective-permute-start(bf16[2,128,256]{2,1,0:T(8,128)(2,1)S(1)} %get-tuple-element.25), channel_id=1, source_target_pairs={{0,12},{4,8},{8,4},{12,0},{16,28},{20,24},{24,20},{28,16},{1,13},{... | collective-permute-start | bytes 393224 | tf_op jit(solution)/shard_map/ppermute | solution.py:400
  7.1 7.3 %collective-permute-start.3 = (bf16[2,128,256]{2,1,0:T(8,128)(2,1)S(1)}, bf16[2,128,256]{2,1,0:T(8,128)(2,1)S(1)}, u32[]{:S(2)}, u32[]{:S(2)}) collective-permute-start(bf16[2,128,256]{2,1,0:T(8,128)(2,1)S(1)} %get-tuple-element.26), channel_id=1, source_target_pairs={{0,16},{4,20},{8,24},{12,28},{16,0},{20,4},{24,8},{28,12},{1,17},{... | collective-permute-start | bytes 393224 | tf_op jit(solution)/shard_map/ppermute | solution.py:400
  8.9 11.8 %collective-permute-start.4 = (bf16[2,128,256]{2,1,0:T(8,128)(2,1)S(1)}, bf16[2,128,256]{2,1,0:T(8,128)(2,1)S(1)}, u32[]{:S(2)}, u32[]{:S(2)}) collective-permute-start(bf16[2,128,256]{2,1,0:T(8,128)(2,1)S(1)} %get-tuple-element.27), channel_id=1, source_target_pairs={{0,20},{4,16},{8,28},{12,24},{16,4},{20,0},{24,12},{28,8},{1,21},{... | collective-permute-start | bytes 393224 | tf_op jit(solution)/shard_map/ppermute | solution.py:400
  8.9 13.8 %collective-permute-start.5 = (bf16[2,128,256]{2,1,0:T(8,128)(2,1)S(1)}, bf16[2,128,256]{2,1,0:T(8,128)(2,1)S(1)}, u32[]{:S(2)}, u32[]{:S(2)}) collective-permute-start(bf16[2,128,256]{2,1,0:T(8,128)(2,1)S(1)} %get-tuple-element.28), channel_id=1, source_target_pairs={{0,24},{4,28},{8,16},{12,20},{16,8},{20,12},{24,0},{28,4},{1,25},{... | collective-permute-start | bytes 393224 | tf_op jit(solution)/shard_map/ppermute | solution.py:400
  11.5 12.8 %collective-permute-start.6 = (bf16[2,128,256]{2,1,0:T(8,128)(2,1)S(1)}, bf16[2,128,256]{2,1,0:T(8,128)(2,1)S(1)}, u32[]{:S(2)}, u32[]{:S(2)}) collective-permute-start(bf16[2,128,256]{2,1,0:T(8,128)(2,1)S(1)} %get-tuple-element.29), channel_id=1, source_target_pairs={{0,28},{4,24},{8,20},{12,16},{16,12},{20,8},{24,4},{28,0},{1,29},{... | collective-permute-start | bytes 393224 | tf_op jit(solution)/shard_map/ppermute | solution.py:400
  13.7 10.6 %collective-permute-start.8 = (bf16[2,128,256]{2,1,0:T(8,128)(2,1)S(1)}, bf16[2,128,256]{2,1,0:T(8,128)(2,1)S(1)}, u32[]{:S(2)}, u32[]{:S(2)}) collective-permute-start(bf16[2,128,256]{2,1,0:T(8,128)(2,1)S(1)} %get-tuple-element.32), channel_id=1, source_target_pairs={{0,4},{4,0},{8,12},{12,8},{16,20},{20,16},{24,28},{28,24},{1,5},{5... | collective-permute-start | bytes 393224 | tf_op jit(solution)/shard_map/ppermute | solution.py:400
  14.4 11.0 %collective-permute-start.9 = (bf16[2,128,256]{2,1,0:T(8,128)(2,1)S(1)}, bf16[2,128,256]{2,1,0:T(8,128)(2,1)S(1)}, u32[]{:S(2)}, u32[]{:S(2)}) collective-permute-start(bf16[2,128,256]{2,1,0:T(8,128)(2,1)S(1)} %get-tuple-element.33), channel_id=1, source_target_pairs={{0,8},{4,12},{8,0},{12,4},{16,24},{20,28},{24,16},{28,20},{1,9},{5... | collective-permute-start | bytes 393224 | tf_op jit(solution)/shard_map/ppermute | solution.py:400
  17.3 1.6 %copy-start.1 = (f32[1,1024,512]{2,1,0:T(8,128)S(1)}, f32[1,1024,512]{2,1,0:T(8,128)}, u32[]{:S(2)}) copy-start(f32[1,1024,512]{2,1,0:T(8,128)} %param.8) | copy-start | bytes 6291460
  18.9 8.3 %copy-start.2 = (bf16[4,512,512]{2,1,0:T(8,128)(2,1)S(1)}, bf16[4,512,512]{2,1,0:T(8,128)(2,1)}, u32[]{:S(2)}) copy-start(bf16[4,512,512]{2,1,0:T(8,128)(2,1)} %constant.5.clone.refs_10_) | copy-start | bytes 6291460
  20.7 14.5 %collective-permute-start.10 = (bf16[2,128,256]{2,1,0:T(8,128)(2,1)S(1)}, bf16[2,128,256]{2,1,0:T(8,128)(2,1)S(1)}, u32[]{:S(2)}, u32[]{:S(2)}) collective-permute-start(bf16[2,128,256]{2,1,0:T(8,128)(2,1)S(1)} %get-tuple-element.34), channel_id=1, source_target_pairs={{0,12},{4,8},{8,4},{12,0},{16,28},{20,24},{24,20},{28,16},{1,13},{... | collective-permute-start | bytes 393224 | tf_op jit(solution)/shard_map/ppermute | solution.py:400
  22.8 16.2 %collective-permute-start.11 = (bf16[2,128,256]{2,1,0:T(8,128)(2,1)S(1)}, bf16[2,128,256]{2,1,0:T(8,128)(2,1)S(1)}, u32[]{:S(2)}, u32[]{:S(2)}) collective-permute-start(bf16[2,128,256]{2,1,0:T(8,128)(2,1)S(1)} %get-tuple-element.35), channel_id=1, source_target_pairs={{0,16},{4,20},{8,24},{12,28},{16,0},{20,4},{24,8},{28,12},{1,17},{... | collective-permute-start | bytes 393224 | tf_op jit(solution)/shard_map/ppermute | solution.py:400
  24.3 14.7 %collective-permute-start.12 = (bf16[2,128,256]{2,1,0:T(8,128)(2,1)S(1)}, bf16[2,128,256]{2,1,0:T(8,128)(2,1)S(1)}, u32[]{:S(2)}, u32[]{:S(2)}) collective-permute-start(bf16[2,128,256]{2,1,0:T(8,128)(2,1)S(1)} %get-tuple-element.36), channel_id=1, source_target_pairs={{0,20},{4,16},{8,28},{12,24},{16,4},{20,0},{24,12},{28,8},{1,21},{... | collective-permute-start | bytes 393224 | tf_op jit(solution)/shard_map/ppermute | solution.py:400
  24.3 14.7 %collective-permute-start.13 = (bf16[2,128,256]{2,1,0:T(8,128)(2,1)S(1)}, bf16[2,128,256]{2,1,0:T(8,128)(2,1)S(1)}, u32[]{:S(2)}, u32[]{:S(2)}) collective-permute-start(bf16[2,128,256]{2,1,0:T(8,128)(2,1)S(1)} %get-tuple-element.37), channel_id=1, source_target_pairs={{0,24},{4,28},{8,16},{12,20},{16,8},{20,12},{24,0},{28,4},{1,25},{... | collective-permute-start | bytes 393224 | tf_op jit(solution)/shard_map/ppermute | solution.py:400
  25.5 13.5 %collective-permute-start.14 = (bf16[2,128,256]{2,1,0:T(8,128)(2,1)S(1)}, bf16[2,128,256]{2,1,0:T(8,128)(2,1)S(1)}, u32[]{:S(2)}, u32[]{:S(2)}) collective-permute-start(bf16[2,128,256]{2,1,0:T(8,128)(2,1)S(1)} %get-tuple-element.38), channel_id=1, source_target_pairs={{0,28},{4,24},{8,20},{12,16},{16,12},{20,8},{24,4},{28,0},{1,29},{... | collective-permute-start | bytes 393224 | tf_op jit(solution)/shard_map/ppermute | solution.py:400
  35.3 15.9 %collective-permute-start.7 = (bf16[8,128,256]{2,1,0:T(8,128)(2,1)S(1)}, bf16[8,128,256]{2,1,0:T(8,128)(2,1)}, u32[]{:S(2)}, u32[]{:S(2)}) collective-permute-start(bf16[8,128,256]{2,1,0:T(8,128)(2,1)S(1)} %get-tuple-element.30), channel_id=1, source_target_pairs={{0,3},{1,0},{2,1},{3,2},{4,7},{5,4},{6,5},{7,6},{8,11},{9,8},{10,9... | collective-permute-start | bytes 1572872 | tf_op jit(solution)/shard_map/ppermute | solution.py:419
  47.1 14.7 %collective-permute-start.15 = (bf16[8,128,256]{2,1,0:T(8,128)(2,1)S(1)}, bf16[8,128,256]{2,1,0:T(8,128)(2,1)S(1)}, u32[]{:S(2)}, u32[]{:S(2)}) collective-permute-start(bf16[8,128,256]{2,1,0:T(8,128)(2,1)S(1)} %get-tuple-element.40), channel_id=1, source_target_pairs={{0,3},{1,0},{2,1},{3,2},{4,7},{5,4},{6,5},{7,6},{8,11},{9,8},{10,9... | collective-permute-start | bytes 1572872 | tf_op jit(solution)/shard_map/ppermute | solution.py:419
  51.2 20.9 %all-to-all-start = ((bf16[8,128,256]{2,1,0:T(8,128)(2,1)}), bf16[8,128,256]{2,1,0:T(8,128)(2,1)S(1)}, u32[]{:S(2)}, u32[]{:S(2)}) async-start(bf16[8,128,256]{2,1,0:T(8,128)(2,1)} %collective-permute-done.7), calls=%async_computation | async-start | bytes 1048576 | tf_op jit(solution)/shard_map/all_to_all | solution.py:398
  61.8 3.6 %collective-permute-start.16 = (bf16[128,256]{1,0:T(8,128)(2,1)S(1)}, bf16[128,256]{1,0:T(8,128)(2,1)S(1)}, u32[]{:S(2)}, u32[]{:S(2)}) collective-permute-start(bf16[128,256]{1,0:T(8,128)(2,1)S(1)} %get-tuple-element.48), channel_id=1, source_target_pairs={{0,4},{4,0},{8,12},{12,8},{16,20},{20,16},{24,28},{28,24},{1,5},{5... | collective-permute-start | bytes 196616 | tf_op jit(solution)/shard_map/ppermute | solution.py:400
  61.9 5.0 %collective-permute-start.17 = (bf16[128,256]{1,0:T(8,128)(2,1)S(1)}, bf16[128,256]{1,0:T(8,128)(2,1)S(1)}, u32[]{:S(2)}, u32[]{:S(2)}) collective-permute-start(bf16[128,256]{1,0:T(8,128)(2,1)S(1)} %get-tuple-element.47), channel_id=1, source_target_pairs={{0,8},{4,12},{8,0},{12,4},{16,24},{20,28},{24,16},{28,20},{1,9},{5... | collective-permute-start | bytes 196616 | tf_op jit(solution)/shard_map/ppermute | solution.py:400
  62.5 5.7 %collective-permute-start.18 = (bf16[128,256]{1,0:T(8,128)(2,1)S(1)}, bf16[128,256]{1,0:T(8,128)(2,1)S(1)}, u32[]{:S(2)}, u32[]{:S(2)}) collective-permute-start(bf16[128,256]{1,0:T(8,128)(2,1)S(1)} %get-tuple-element.46), channel_id=1, source_target_pairs={{0,12},{4,8},{8,4},{12,0},{16,28},{20,24},{24,20},{28,16},{1,13},{... | collective-permute-start | bytes 196616 | tf_op jit(solution)/shard_map/ppermute | solution.py:400
  63.7 4.7 %collective-permute-start.19 = (bf16[128,256]{1,0:T(8,128)(2,1)S(1)}, bf16[128,256]{1,0:T(8,128)(2,1)S(1)}, u32[]{:S(2)}, u32[]{:S(2)}) collective-permute-start(bf16[128,256]{1,0:T(8,128)(2,1)S(1)} %get-tuple-element.45), channel_id=1, source_target_pairs={{0,16},{4,20},{8,24},{12,28},{16,0},{20,4},{24,8},{28,12},{1,17},{... | collective-permute-start | bytes 196616 | tf_op jit(solution)/shard_map/ppermute | solution.py:400
  64.8 4.3 %collective-permute-start.20 = (bf16[128,256]{1,0:T(8,128)(2,1)S(1)}, bf16[128,256]{1,0:T(8,128)(2,1)S(1)}, u32[]{:S(2)}, u32[]{:S(2)}) collective-permute-start(bf16[128,256]{1,0:T(8,128)(2,1)S(1)} %get-tuple-element.44), channel_id=1, source_target_pairs={{0,20},{4,16},{8,28},{12,24},{16,4},{20,0},{24,12},{28,8},{1,21},{... | collective-permute-start | bytes 196616 | tf_op jit(solution)/shard_map/ppermute | solution.py:400
  65.4 5.6 %collective-permute-start.21 = (bf16[128,256]{1,0:T(8,128)(2,1)S(1)}, bf16[128,256]{1,0:T(8,128)(2,1)S(1)}, u32[]{:S(2)}, u32[]{:S(2)}) collective-permute-start(bf16[128,256]{1,0:T(8,128)(2,1)S(1)} %get-tuple-element.43), channel_id=1, source_target_pairs={{0,24},{4,28},{8,16},{12,20},{16,8},{20,12},{24,0},{28,4},{1,25},{... | collective-permute-start | bytes 196616 | tf_op jit(solution)/shard_map/ppermute | solution.py:400
  66.8 5.3 %collective-permute-start.22 = (bf16[128,256]{1,0:T(8,128)(2,1)S(1)}, bf16[128,256]{1,0:T(8,128)(2,1)S(1)}, u32[]{:S(2)}, u32[]{:S(2)}) collective-permute-start(bf16[128,256]{1,0:T(8,128)(2,1)S(1)} %get-tuple-element.42), channel_id=1, source_target_pairs={{0,28},{4,24},{8,20},{12,16},{16,12},{20,8},{24,4},{28,0},{1,29},{... | collective-permute-start | bytes 196616 | tf_op jit(solution)/shard_map/ppermute | solution.py:400

commit v4 on v3

--- a/solution.py
+++ b/solution.py
@@ -17,7 +17,8 @@
 LAST_TILE = 64
 DENSE_ROWS = 1024
 SPECTRUM_VMEM = 12 * 1024 * 1024
-SECTION_VMEM = 28 * 1024 * 1024
+FILTER_VMEM = 10 * 1024 * 1024
+SECTION_VMEM = 21 * 1024 * 1024
 COS = [math.cos(math.pi / 8 * j) for j in range(4)]
 SIN = [math.sin(math.pi / 8 * j) for j in range(4)]
 
@@ -184,14 +185,12 @@
     )(kernel, fwd)
 
 
-def section_kernel(devices, chunk, aliased, whole_in, whole_out, *refs):
+def section_kernel(devices, chunk, whole_in, whole_out, *refs):
     taken = 1 if whole_in else devices
     (pieces,) = by_target(refs[:taken], devices, [whole_in])
-    refs = refs[taken:]
-    tap_ref, fwd_ref, inv_ref, spec_ref = refs[:4]
-    refs = refs[4 + aliased :]
-    out_ref, filt_ref, padded, upstream, key_rows, value_rows, turned, mixed, back = refs[:9]
-    shifted_rows, filt_rows, grad_rows, tap_rows, filt_sem, tap_sem = refs[9:]
+    tap_ref, spec_ref, fwd_ref, inv_ref, out_ref, cross_ref = refs[taken : taken + 6]
+    padded, upstream, key_rows, value_rows, turned, mixed, back = refs[taken + 6 : taken + 13]
+    shifted_rows, grad_rows, tap_rows, tap_sem = refs[taken + 13 :]
     me = lax.axis_index("seq")
     length, width = pieces[0][1].shape[1:]
     rows = length * devices
@@ -225,8 +224,8 @@
             value_rows[here, :] = value
             products.append(key * value)
             adjoints.append(upstream[here, :] * query)
-        for half, signals in enumerate((products, adjoints)):
-            into = slice(half * width, (half + 1) * width)
+        for number, signals in enumerate((products, adjoints)):
+            into = slice(number * width, (number + 1) * width)
             for j, (real, imag) in enumerate(split(*signals)):
                 turned[j, pl.ds(begin, TILE), into] = real.astype(jnp.bfloat16)
                 turned[j, pl.ds(begin + quarter, TILE), into] = imag.astype(jnp.bfloat16)
@@ -236,16 +235,12 @@
         p_re, p_im = both[:quarter, :width], both[quarter:, :width]
         a_re, a_im = both[:quarter, width:], both[quarter:, width:]
         h_re, h_im = spec_ref[j, :quarter, columns], spec_ref[j, quarter:, columns]
-        for number, (real, imag) in enumerate(
-            (
-                (p_re * h_re - p_im * h_im, p_re * h_im + p_im * h_re),
-                (h_re * a_re + h_im * a_im, h_re * a_im - h_im * a_re),
-                (p_re * a_re + p_im * a_im, p_re * a_im - p_im * a_re),
-            )
-        ):
-            into = slice(number * width, (number + 1) * width)
-            mixed[j, :quarter, into] = real.astype(jnp.bfloat16)
-            mixed[j, quarter:, into] = imag.astype(jnp.bfloat16)
+        mixed[j, :quarter, :width] = (p_re * h_re - p_im * h_im).astype(jnp.bfloat16)
+        mixed[j, quarter:, :width] = (p_re * h_im + p_im * h_re).astype(jnp.bfloat16)
+        mixed[j, :quarter, width:] = (h_re * a_re + h_im * a_im).astype(jnp.bfloat16)
+        mixed[j, quarter:, width:] = (h_re * a_im - h_im * a_re).astype(jnp.bfloat16)
+        cross_ref[j, :quarter, :] = (p_re * a_re + p_im * a_im).astype(jnp.bfloat16)
+        cross_ref[j, quarter:, :] = (p_re * a_im - p_im * a_re).astype(jnp.bfloat16)
         back[j] = jnp.dot(inv_ref[j], mixed[j], preferred_element_type=jnp.float32)
 
     @pl.loop(0, quarter // TILE)
@@ -253,15 +248,10 @@
         begin = pl.multiple_of(step * TILE, TILE)
         real, imag = pl.ds(begin, TILE), pl.ds(begin + quarter, TILE)
         results = []
-        for number in range(3):
-            part = slice(number * width, (number + 1) * width)
+        for part in (slice(0, width), slice(width, 2 * width)):
             results.append(joined(*((back[j, real, part], back[j, imag, part]) for j in range(4))))
-        for j, (combined, backward, filt) in enumerate(zip(*results)):
+        for j, (combined, backward) in enumerate(zip(*results)):
             here = pl.ds(begin + j * quarter, TILE)
-            filt_rows[here, :] = filt * (1.0 / math.sqrt(rows))
-            pltpu.make_async_copy(
-                filt_rows.at[here, :], filt_ref.at[here, columns], filt_sem
-            ).start()
             grads = (
                 low(upstream[here, :] * combined),
                 low(backward * value_rows[here, :]),
@@ -281,46 +271,88 @@
 
     for k in range(devices):
         out_ref[k] = grad_rows[place(k if whole_out else me ^ k, 0), :]
-    pltpu.make_async_copy(filt_rows, filt_ref.at[:, columns], filt_sem).wait()
-
-
-def section(pieces, taps, fwd, inv, spec, chunk, filt, devices, whole_in, whole_out):
+
+
+def section(pieces, taps, spec, fwd, inv, chunk, devices, whole_in, whole_out):
     length, width = pieces[0].shape[-2:]
     rows = devices * length
     near = pl.BlockSpec(memory_space=pltpu.VMEM)
     far = pl.BlockSpec(memory_space=pl.ANY)
-    more = [] if filt is None else [filt]
-    vmem = lambda *shape: pltpu.VMEM(shape, jnp.float32)
+    single = lambda *shape: pltpu.VMEM(shape, jnp.float32)
+    half = lambda *shape: pltpu.VMEM(shape, jnp.bfloat16)
     return pl.pallas_call(
-        functools.partial(section_kernel, devices, chunk, len(more), whole_in, whole_out),
-        in_specs=[near] * len(pieces) + [far] + [near] * 3 + [far] * len(more),
-        out_specs=[near, far],
+        functools.partial(section_kernel, devices, chunk, whole_in, whole_out),
+        in_specs=[near] * len(pieces) + [far] + [near] * 3,
+        out_specs=[near] * 2,
         out_shape=[
             jax.ShapeDtypeStruct((devices, length, width), jnp.bfloat16),
-            jax.ShapeDtypeStruct((rows, spec.shape[2]), jnp.float32),
+            jax.ShapeDtypeStruct((4, rows // 2, width), jnp.bfloat16),
         ],
         scratch_shapes=[
-            vmem(rows + PAD, width),
-            vmem(rows, width),
-            vmem(rows, width),
-            vmem(rows, width),
-            pltpu.VMEM((4, rows // 2, 2 * width), jnp.bfloat16),
-            pltpu.VMEM((4, rows // 2, 3 * width), jnp.bfloat16),
-            vmem(4, rows // 2, 3 * width),
-            vmem(3, rows + PAD, width),
-            vmem(rows, width),
-            pltpu.VMEM((rows, width), jnp.bfloat16),
-            vmem(*taps.shape[1:3], width),
-            pltpu.SemaphoreType.DMA,
+            single(rows + PAD, width),
+            single(rows, width),
+            single(rows, width),
+            single(rows, width),
+            half(4, rows // 2, 2 * width),
+            half(4, rows // 2, 2 * width),
+            single(4, rows // 2, 2 * width),
+            single(3, rows + PAD, width),
+            half(rows, width),
+            single(*taps.shape[1:3], width),
             pltpu.SemaphoreType.DMA,
         ],
-        input_output_aliases={len(pieces) + 4: 1} if more else {},
         compiler_params=pltpu.CompilerParams(vmem_limit_bytes=SECTION_VMEM),
         cost_estimate=pl.CostEstimate(
-            flops=10 * rows * rows * width, bytes_accessed=30 * rows * width, transcendentals=0
+            flops=10 * rows * rows * width, bytes_accessed=20 * rows * width, transcendentals=0
         ),
         name="section",
-    )(*pieces, taps, fwd, inv, spec, *more)
+    )(*pieces, taps, spec, fwd, inv)
+
+
+def filter_kernel(inv_ref, *refs):
+    crosses, (filt_ref, back, filt_rows, sem) = refs[:-4], refs[-4:]
+    rows, width = filt_rows.shape[1:]
+    quarter = rows // 4
+    for chunk, cross_ref in enumerate(crosses):
+        columns = slice(chunk * width, (chunk + 1) * width)
+        for j in range(4):
+            back[chunk, j] = jnp.dot(inv_ref[j], cross_ref[j], preferred_element_type=jnp.float32)
+
+        @pl.loop(0, quarter // TILE)
+        def _(step):
+            begin = pl.multiple_of(step * TILE, TILE)
+            real, imag = pl.ds(begin, TILE), pl.ds(begin + quarter, TILE)
+            parts = joined(*((back[chunk, j, real, :], back[chunk, j, imag, :]) for j in range(4)))
+            for j, part in enumerate(parts):
+                filt_rows[chunk, pl.ds(begin + j * quarter, TILE), :] = part * (1.0 / math.sqrt(rows))
+
+        pltpu.make_async_copy(filt_rows.at[chunk], filt_ref.at[:, columns], sem.at[chunk]).start()
+    for chunk in range(len(crosses)):
+        columns = slice(chunk * width, (chunk + 1) * width)
+        pltpu.make_async_copy(filt_rows.at[chunk], filt_ref.at[:, columns], sem.at[chunk]).wait()
+
+
+def filter_gradient(inv, crosses):
+    rows, width = 2 * crosses[0].shape[1], crosses[0].shape[2]
+    count = len(crosses)
+    return pl.pallas_call(
+        filter_kernel,
+        in_specs=[pl.BlockSpec(memory_space=pltpu.VMEM)] * (1 + count),
+        out_specs=pl.BlockSpec(memory_space=pl.ANY),
+        out_shape=jax.ShapeDtypeStruct((rows, width * count), jnp.float32),
+        scratch_shapes=[
+            pltpu.VMEM((count, 4, rows // 2, width), jnp.float32),
+            pltpu.VMEM((count, rows, width), jnp.float32),
+            pltpu.SemaphoreType.DMA((count,)),
+        ],
+        compiler_params=pltpu.CompilerParams(vmem_limit_bytes=FILTER_VMEM),
+        cost_estimate=pl.CostEstimate(
+            flops=2 * rows * rows * width * count,
+            bytes_accessed=6 * rows * width * count,
+            transcendentals=0,
+        ),
+        name="filter",
+    )(inv, *crosses)
 
 
 def phase_table(row_count, col_count, modulus, direction):
@@ -403,20 +435,21 @@
 def fast(inputs, upstream, kernel, taps):
     devices, count = lax.axis_size("seq"), lax.axis_size("pipe")
     before = [(p, (p - 1) % count) for p in range(count)]
-    arrived = [
-        exchanged(chunk, devices, whole)
-        for chunk, whole in zip(pack(inputs, upstream, devices, WHOLE_IN), WHOLE_IN)
-    ]
+    pieces = pack(inputs, upstream, devices, WHOLE_IN)
     fwd, inv = quarter_tables(kernel.shape[0])
     spec = spectrum(kernel, fwd)
-    filter_grad, home = None, []
+    grads, crosses = [], []
     for chunk in range(CHUNKS):
-        whole = WHOLE_OUT[chunk]
-        grad, filter_grad = section(
-            arrived[chunk], taps, fwd, inv, spec, chunk, filter_grad,
-            devices, WHOLE_IN[chunk], whole,
+        arrived = exchanged(pieces[chunk], devices, WHOLE_IN[chunk])
+        grad, cross = section(
+            arrived, taps, spec, fwd, inv, chunk, devices, WHOLE_IN[chunk], WHOLE_OUT[chunk]
         )
-        grad = lax.ppermute(grad, "pipe", before)
+        grads.append(lax.ppermute(grad, "pipe", before))
+        crosses.append(cross)
+    filter_grad = filter_gradient(inv, crosses)
+    home = []
+    for grad, whole in zip(grads, WHOLE_OUT):
+        grad, filter_grad = lax.optimization_barrier((grad, filter_grad))
         home.append(
             exchanged([grad] if whole else [grad[k] for k in range(devices)], devices, whole)
         )

time: 73.5 us -> 72.7 us (0.989)
  waiting for transfers between devices: 15.6 us -> 12.5 us
  Pallas kernels: 19.9 us -> 21.5 us
    ppermute x2, waiting for transfers between devices: 10.7 us -> 7.64 us  [fast(): grads.append(lax.ppermute(grad, 'pipe', before))]
    pallas_call x2 -> x3, Pallas kernels: 16.2 us -> 17.8 us  [the longest x2 14.7 us: section(): pl.pallas_call(functools.partial(section_kernel, devices, chunk, whole_in...]
  transfers between devices with their start and end apart: 24 -> 24, of which waited for: 8 -> 8; matrix products, arithmetic and copies ran while one was open for 1% -> 1% of each run, Pallas kernels for 25% -> 27%
where the time goes in v4:
time: 72.7 us; the launch traced here: 72.5 us
  starting transfers between devices  32.4 us (45%)
  Pallas kernels  21.5 us (30%)
  waiting for transfers between devices  12.5 us (17%)
  local copies, waits for them, and re-layouts  5.23 us (7%)
  between operations  0.77 us (1%)
    ppermute x21, starting transfers between devices, exchanged(): lax.ppermute(chunk[k], 'seq', pairs(k))  24.2 us
    pallas_call x2, Pallas kernels, section(): pl.pallas_call(functools.partial(section_kernel, devices, chunk, whole_in...  14.7 us
    ppermute x2, waiting for transfers between devices, fast(): grads.append(lax.ppermute(grad, 'pipe', before))  7.64 us
    unnamed x11, local copies, waits for them, and re-layouts  5.2 us
    ppermute x21, waiting for transfers between devices, exchanged(): lax.ppermute(chunk[k], 'seq', pairs(k))  4.89 us
    ppermute x2, starting transfers between devices, fast(): grads.append(lax.ppermute(grad, 'pipe', before))  4.79 us
    all_to_all x1, starting transfers between devices, exchanged(): lax.all_to_all(chunk[0], 'seq', split_axis=0, concat_axis=0, tiled=True)  3.49 us
    pallas_call x1, Pallas kernels, filter_gradient(): pl.pallas_call(filter_kernel, in_specs=[pl.BlockSpec(memory_space=pltpu.V...  3.16 us
  transfers between devices with their start and end apart: 24, of which 8 were waited for; matrix products, arithmetic and copies ran while one was open for 1% of the time, Pallas kernels for 27%

profile of v4, /device:TPU:0, one launch (start us, length us, event | category | flops | bytes accessed | tf_op | source)
XLA Modules:
  0.0 72.5 jit_solution(7052983524926626403)
XLA Ops:
  0.6 0.0 copy-start.1
  0.6 0.0 copy-start.3
  0.6 1.4 %copy-done.3 = bf16[1,128,4096]{2,1,0:T(8,128)(2,1)S(1)} copy-done((bf16[1,128,4096]{2,1,0:T(8,128)(2,1)S(1)}, bf16[1,128,4096]{2,1,0:T(8,128)(2,1)}, u32[]{:S(2)}) %copy-start.3) | copy-done | bytes 1048600
  2.0 0.0 copy-start.4
  2.0 1.2 %copy-done.4 = bf16[1,128,4096]{2,1,0:T(8,128)(2,1)S(1)} copy-done((bf16[1,128,4096]{2,1,0:T(8,128)(2,1)S(1)}, bf16[1,128,4096]{2,1,0:T(8,128)(2,1)}, u32[]{:S(2)}) %copy-start.4) | copy-done | bytes 1048600
  3.2 0.7 %pack.1 = (bf16[2,128,256]{2,1,0:T(8,128)(2,1)S(1)}, bf16[2,128,256]{2,1,0:T(8,128)(2,1)S(1)}, bf16[2,128,256]{2,1,0:T(8,128)(2,1)S(1)}, bf16[2,128,256]{2,1,0:T...) custom-call(bf16[128,4096]{1,0:T(8,128)(2,1)S(1)} %bitcast.21, ...), custom_call_target="tpu_custom_call" | custom-call | tf_op jit(solution)/shard_map/pack/pallas_call | solution.py:102
  4.0 0.5 collective-permute-start
  4.5 2.6 %collective-permute-start.1 = (bf16[2,128,256]{2,1,0:T(8,128)(2,1)S(1)}, bf16[2,128,256]{2,1,0:T(8,128)(2,1)S(1)}, u32[]{:S(2)}, u32[]{:S(2)}) collective-permute-start(bf16[2,128,256]{2,1,0:T(8,128)(2,1)S(1)} %get-tuple-element.28), channel_id=1, source_target_pairs={{0,8},{4,12},{8,0},{12,4},{16,24},{20,28},{24,16},{28,20},{1,9},{5... | collective-permute-start | bytes 393224 | tf_op jit(solution)/shard_map/ppermute | solution.py:432
  7.1 0.1 collective-permute-start.2
  7.1 1.8 %collective-permute-start.3 = (bf16[2,128,256]{2,1,0:T(8,128)(2,1)S(1)}, bf16[2,128,256]{2,1,0:T(8,128)(2,1)S(1)}, u32[]{:S(2)}, u32[]{:S(2)}) collective-permute-start(bf16[2,128,256]{2,1,0:T(8,128)(2,1)S(1)} %get-tuple-element.30), channel_id=1, source_target_pairs={{0,16},{4,20},{8,24},{12,28},{16,0},{20,4},{24,8},{28,12},{1,17},{... | collective-permute-start | bytes 393224 | tf_op jit(solution)/shard_map/ppermute | solution.py:432
  8.9 0.0 collective-permute-start.4
  8.9 0.0 collective-permute-done.refs_1_
  8.9 2.6 %collective-permute-start.5 = (bf16[2,128,256]{2,1,0:T(8,128)(2,1)S(1)}, bf16[2,128,256]{2,1,0:T(8,128)(2,1)S(1)}, u32[]{:S(2)}, u32[]{:S(2)}) collective-permute-start(bf16[2,128,256]{2,1,0:T(8,128)(2,1)S(1)} %get-tuple-element.32), channel_id=1, source_target_pairs={{0,24},{4,28},{8,16},{12,20},{16,8},{20,12},{24,0},{28,4},{1,25},{... | collective-permute-start | bytes 393224 | tf_op jit(solution)/shard_map/ppermute | solution.py:432
  11.5 0.0 collective-permute-done.1.refs_2_
  11.5 1.6 %collective-permute-start.6 = (bf16[2,128,256]{2,1,0:T(8,128)(2,1)S(1)}, bf16[2,128,256]{2,1,0:T(8,128)(2,1)S(1)}, u32[]{:S(2)}, u32[]{:S(2)}) collective-permute-start(bf16[2,128,256]{2,1,0:T(8,128)(2,1)S(1)} %get-tuple-element.33), channel_id=1, source_target_pairs={{0,28},{4,24},{8,20},{12,16},{16,12},{20,8},{24,4},{28,0},{1,29},{... | collective-permute-start | bytes 393224 | tf_op jit(solution)/shard_map/ppermute | solution.py:432
  13.1 0.6 collective-permute-done.2.refs_3_
  13.7 0.7 %collective-permute-start.8 = (bf16[2,128,256]{2,1,0:T(8,128)(2,1)S(1)}, bf16[2,128,256]{2,1,0:T(8,128)(2,1)S(1)}, u32[]{:S(2)}, u32[]{:S(2)}) collective-permute-start(bf16[2,128,256]{2,1,0:T(8,128)(2,1)S(1)} %get-tuple-element.37), channel_id=1, source_target_pairs={{0,4},{4,0},{8,12},{12,8},{16,20},{20,16},{24,28},{28,24},{1,5},{5... | collective-permute-start | bytes 393224 | tf_op jit(solution)/shard_map/ppermute | solution.py:432
  14.4 0.0 collective-permute-done.3.refs_4_
  14.4 1.8 %collective-permute-start.9 = (bf16[2,128,256]{2,1,0:T(8,128)(2,1)S(1)}, bf16[2,128,256]{2,1,0:T(8,128)(2,1)S(1)}, u32[]{:S(2)}, u32[]{:S(2)}) collective-permute-start(bf16[2,128,256]{2,1,0:T(8,128)(2,1)S(1)} %get-tuple-element.38), channel_id=1, source_target_pairs={{0,8},{4,12},{8,0},{12,4},{16,24},{20,28},{24,16},{28,20},{1,9},{5... | collective-permute-start | bytes 393224 | tf_op jit(solution)/shard_map/ppermute | solution.py:432
  16.3 1.0 %copy.8.refs_8_ = f32[1,3,3,4096]{3,2,1,0:T(4,128)S(1)} copy(f32[1,3,3,4096]{3,0,2,1:T(1,128)} %param.9) | data formatting | bytes 294912 | tf_op args[3]
  17.3 0.0 copy-done.1
  17.3 0.0 copy-start.2
  17.3 1.6 %copy-done.2 = bf16[4,512,512]{2,1,0:T(8,128)(2,1)S(1)} copy-done((bf16[4,512,512]{2,1,0:T(8,128)(2,1)S(1)}, bf16[4,512,512]{2,1,0:T(8,128)(2,1)}, u32[]{:S(2)}) %copy-start.2) | copy-done | bytes 2097176
  18.9 1.8 %spectrum.1.refs_9_ = f32[4,512,512]{2,1,0:T(8,128)S(1)} custom-call(f32[1024,512]{1,0:T(8,128)S(1)} %bitcast.20, bf16[4,512,512]{2,1,0:T(8,128)(2,1)S(1)} %copy-done.2), custom_call_target="tpu_custom_call" | custom-call | flops 1073741824 | bytes 7340032 | tf_op jit(solution)/shard_map/spectrum/pallas_call | solution.py:174
  20.7 0.0 collective-permute-done.4.refs_5_
  20.7 2.0 %collective-permute-start.10 = (bf16[2,128,256]{2,1,0:T(8,128)(2,1)S(1)}, bf16[2,128,256]{2,1,0:T(8,128)(2,1)S(1)}, u32[]{:S(2)}, u32[]{:S(2)}) collective-permute-start(bf16[2,128,256]{2,1,0:T(8,128)(2,1)S(1)} %get-tuple-element.39), channel_id=1, source_target_pairs={{0,12},{4,8},{8,4},{12,0},{16,28},{20,24},{24,20},{28,16},{1,13},{... | collective-permute-start | bytes 393224 | tf_op jit(solution)/shard_map/ppermute | solution.py:432
  22.7 0.0 collective-permute-done.5.refs_6_
  22.8 1.5 %collective-permute-start.11 = (bf16[2,128,256]{2,1,0:T(8,128)(2,1)S(1)}, bf16[2,128,256]{2,1,0:T(8,128)(2,1)S(1)}, u32[]{:S(2)}, u32[]{:S(2)}) collective-permute-start(bf16[2,128,256]{2,1,0:T(8,128)(2,1)S(1)} %get-tuple-element.40), channel_id=1, source_target_pairs={{0,16},{4,20},{8,24},{12,28},{16,0},{20,4},{24,8},{28,12},{1,17},{... | collective-permute-start | bytes 393224 | tf_op jit(solution)/shard_map/ppermute | solution.py:432
  24.3 0.0 collective-permute-done.6.refs_7_
  24.3 0.0 collective-permute-start.12
  24.3 0.0 collective-permute-done.8.refs_1_
  24.3 1.2 %collective-permute-start.13 = (bf16[2,128,256]{2,1,0:T(8,128)(2,1)S(1)}, bf16[2,128,256]{2,1,0:T(8,128)(2,1)S(1)}, u32[]{:S(2)}, u32[]{:S(2)}) collective-permute-start(bf16[2,128,256]{2,1,0:T(8,128)(2,1)S(1)} %get-tuple-element.42), channel_id=1, source_target_pairs={{0,24},{4,28},{8,16},{12,20},{16,8},{20,12},{24,0},{28,4},{1,25},{... | collective-permute-start | bytes 393224 | tf_op jit(solution)/shard_map/ppermute | solution.py:432
  25.5 0.0 collective-permute-done.9.refs_2_
  25.5 1.7 %collective-permute-start.14 = (bf16[2,128,256]{2,1,0:T(8,128)(2,1)S(1)}, bf16[2,128,256]{2,1,0:T(8,128)(2,1)S(1)}, u32[]{:S(2)}, u32[]{:S(2)}) collective-permute-start(bf16[2,128,256]{2,1,0:T(8,128)(2,1)S(1)} %get-tuple-element.43), channel_id=1, source_target_pairs={{0,28},{4,24},{8,20},{12,16},{16,12},{20,8},{24,4},{28,0},{1,29},{... | collective-permute-start | bytes 393224 | tf_op jit(solution)/shard_map/ppermute | solution.py:432
  27.2 0.0 copy-done
  27.2 7.3 %section.2 = (bf16[8,128,256]{2,1,0:T(8,128)(2,1)S(1)}, bf16[4,512,256]{2,1,0:T(8,128)(2,1)S(1)}) custom-call(bf16[2,128,256]{2,1,0:T(8,128)(2,1)S(1)} %get-tuple-element.26.refs_0_, bf16[2,128,256]{2,1,0:T(8,128)(2,1)S(1)} %collective-permute-done.refs_1_, bf16[2,128,256]{2,1,0:T(8,128)(2,1)S(1)} %collective-permute-done.1.refs_2_, ...), custom_call_target="tpu_custom_call" | custom-call | flops 2684354560 | bytes 5242880 | tf_op jit(solution)/shard_map/section/pallas_call | solution.py:283
  34.5 0.0 collective-permute-done.10.refs_3_
  34.5 3.7 %collective-permute-start.7 = (bf16[8,128,256]{2,1,0:T(8,128)(2,1)S(1)}, bf16[8,128,256]{2,1,0:T(8,128)(2,1)}, u32[]{:S(2)}, u32[]{:S(2)}) collective-permute-start(bf16[8,128,256]{2,1,0:T(8,128)(2,1)S(1)} %get-tuple-element.34), channel_id=1, source_target_pairs={{0,3},{1,0},{2,1},{3,2},{4,7},{5,4},{6,5},{7,6},{8,11},{9,8},{10,9... | collective-permute-start | bytes 1572872 | tf_op jit(solution)/shard_map/ppermute | solution.py:447
  38.2 0.0 collective-permute-done.11.refs_4_
  38.2 0.0 collective-permute-done.12.refs_5_
  38.2 0.0 collective-permute-done.13.refs_6_
  38.2 0.0 collective-permute-done.14.refs_7_
  38.2 7.3 %section.3 = (bf16[8,128,256]{2,1,0:T(8,128)(2,1)S(1)}, bf16[4,512,256]{2,1,0:T(8,128)(2,1)S(1)}) custom-call(bf16[2,128,256]{2,1,0:T(8,128)(2,1)S(1)} %get-tuple-element.36.refs_0_, bf16[2,128,256]{2,1,0:T(8,128)(2,1)S(1)} %collective-permute-done.8.refs_1_, bf16[2,128,256]{2,1,0:T(8,128)(2,1)S(1)} %collective-permute-done.9.refs_2_, ...), custom_call_target="tpu_custom_call" | custom-call | flops 2684354560 | bytes 5242880 | tf_op jit(solution)/shard_map/section/pallas_call | solution.py:283
  45.5 1.1 %collective-permute-start.15 = (bf16[8,128,256]{2,1,0:T(8,128)(2,1)S(1)}, bf16[8,128,256]{2,1,0:T(8,128)(2,1)S(1)}, u32[]{:S(2)}, u32[]{:S(2)}) collective-permute-start(bf16[8,128,256]{2,1,0:T(8,128)(2,1)S(1)} %get-tuple-element.46), channel_id=1, source_target_pairs={{0,3},{1,0},{2,1},{3,2},{4,7},{5,4},{6,5},{7,6},{8,11},{9,8},{10,9... | collective-permute-start | bytes 1572872 | tf_op jit(solution)/shard_map/ppermute | solution.py:447
  46.7 3.2 %filter.1 = f32[1024,512]{1,0:T(8,128)} custom-call(bf16[4,512,512]{2,1,0:T(8,128)(2,1)S(1)} %copy-done, bf16[4,512,256]{2,1,0:T(8,128)(2,1)S(1)} %get-tuple-element.35.refs_0_, bf16[4,512,256]{2,1,0:T(8,128)(2,1)S(1)} %get-tuple-element.44.refs_1_), custom_call_target="tpu_custom_call" | custom-call | flops 1073741824 | bytes 3145728 | tf_op jit(solution)/shard_map/filter/pallas_call | solution.py:338
  49.9 0.6 collective-permute-done.7
  50.4 3.5 %all-to-all-start = ((bf16[8,128,256]{2,1,0:T(8,128)(2,1)}), bf16[8,128,256]{2,1,0:T(8,128)(2,1)S(1)}, u32[]{:S(2)}, u32[]{:S(2)}) async-start(bf16[8,128,256]{2,1,0:T(8,128)(2,1)} %collective-permute-done.7), calls=%async_computation | async-start | bytes 1048576 | tf_op jit(solution)/shard_map/all_to_all | solution.py:430
  53.9 7.0 %collective-permute-done.15 = bf16[8,128,256]{2,1,0:T(8,128)(2,1)S(1)} collective-permute-done((bf16[8,128,256]{2,1,0:T(8,128)(2,1)S(1)}, bf16[8,128,256]{2,1,0:T(8,128)(2,1)S(1)}, u32[]{:S(2)}, u32[]{:S(2)}) %collective-permute-start.15) | collective-permute-done | bytes 524320 | tf_op jit(solution)/shard_map/ppermute | solution.py:447
  61.0 0.1 collective-permute-start.16
  61.1 0.6 collective-permute-start.17
  61.7 1.3 %collective-permute-start.18 = (bf16[128,256]{1,0:T(8,128)(2,1)S(1)}, bf16[128,256]{1,0:T(8,128)(2,1)S(1)}, u32[]{:S(2)}, u32[]{:S(2)}) collective-permute-start(bf16[128,256]{1,0:T(8,128)(2,1)S(1)} %get-tuple-element.54), channel_id=1, source_target_pairs={{0,12},{4,8},{8,4},{12,0},{16,28},{20,24},{24,20},{28,16},{1,13},{... | collective-permute-start | bytes 196616 | tf_op jit(solution)/shard_map/ppermute | solution.py:432
  63.0 1.1 %collective-permute-start.19 = (bf16[128,256]{1,0:T(8,128)(2,1)S(1)}, bf16[128,256]{1,0:T(8,128)(2,1)S(1)}, u32[]{:S(2)}, u32[]{:S(2)}) collective-permute-start(bf16[128,256]{1,0:T(8,128)(2,1)S(1)} %get-tuple-element.53), channel_id=1, source_target_pairs={{0,16},{4,20},{8,24},{12,28},{16,0},{20,4},{24,8},{28,12},{1,17},{... | collective-permute-start | bytes 196616 | tf_op jit(solution)/shard_map/ppermute | solution.py:432
  64.1 0.6 collective-permute-start.20
  64.7 0.0 collective-permute-done.16.refs_2_
  64.7 1.1 %collective-permute-start.21 = (bf16[128,256]{1,0:T(8,128)(2,1)S(1)}, bf16[128,256]{1,0:T(8,128)(2,1)S(1)}, u32[]{:S(2)}, u32[]{:S(2)}) collective-permute-start(bf16[128,256]{1,0:T(8,128)(2,1)S(1)} %get-tuple-element.51), channel_id=1, source_target_pairs={{0,24},{4,28},{8,16},{12,20},{16,8},{20,12},{24,0},{28,4},{1,25},{... | collective-permute-start | bytes 196616 | tf_op jit(solution)/shard_map/ppermute | solution.py:432
  65.8 0.3 collective-permute-done.17.refs_3_
  66.1 1.3 %collective-permute-start.22 = (bf16[128,256]{1,0:T(8,128)(2,1)S(1)}, bf16[128,256]{1,0:T(8,128)(2,1)S(1)}, u32[]{:S(2)}, u32[]{:S(2)}) collective-permute-start(bf16[128,256]{1,0:T(8,128)(2,1)S(1)} %get-tuple-element.50), channel_id=1, source_target_pairs={{0,28},{4,24},{8,20},{12,16},{16,12},{20,8},{24,4},{28,0},{1,29},{... | collective-permute-start | bytes 196616 | tf_op jit(solution)/shard_map/ppermute | solution.py:432
  67.4 0.0 collective-permute-done.18.refs_4_
  67.4 0.3 collective-permute-done.19.refs_5_
  67.6 0.8 %collective-permute-done.20.refs_6_ = bf16[128,256]{1,0:T(8,128)(2,1)S(1)} collective-permute-done((bf16[128,256]{1,0:T(8,128)(2,1)S(1)}, bf16[128,256]{1,0:T(8,128)(2,1)S(1)}, u32[]{:S(2)}, u32[]{:S(2)}) %collective-permute-start.20) | collective-permute-done | bytes 65568 | tf_op jit(solution)/shard_map/ppermute | solution.py:432
  68.4 1.8 %collective-permute-done.21.refs_7_ = bf16[128,256]{1,0:T(8,128)(2,1)S(1)} collective-permute-done((bf16[128,256]{1,0:T(8,128)(2,1)S(1)}, bf16[128,256]{1,0:T(8,128)(2,1)S(1)}, u32[]{:S(2)}, u32[]{:S(2)}) %collective-permute-start.21) | collective-permute-done | bytes 65568 | tf_op jit(solution)/shard_map/ppermute | solution.py:432
  70.2 1.1 %collective-permute-done.22.refs_8_ = bf16[128,256]{1,0:T(8,128)(2,1)S(1)} collective-permute-done((bf16[128,256]{1,0:T(8,128)(2,1)S(1)}, bf16[128,256]{1,0:T(8,128)(2,1)S(1)}, u32[]{:S(2)}, u32[]{:S(2)}) %collective-permute-start.22) | collective-permute-done | bytes 65568 | tf_op jit(solution)/shard_map/ppermute | solution.py:432
  71.4 0.0 all-to-all-done.refs_0_
  71.4 1.1 %unpack.1 = bf16[1,128,4096]{2,1,0:T(8,128)(2,1)} custom-call(bf16[8,128,256]{2,1,0:T(8,128)(2,1)S(1)} %all-to-all-done.refs_0_, bf16[128,256]{1,0:T(8,128)(2,1)S(1)} %get-tuple-element.57.refs_1_, bf16[128,256]{1,0:T(8,128)(2,1)S(1)} %collective-permute-done.16.refs_2_, bf16[128,256]{1,0:T(8,128)(2,1)S(1)} %collective-permute-done.17.refs_3_, ...), custom_call_target="tpu_custom_call" | custom-call | tf_op jit(solution)/shard_map/unpack/pallas_call | solution.py:144
  (2 shorter events, 0.0 us)
Async XLA Ops:
  0.6 16.7 %copy-start.1 = (f32[1,1024,512]{2,1,0:T(8,128)S(1)}, f32[1,1024,512]{2,1,0:T(8,128)}, u32[]{:S(2)}) copy-start(f32[1,1024,512]{2,1,0:T(8,128)} %param.8) | copy-start | bytes 6291460
  0.6 1.4 %copy-start.3 = (bf16[1,128,4096]{2,1,0:T(8,128)(2,1)S(1)}, bf16[1,128,4096]{2,1,0:T(8,128)(2,1)}, u32[]{:S(2)}) copy-start(bf16[1,128,4096]{2,1,0:T(8,128)(2,1)} %param.6) | copy-start | bytes 3145732
  2.0 1.2 %copy-start.4 = (bf16[1,128,4096]{2,1,0:T(8,128)(2,1)S(1)}, bf16[1,128,4096]{2,1,0:T(8,128)(2,1)}, u32[]{:S(2)}) copy-start(bf16[1,128,4096]{2,1,0:T(8,128)(2,1)} %param.7) | copy-start | bytes 3145732
  4.0 4.9 %collective-permute-start = (bf16[2,128,256]{2,1,0:T(8,128)(2,1)S(1)}, bf16[2,128,256]{2,1,0:T(8,128)(2,1)S(1)}, u32[]{:S(2)}, u32[]{:S(2)}) collective-permute-start(bf16[2,128,256]{2,1,0:T(8,128)(2,1)S(1)} %get-tuple-element.27), channel_id=1, source_target_pairs={{0,4},{4,0},{8,12},{12,8},{16,20},{20,16},{24,28},{28,24},{1,5},{5... | collective-permute-start | bytes 393224 | tf_op jit(solution)/shard_map/ppermute | solution.py:432
  4.5 7.0 %collective-permute-start.1 = (bf16[2,128,256]{2,1,0:T(8,128)(2,1)S(1)}, bf16[2,128,256]{2,1,0:T(8,128)(2,1)S(1)}, u32[]{:S(2)}, u32[]{:S(2)}) collective-permute-start(bf16[2,128,256]{2,1,0:T(8,128)(2,1)S(1)} %get-tuple-element.28), channel_id=1, source_target_pairs={{0,8},{4,12},{8,0},{12,4},{16,24},{20,28},{24,16},{28,20},{1,9},{5... | collective-permute-start | bytes 393224 | tf_op jit(solution)/shard_map/ppermute | solution.py:432
  7.1 6.6 %collective-permute-start.2 = (bf16[2,128,256]{2,1,0:T(8,128)(2,1)S(1)}, bf16[2,128,256]{2,1,0:T(8,128)(2,1)S(1)}, u32[]{:S(2)}, u32[]{:S(2)}) collective-permute-start(bf16[2,128,256]{2,1,0:T(8,128)(2,1)S(1)} %get-tuple-element.29), channel_id=1, source_target_pairs={{0,12},{4,8},{8,4},{12,0},{16,28},{20,24},{24,20},{28,16},{1,13},{... | collective-permute-start | bytes 393224 | tf_op jit(solution)/shard_map/ppermute | solution.py:432
  7.1 7.3 %collective-permute-start.3 = (bf16[2,128,256]{2,1,0:T(8,128)(2,1)S(1)}, bf16[2,128,256]{2,1,0:T(8,128)(2,1)S(1)}, u32[]{:S(2)}, u32[]{:S(2)}) collective-permute-start(bf16[2,128,256]{2,1,0:T(8,128)(2,1)S(1)} %get-tuple-element.30), channel_id=1, source_target_pairs={{0,16},{4,20},{8,24},{12,28},{16,0},{20,4},{24,8},{28,12},{1,17},{... | collective-permute-start | bytes 393224 | tf_op jit(solution)/shard_map/ppermute | solution.py:432
  8.9 11.8 %collective-permute-start.4 = (bf16[2,128,256]{2,1,0:T(8,128)(2,1)S(1)}, bf16[2,128,256]{2,1,0:T(8,128)(2,1)S(1)}, u32[]{:S(2)}, u32[]{:S(2)}) collective-permute-start(bf16[2,128,256]{2,1,0:T(8,128)(2,1)S(1)} %get-tuple-element.31), channel_id=1, source_target_pairs={{0,20},{4,16},{8,28},{12,24},{16,4},{20,0},{24,12},{28,8},{1,21},{... | collective-permute-start | bytes 393224 | tf_op jit(solution)/shard_map/ppermute | solution.py:432
  8.9 13.8 %collective-permute-start.5 = (bf16[2,128,256]{2,1,0:T(8,128)(2,1)S(1)}, bf16[2,128,256]{2,1,0:T(8,128)(2,1)S(1)}, u32[]{:S(2)}, u32[]{:S(2)}) collective-permute-start(bf16[2,128,256]{2,1,0:T(8,128)(2,1)S(1)} %get-tuple-element.32), channel_id=1, source_target_pairs={{0,24},{4,28},{8,16},{12,20},{16,8},{20,12},{24,0},{28,4},{1,25},{... | collective-permute-start | bytes 393224 | tf_op jit(solution)/shard_map/ppermute | solution.py:432
  11.5 12.8 %collective-permute-start.6 = (bf16[2,128,256]{2,1,0:T(8,128)(2,1)S(1)}, bf16[2,128,256]{2,1,0:T(8,128)(2,1)S(1)}, u32[]{:S(2)}, u32[]{:S(2)}) collective-permute-start(bf16[2,128,256]{2,1,0:T(8,128)(2,1)S(1)} %get-tuple-element.33), channel_id=1, source_target_pairs={{0,28},{4,24},{8,20},{12,16},{16,12},{20,8},{24,4},{28,0},{1,29},{... | collective-permute-start | bytes 393224 | tf_op jit(solution)/shard_map/ppermute | solution.py:432
  13.7 10.6 %collective-permute-start.8 = (bf16[2,128,256]{2,1,0:T(8,128)(2,1)S(1)}, bf16[2,128,256]{2,1,0:T(8,128)(2,1)S(1)}, u32[]{:S(2)}, u32[]{:S(2)}) collective-permute-start(bf16[2,128,256]{2,1,0:T(8,128)(2,1)S(1)} %get-tuple-element.37), channel_id=1, source_target_pairs={{0,4},{4,0},{8,12},{12,8},{16,20},{20,16},{24,28},{28,24},{1,5},{5... | collective-permute-start | bytes 393224 | tf_op jit(solution)/shard_map/ppermute | solution.py:432
  14.4 11.0 %collective-permute-start.9 = (bf16[2,128,256]{2,1,0:T(8,128)(2,1)S(1)}, bf16[2,128,256]{2,1,0:T(8,128)(2,1)S(1)}, u32[]{:S(2)}, u32[]{:S(2)}) collective-permute-start(bf16[2,128,256]{2,1,0:T(8,128)(2,1)S(1)} %get-tuple-element.38), channel_id=1, source_target_pairs={{0,8},{4,12},{8,0},{12,4},{16,24},{20,28},{24,16},{28,20},{1,9},{5... | collective-permute-start | bytes 393224 | tf_op jit(solution)/shard_map/ppermute | solution.py:432
  17.3 1.6 %copy-start.2 = (bf16[4,512,512]{2,1,0:T(8,128)(2,1)S(1)}, bf16[4,512,512]{2,1,0:T(8,128)(2,1)}, u32[]{:S(2)}) copy-start(bf16[4,512,512]{2,1,0:T(8,128)(2,1)} %constant.4.clone.fwd_ref.refs_10_) | copy-start | bytes 6291460
  18.9 8.3 %copy-start = (bf16[4,512,512]{2,1,0:T(8,128)(2,1)S(1)}, bf16[4,512,512]{2,1,0:T(8,128)(2,1)}, u32[]{:S(2)}) copy-start(bf16[4,512,512]{2,1,0:T(8,128)(2,1)} %constant.5.clone.refs_11_.inv_ref) | copy-start | bytes 6291460
  20.7 13.8 %collective-permute-start.10 = (bf16[2,128,256]{2,1,0:T(8,128)(2,1)S(1)}, bf16[2,128,256]{2,1,0:T(8,128)(2,1)S(1)}, u32[]{:S(2)}, u32[]{:S(2)}) collective-permute-start(bf16[2,128,256]{2,1,0:T(8,128)(2,1)S(1)} %get-tuple-element.39), channel_id=1, source_target_pairs={{0,12},{4,8},{8,4},{12,0},{16,28},{20,24},{24,20},{28,16},{1,13},{... | collective-permute-start | bytes 393224 | tf_op jit(solution)/shard_map/ppermute | solution.py:432
  22.8 15.4 %collective-permute-start.11 = (bf16[2,128,256]{2,1,0:T(8,128)(2,1)S(1)}, bf16[2,128,256]{2,1,0:T(8,128)(2,1)S(1)}, u32[]{:S(2)}, u32[]{:S(2)}) collective-permute-start(bf16[2,128,256]{2,1,0:T(8,128)(2,1)S(1)} %get-tuple-element.40), channel_id=1, source_target_pairs={{0,16},{4,20},{8,24},{12,28},{16,0},{20,4},{24,8},{28,12},{1,17},{... | collective-permute-start | bytes 393224 | tf_op jit(solution)/shard_map/ppermute | solution.py:432
  24.3 13.9 %collective-permute-start.12 = (bf16[2,128,256]{2,1,0:T(8,128)(2,1)S(1)}, bf16[2,128,256]{2,1,0:T(8,128)(2,1)S(1)}, u32[]{:S(2)}, u32[]{:S(2)}) collective-permute-start(bf16[2,128,256]{2,1,0:T(8,128)(2,1)S(1)} %get-tuple-element.41), channel_id=1, source_target_pairs={{0,20},{4,16},{8,28},{12,24},{16,4},{20,0},{24,12},{28,8},{1,21},{... | collective-permute-start | bytes 393224 | tf_op jit(solution)/shard_map/ppermute | solution.py:432
  24.3 13.9 %collective-permute-start.13 = (bf16[2,128,256]{2,1,0:T(8,128)(2,1)S(1)}, bf16[2,128,256]{2,1,0:T(8,128)(2,1)S(1)}, u32[]{:S(2)}, u32[]{:S(2)}) collective-permute-start(bf16[2,128,256]{2,1,0:T(8,128)(2,1)S(1)} %get-tuple-element.42), channel_id=1, source_target_pairs={{0,24},{4,28},{8,16},{12,20},{16,8},{20,12},{24,0},{28,4},{1,25},{... | collective-permute-start | bytes 393224 | tf_op jit(solution)/shard_map/ppermute | solution.py:432
  25.5 12.7 %collective-permute-start.14 = (bf16[2,128,256]{2,1,0:T(8,128)(2,1)S(1)}, bf16[2,128,256]{2,1,0:T(8,128)(2,1)S(1)}, u32[]{:S(2)}, u32[]{:S(2)}) collective-permute-start(bf16[2,128,256]{2,1,0:T(8,128)(2,1)S(1)} %get-tuple-element.43), channel_id=1, source_target_pairs={{0,28},{4,24},{8,20},{12,16},{16,12},{20,8},{24,4},{28,0},{1,29},{... | collective-permute-start | bytes 393224 | tf_op jit(solution)/shard_map/ppermute | solution.py:432
  34.5 15.9 %collective-permute-start.7 = (bf16[8,128,256]{2,1,0:T(8,128)(2,1)S(1)}, bf16[8,128,256]{2,1,0:T(8,128)(2,1)}, u32[]{:S(2)}, u32[]{:S(2)}) collective-permute-start(bf16[8,128,256]{2,1,0:T(8,128)(2,1)S(1)} %get-tuple-element.34), channel_id=1, source_target_pairs={{0,3},{1,0},{2,1},{3,2},{4,7},{5,4},{6,5},{7,6},{8,11},{9,8},{10,9... | collective-permute-start | bytes 1572872 | tf_op jit(solution)/shard_map/ppermute | solution.py:447
  45.5 15.4 %collective-permute-start.15 = (bf16[8,128,256]{2,1,0:T(8,128)(2,1)S(1)}, bf16[8,128,256]{2,1,0:T(8,128)(2,1)S(1)}, u32[]{:S(2)}, u32[]{:S(2)}) collective-permute-start(bf16[8,128,256]{2,1,0:T(8,128)(2,1)S(1)} %get-tuple-element.46), channel_id=1, source_target_pairs={{0,3},{1,0},{2,1},{3,2},{4,7},{5,4},{6,5},{7,6},{8,11},{9,8},{10,9... | collective-permute-start | bytes 1572872 | tf_op jit(solution)/shard_map/ppermute | solution.py:447
  50.4 20.9 %all-to-all-start = ((bf16[8,128,256]{2,1,0:T(8,128)(2,1)}), bf16[8,128,256]{2,1,0:T(8,128)(2,1)S(1)}, u32[]{:S(2)}, u32[]{:S(2)}) async-start(bf16[8,128,256]{2,1,0:T(8,128)(2,1)} %collective-permute-done.7), calls=%async_computation | async-start | bytes 1048576 | tf_op jit(solution)/shard_map/all_to_all | solution.py:430
  61.0 3.6 %collective-permute-start.16 = (bf16[128,256]{1,0:T(8,128)(2,1)S(1)}, bf16[128,256]{1,0:T(8,128)(2,1)S(1)}, u32[]{:S(2)}, u32[]{:S(2)}) collective-permute-start(bf16[128,256]{1,0:T(8,128)(2,1)S(1)} %get-tuple-element.56), channel_id=1, source_target_pairs={{0,4},{4,0},{8,12},{12,8},{16,20},{20,16},{24,28},{28,24},{1,5},{5... | collective-permute-start | bytes 196616 | tf_op jit(solution)/shard_map/ppermute | solution.py:432
  61.1 5.0 %collective-permute-start.17 = (bf16[128,256]{1,0:T(8,128)(2,1)S(1)}, bf16[128,256]{1,0:T(8,128)(2,1)S(1)}, u32[]{:S(2)}, u32[]{:S(2)}) collective-permute-start(bf16[128,256]{1,0:T(8,128)(2,1)S(1)} %get-tuple-element.55), channel_id=1, source_target_pairs={{0,8},{4,12},{8,0},{12,4},{16,24},{20,28},{24,16},{28,20},{1,9},{5... | collective-permute-start | bytes 196616 | tf_op jit(solution)/shard_map/ppermute | solution.py:432
  61.7 5.7 %collective-permute-start.18 = (bf16[128,256]{1,0:T(8,128)(2,1)S(1)}, bf16[128,256]{1,0:T(8,128)(2,1)S(1)}, u32[]{:S(2)}, u32[]{:S(2)}) collective-permute-start(bf16[128,256]{1,0:T(8,128)(2,1)S(1)} %get-tuple-element.54), channel_id=1, source_target_pairs={{0,12},{4,8},{8,4},{12,0},{16,28},{20,24},{24,20},{28,16},{1,13},{... | collective-permute-start | bytes 196616 | tf_op jit(solution)/shard_map/ppermute | solution.py:432
  63.0 4.7 %collective-permute-start.19 = (bf16[128,256]{1,0:T(8,128)(2,1)S(1)}, bf16[128,256]{1,0:T(8,128)(2,1)S(1)}, u32[]{:S(2)}, u32[]{:S(2)}) collective-permute-start(bf16[128,256]{1,0:T(8,128)(2,1)S(1)} %get-tuple-element.53), channel_id=1, source_target_pairs={{0,16},{4,20},{8,24},{12,28},{16,0},{20,4},{24,8},{28,12},{1,17},{... | collective-permute-start | bytes 196616 | tf_op jit(solution)/shard_map/ppermute | solution.py:432
  64.1 4.3 %collective-permute-start.20 = (bf16[128,256]{1,0:T(8,128)(2,1)S(1)}, bf16[128,256]{1,0:T(8,128)(2,1)S(1)}, u32[]{:S(2)}, u32[]{:S(2)}) collective-permute-start(bf16[128,256]{1,0:T(8,128)(2,1)S(1)} %get-tuple-element.52), channel_id=1, source_target_pairs={{0,20},{4,16},{8,28},{12,24},{16,4},{20,0},{24,12},{28,8},{1,21},{... | collective-permute-start | bytes 196616 | tf_op jit(solution)/shard_map/ppermute | solution.py:432
  64.7 5.6 %collective-permute-start.21 = (bf16[128,256]{1,0:T(8,128)(2,1)S(1)}, bf16[128,256]{1,0:T(8,128)(2,1)S(1)}, u32[]{:S(2)}, u32[]{:S(2)}) collective-permute-start(bf16[128,256]{1,0:T(8,128)(2,1)S(1)} %get-tuple-element.51), channel_id=1, source_target_pairs={{0,24},{4,28},{8,16},{12,20},{16,8},{20,12},{24,0},{28,4},{1,25},{... | collective-permute-start | bytes 196616 | tf_op jit(solution)/shard_map/ppermute | solution.py:432
  66.1 5.3 %collective-permute-start.22 = (bf16[128,256]{1,0:T(8,128)(2,1)S(1)}, bf16[128,256]{1,0:T(8,128)(2,1)S(1)}, u32[]{:S(2)}, u32[]{:S(2)}) collective-permute-start(bf16[128,256]{1,0:T(8,128)(2,1)S(1)} %get-tuple-element.50), channel_id=1, source_target_pairs={{0,28},{4,24},{8,20},{12,16},{16,12},{20,8},{24,4},{28,0},{1,29},{... | collective-permute-start | bytes 196616 | tf_op jit(solution)/shard_map/ppermute | solution.py:432

commit v5 on v4

--- a/solution.py
+++ b/solution.py
@@ -11,6 +11,7 @@
 
 WHOLE_IN = (False, False)
 WHOLE_OUT = (True, False)
+PARTS = (1, 2)
 CHUNKS = len(WHOLE_IN)
 PAD = 8
 TILE = 16
@@ -185,12 +186,15 @@
     )(kernel, fwd)
 
 
-def section_kernel(devices, chunk, whole_in, whole_out, *refs):
+def section_kernel(devices, chunk, whole_in, whole_out, parts, *refs):
     taken = 1 if whole_in else devices
     (pieces,) = by_target(refs[:taken], devices, [whole_in])
-    tap_ref, spec_ref, fwd_ref, inv_ref, out_ref, cross_ref = refs[taken : taken + 6]
-    padded, upstream, key_rows, value_rows, turned, mixed, back = refs[taken + 6 : taken + 13]
-    shifted_rows, grad_rows, tap_rows, tap_sem = refs[taken + 13 :]
+    tap_ref, spec_ref, fwd_ref, inv_ref = refs[taken : taken + 4]
+    refs = refs[taken + 4 :]
+    out_refs, refs = refs[:parts], refs[parts:]
+    cross_ref, refs = refs[0], refs[1:]
+    padded, upstream, key_rows, value_rows, turned, mixed, back = refs[:7]
+    shifted_rows, grad_rows, tap_rows, tap_sem = refs[7:]
     me = lax.axis_index("seq")
     length, width = pieces[0][1].shape[1:]
     rows = length * devices
@@ -270,10 +274,11 @@
         grad_rows[pl.ds(begin, LAST_TILE), :] = total.astype(jnp.bfloat16)
 
     for k in range(devices):
-        out_ref[k] = grad_rows[place(k if whole_out else me ^ k, 0), :]
-
-
-def section(pieces, taps, spec, fwd, inv, chunk, devices, whole_in, whole_out):
+        number, within = divmod(k, devices // parts)
+        out_refs[number][within] = grad_rows[place(k if whole_out else me ^ k, 0), :]
+
+
+def section(pieces, taps, spec, fwd, inv, chunk, devices, whole_in, whole_out, parts):
     length, width = pieces[0].shape[-2:]
     rows = devices * length
     near = pl.BlockSpec(memory_space=pltpu.VMEM)
@@ -281,11 +286,11 @@
     single = lambda *shape: pltpu.VMEM(shape, jnp.float32)
     half = lambda *shape: pltpu.VMEM(shape, jnp.bfloat16)
     return pl.pallas_call(
-        functools.partial(section_kernel, devices, chunk, whole_in, whole_out),
+        functools.partial(section_kernel, devices, chunk, whole_in, whole_out, parts),
         in_specs=[near] * len(pieces) + [far] + [near] * 3,
-        out_specs=[near] * 2,
-        out_shape=[
-            jax.ShapeDtypeStruct((devices, length, width), jnp.bfloat16),
+        out_specs=[near] * (parts + 1),
+        out_shape=[jax.ShapeDtypeStruct((devices // parts, length, width), jnp.bfloat16)] * parts
+        + [
             jax.ShapeDtypeStruct((4, rows // 2, width), jnp.bfloat16),
         ],
         scratch_shapes=[
@@ -441,17 +446,27 @@
     grads, crosses = [], []
     for chunk in range(CHUNKS):
         arrived = exchanged(pieces[chunk], devices, WHOLE_IN[chunk])
-        grad, cross = section(
-            arrived, taps, spec, fwd, inv, chunk, devices, WHOLE_IN[chunk], WHOLE_OUT[chunk]
+        *parts, cross = section(
+            arrived, taps, spec, fwd, inv, chunk, devices, WHOLE_IN[chunk], WHOLE_OUT[chunk],
+            PARTS[chunk],
         )
-        grads.append(lax.ppermute(grad, "pipe", before))
+        moved = [lax.ppermute(part, "pipe", before) for part in parts[::-1]]
+        grads.append(moved[::-1])
         crosses.append(cross)
     filter_grad = filter_gradient(inv, crosses)
     home = []
-    for grad, whole in zip(grads, WHOLE_OUT):
-        grad, filter_grad = lax.optimization_barrier((grad, filter_grad))
+    for parts, whole in zip(grads, WHOLE_OUT):
+        ready = []
+        for part in parts:
+            part, filter_grad = lax.optimization_barrier((part, filter_grad))
+            ready.append(part)
+        each = devices // len(ready)
         home.append(
-            exchanged([grad] if whole else [grad[k] for k in range(devices)], devices, whole)
+            exchanged(
+                ready if whole else [ready[k // each][k % each] for k in range(devices)],
+                devices,
+                whole,
+            )
         )
     return unpack(home, devices, WHOLE_OUT), filter_grad[None]
 

time: 72.7 us -> 70.9 us (0.975)
  waiting for transfers between devices: 12.5 us -> 11.4 us
    ppermute x2 -> x3, waiting for transfers between devices: 7.64 us -> 5.22 us  [fast(): moved = [lax.ppermute(part, 'pipe', before) for part in parts[::-1]]]
    ppermute x21, waiting for transfers between devices: 4.89 us -> 6.17 us  [exchanged(): lax.ppermute(chunk[k], 'seq', pairs(k))]
    ppermute x21, starting transfers between devices: 24.2 us -> 23 us  [exchanged(): lax.ppermute(chunk[k], 'seq', pairs(k))]
    ppermute x2 -> x3, starting transfers between devices: 4.79 us -> 5.23 us  [fast(): moved = [lax.ppermute(part, 'pipe', before) for part in parts[::-1]]]
  transfers between devices with their start and end apart: 24 -> 25, of which waited for: 8 -> 9; matrix products, arithmetic and copies ran while one was open for 1% -> 1% of each run, Pallas kernels for 27% -> 28%
where the time goes in v5:
time: 70.9 us; the launch traced here: 70.6 us
  starting transfers between devices  31.7 us (45%)
  Pallas kernels  21.5 us (30%)
  waiting for transfers between devices  11.4 us (16%)
  local copies, waits for them, and re-layouts  5.23 us (7%)
  between operations  0.78 us (1%)
    ppermute x21, starting transfers between devices, exchanged(): lax.ppermute(chunk[k], 'seq', pairs(k))  23 us
    pallas_call x2, Pallas kernels, section(): pl.pallas_call(functools.partial(section_kernel, devices, chunk, whole_in...  14.7 us
    ppermute x21, waiting for transfers between devices, exchanged(): lax.ppermute(chunk[k], 'seq', pairs(k))  6.17 us
    ppermute x3, starting transfers between devices, fast(): moved = [lax.ppermute(part, 'pipe', before) for part in parts[::-1]]  5.23 us
    ppermute x3, waiting for transfers between devices, fast(): moved = [lax.ppermute(part, 'pipe', before) for part in parts[::-1]]  5.22 us
    unnamed x11, local copies, waits for them, and re-layouts  5.2 us
    all_to_all x1, starting transfers between devices, exchanged(): lax.all_to_all(chunk[0], 'seq', split_axis=0, concat_axis=0, tiled=True)  3.49 us
    pallas_call x1, Pallas kernels, filter_gradient(): pl.pallas_call(filter_kernel, in_specs=[pl.BlockSpec(memory_space=pltpu.V...  3.16 us
  transfers between devices with their start and end apart: 25, of which 9 were waited for; matrix products, arithmetic and copies ran while one was open for 1% of the time, Pallas kernels for 28%

profile of v5, /device:TPU:0, one launch (start us, length us, event | category | flops | bytes accessed | tf_op | source)
XLA Modules:
  0.0 70.6 jit_solution(11889624436021073037)
XLA Ops:
  0.6 0.0 copy-start.1
  0.6 0.0 copy-start.3
  0.6 1.4 %copy-done.3 = bf16[1,128,4096]{2,1,0:T(8,128)(2,1)S(1)} copy-done((bf16[1,128,4096]{2,1,0:T(8,128)(2,1)S(1)}, bf16[1,128,4096]{2,1,0:T(8,128)(2,1)}, u32[]{:S(2)}) %copy-start.3) | copy-done | bytes 1048600
  2.0 1.2 %copy-done.4 = bf16[1,128,4096]{2,1,0:T(8,128)(2,1)S(1)} copy-done((bf16[1,128,4096]{2,1,0:T(8,128)(2,1)S(1)}, bf16[1,128,4096]{2,1,0:T(8,128)(2,1)}, u32[]{:S(2)}) %copy-start.4) | copy-done | bytes 1048600
  3.2 0.7 %pack.1 = (bf16[2,128,256]{2,1,0:T(8,128)(2,1)S(1)}, bf16[2,128,256]{2,1,0:T(8,128)(2,1)S(1)}, bf16[2,128,256]{2,1,0:T(8,128)(2,1)S(1)}, bf16[2,128,256]{2,1,0:T...) custom-call(bf16[128,4096]{1,0:T(8,128)(2,1)S(1)} %bitcast.21, ...), custom_call_target="tpu_custom_call" | custom-call | tf_op jit(solution)/shard_map/pack/pallas_call | solution.py:103
  4.0 0.5 collective-permute-start
  4.5 2.6 %collective-permute-start.1 = (bf16[2,128,256]{2,1,0:T(8,128)(2,1)S(1)}, bf16[2,128,256]{2,1,0:T(8,128)(2,1)S(1)}, u32[]{:S(2)}, u32[]{:S(2)}) collective-permute-start(bf16[2,128,256]{2,1,0:T(8,128)(2,1)S(1)} %get-tuple-element.31), channel_id=1, source_target_pairs={{0,8},{4,12},{8,0},{12,4},{16,24},{20,28},{24,16},{28,20},{1,9},{5... | collective-permute-start | bytes 393224 | tf_op jit(solution)/shard_map/ppermute | solution.py:437
  7.1 0.1 collective-permute-start.2
  7.1 1.8 %collective-permute-start.3 = (bf16[2,128,256]{2,1,0:T(8,128)(2,1)S(1)}, bf16[2,128,256]{2,1,0:T(8,128)(2,1)S(1)}, u32[]{:S(2)}, u32[]{:S(2)}) collective-permute-start(bf16[2,128,256]{2,1,0:T(8,128)(2,1)S(1)} %get-tuple-element.33), channel_id=1, source_target_pairs={{0,16},{4,20},{8,24},{12,28},{16,0},{20,4},{24,8},{28,12},{1,17},{... | collective-permute-start | bytes 393224 | tf_op jit(solution)/shard_map/ppermute | solution.py:437
  8.9 0.0 collective-permute-start.4
  8.9 0.0 collective-permute-done.refs_1_
  8.9 2.6 %collective-permute-start.5 = (bf16[2,128,256]{2,1,0:T(8,128)(2,1)S(1)}, bf16[2,128,256]{2,1,0:T(8,128)(2,1)S(1)}, u32[]{:S(2)}, u32[]{:S(2)}) collective-permute-start(bf16[2,128,256]{2,1,0:T(8,128)(2,1)S(1)} %get-tuple-element.35), channel_id=1, source_target_pairs={{0,24},{4,28},{8,16},{12,20},{16,8},{20,12},{24,0},{28,4},{1,25},{... | collective-permute-start | bytes 393224 | tf_op jit(solution)/shard_map/ppermute | solution.py:437
  11.5 0.0 collective-permute-done.1.refs_2_
  11.5 1.6 %collective-permute-start.6 = (bf16[2,128,256]{2,1,0:T(8,128)(2,1)S(1)}, bf16[2,128,256]{2,1,0:T(8,128)(2,1)S(1)}, u32[]{:S(2)}, u32[]{:S(2)}) collective-permute-start(bf16[2,128,256]{2,1,0:T(8,128)(2,1)S(1)} %get-tuple-element.36), channel_id=1, source_target_pairs={{0,28},{4,24},{8,20},{12,16},{16,12},{20,8},{24,4},{28,0},{1,29},{... | collective-permute-start | bytes 393224 | tf_op jit(solution)/shard_map/ppermute | solution.py:437
  13.1 0.6 collective-permute-done.2.refs_3_
  13.7 0.7 %collective-permute-start.8 = (bf16[2,128,256]{2,1,0:T(8,128)(2,1)S(1)}, bf16[2,128,256]{2,1,0:T(8,128)(2,1)S(1)}, u32[]{:S(2)}, u32[]{:S(2)}) collective-permute-start(bf16[2,128,256]{2,1,0:T(8,128)(2,1)S(1)} %get-tuple-element.40), channel_id=1, source_target_pairs={{0,4},{4,0},{8,12},{12,8},{16,20},{20,16},{24,28},{28,24},{1,5},{5... | collective-permute-start | bytes 393224 | tf_op jit(solution)/shard_map/ppermute | solution.py:437
  14.4 0.0 collective-permute-done.3.refs_4_
  14.4 1.8 %collective-permute-start.9 = (bf16[2,128,256]{2,1,0:T(8,128)(2,1)S(1)}, bf16[2,128,256]{2,1,0:T(8,128)(2,1)S(1)}, u32[]{:S(2)}, u32[]{:S(2)}) collective-permute-start(bf16[2,128,256]{2,1,0:T(8,128)(2,1)S(1)} %get-tuple-element.41), channel_id=1, source_target_pairs={{0,8},{4,12},{8,0},{12,4},{16,24},{20,28},{24,16},{28,20},{1,9},{5... | collective-permute-start | bytes 393224 | tf_op jit(solution)/shard_map/ppermute | solution.py:437
  16.3 1.0 %copy.8.refs_8_ = f32[1,3,3,4096]{3,2,1,0:T(4,128)S(1)} copy(f32[1,3,3,4096]{3,0,2,1:T(1,128)} %param.9) | data formatting | bytes 294912 | tf_op args[3]
  17.3 0.0 copy-done.1
  17.3 0.0 copy-start.2
  17.3 1.6 %copy-done.2 = bf16[4,512,512]{2,1,0:T(8,128)(2,1)S(1)} copy-done((bf16[4,512,512]{2,1,0:T(8,128)(2,1)S(1)}, bf16[4,512,512]{2,1,0:T(8,128)(2,1)}, u32[]{:S(2)}) %copy-start.2) | copy-done | bytes 2097176
  18.9 1.8 %spectrum.1.refs_9_ = f32[4,512,512]{2,1,0:T(8,128)S(1)} custom-call(f32[1024,512]{1,0:T(8,128)S(1)} %bitcast.20, bf16[4,512,512]{2,1,0:T(8,128)(2,1)S(1)} %copy-done.2), custom_call_target="tpu_custom_call" | custom-call | flops 1073741824 | bytes 7340032 | tf_op jit(solution)/shard_map/spectrum/pallas_call | solution.py:175
  20.7 0.0 collective-permute-done.4.refs_5_
  20.7 2.0 %collective-permute-start.10 = (bf16[2,128,256]{2,1,0:T(8,128)(2,1)S(1)}, bf16[2,128,256]{2,1,0:T(8,128)(2,1)S(1)}, u32[]{:S(2)}, u32[]{:S(2)}) collective-permute-start(bf16[2,128,256]{2,1,0:T(8,128)(2,1)S(1)} %get-tuple-element.42), channel_id=1, source_target_pairs={{0,12},{4,8},{8,4},{12,0},{16,28},{20,24},{24,20},{28,16},{1,13},{... | collective-permute-start | bytes 393224 | tf_op jit(solution)/shard_map/ppermute | solution.py:437
  22.7 0.0 collective-permute-done.5.refs_6_
  22.8 1.5 %collective-permute-start.11 = (bf16[2,128,256]{2,1,0:T(8,128)(2,1)S(1)}, bf16[2,128,256]{2,1,0:T(8,128)(2,1)S(1)}, u32[]{:S(2)}, u32[]{:S(2)}) collective-permute-start(bf16[2,128,256]{2,1,0:T(8,128)(2,1)S(1)} %get-tuple-element.43), channel_id=1, source_target_pairs={{0,16},{4,20},{8,24},{12,28},{16,0},{20,4},{24,8},{28,12},{1,17},{... | collective-permute-start | bytes 393224 | tf_op jit(solution)/shard_map/ppermute | solution.py:437
  24.3 0.0 collective-permute-done.6.refs_7_
  24.3 0.0 collective-permute-start.12
  24.3 0.0 collective-permute-done.8.refs_1_
  24.3 1.2 %collective-permute-start.13 = (bf16[2,128,256]{2,1,0:T(8,128)(2,1)S(1)}, bf16[2,128,256]{2,1,0:T(8,128)(2,1)S(1)}, u32[]{:S(2)}, u32[]{:S(2)}) collective-permute-start(bf16[2,128,256]{2,1,0:T(8,128)(2,1)S(1)} %get-tuple-element.45), channel_id=1, source_target_pairs={{0,24},{4,28},{8,16},{12,20},{16,8},{20,12},{24,0},{28,4},{1,25},{... | collective-permute-start | bytes 393224 | tf_op jit(solution)/shard_map/ppermute | solution.py:437
  25.5 0.0 collective-permute-done.9.refs_2_
  25.5 1.7 %collective-permute-start.14 = (bf16[2,128,256]{2,1,0:T(8,128)(2,1)S(1)}, bf16[2,128,256]{2,1,0:T(8,128)(2,1)S(1)}, u32[]{:S(2)}, u32[]{:S(2)}) collective-permute-start(bf16[2,128,256]{2,1,0:T(8,128)(2,1)S(1)} %get-tuple-element.46), channel_id=1, source_target_pairs={{0,28},{4,24},{8,20},{12,16},{16,12},{20,8},{24,4},{28,0},{1,29},{... | collective-permute-start | bytes 393224 | tf_op jit(solution)/shard_map/ppermute | solution.py:437
  27.2 7.3 %section.2 = (bf16[8,128,256]{2,1,0:T(8,128)(2,1)S(1)}, bf16[4,512,256]{2,1,0:T(8,128)(2,1)S(1)}) custom-call(bf16[2,128,256]{2,1,0:T(8,128)(2,1)S(1)} %get-tuple-element.29.refs_0_, bf16[2,128,256]{2,1,0:T(8,128)(2,1)S(1)} %collective-permute-done.refs_1_, bf16[2,128,256]{2,1,0:T(8,128)(2,1)S(1)} %collective-permute-done.1.refs_2_, ...), custom_call_target="tpu_custom_call" | custom-call | flops 2684354560 | bytes 5242880 | tf_op jit(solution)/shard_map/section/pallas_call | solution.py:288
  34.5 0.0 collective-permute-done.10.refs_3_
  34.5 3.7 %collective-permute-start.7 = (bf16[8,128,256]{2,1,0:T(8,128)(2,1)S(1)}, bf16[8,128,256]{2,1,0:T(8,128)(2,1)}, u32[]{:S(2)}, u32[]{:S(2)}) collective-permute-start(bf16[8,128,256]{2,1,0:T(8,128)(2,1)S(1)} %get-tuple-element.37), channel_id=1, source_target_pairs={{0,3},{1,0},{2,1},{3,2},{4,7},{5,4},{6,5},{7,6},{8,11},{9,8},{10,9... | collective-permute-start | bytes 1572872 | tf_op jit(solution)/shard_map/ppermute | solution.py:453
  38.2 0.0 collective-permute-done.11.refs_4_
  38.2 0.0 collective-permute-done.12.refs_5_
  38.2 0.0 collective-permute-done.13.refs_6_
  38.2 0.0 collective-permute-done.14.refs_7_
  38.2 7.4 %section.3 = (bf16[4,128,256]{2,1,0:T(8,128)(2,1)S(1)}, bf16[4,128,256]{2,1,0:T(8,128)(2,1)S(1)}, bf16[4,512,256]{2,1,0:T(8,128)(2,1)S(1)}) custom-call(bf16[2,128,256]{2,1,0:T(8,128)(2,1)S(1)} %get-tuple-element.39.refs_0_, bf16[2,128,256]{2,1,0:T(8,128)(2,1)S(1)} %collective-permute-done.8.refs_1_, ...), custom_call_target="tpu_custom_call" | custom-call | flops 2684354560 | bytes 5242880 | tf_op jit(solution)/shard_map/section/pallas_call | solution.py:288
  45.6 1.1 %collective-permute-start.15 = (bf16[4,128,256]{2,1,0:T(8,128)(2,1)S(1)}, bf16[4,128,256]{2,1,0:T(8,128)(2,1)S(1)}, u32[]{:S(2)}, u32[]{:S(2)}) collective-permute-start(bf16[4,128,256]{2,1,0:T(8,128)(2,1)S(1)} %get-tuple-element.49), channel_id=1, source_target_pairs={{0,3},{1,0},{2,1},{3,2},{4,7},{5,4},{6,5},{7,6},{8,11},{9,8},{10,9... | collective-permute-start | bytes 786440 | tf_op jit(solution)/shard_map/ppermute | solution.py:453
  46.7 0.4 collective-permute-start.19
  47.1 3.2 %filter.1 = f32[1024,512]{1,0:T(8,128)} custom-call(bf16[4,512,512]{2,1,0:T(8,128)(2,1)S(1)} %copy-done, bf16[4,512,256]{2,1,0:T(8,128)(2,1)S(1)} %get-tuple-element.38.refs_0_, bf16[4,512,256]{2,1,0:T(8,128)(2,1)S(1)} %get-tuple-element.47.refs_1_), custom_call_target="tpu_custom_call" | custom-call | flops 1073741824 | bytes 3145728 | tf_op jit(solution)/shard_map/filter/pallas_call | solution.py:343
  50.3 0.1 collective-permute-done.7
  50.4 3.5 %all-to-all-start = ((bf16[8,128,256]{2,1,0:T(8,128)(2,1)}), bf16[8,128,256]{2,1,0:T(8,128)(2,1)S(1)}, u32[]{:S(2)}, u32[]{:S(2)}) async-start(bf16[8,128,256]{2,1,0:T(8,128)(2,1)} %collective-permute-done.7), calls=%async_computation | async-start | bytes 1048576 | tf_op jit(solution)/shard_map/all_to_all | solution.py:435
  53.9 2.1 %collective-permute-done.15 = bf16[4,128,256]{2,1,0:T(8,128)(2,1)S(1)} collective-permute-done((bf16[4,128,256]{2,1,0:T(8,128)(2,1)S(1)}, bf16[4,128,256]{2,1,0:T(8,128)(2,1)S(1)}, u32[]{:S(2)}, u32[]{:S(2)}) %collective-permute-start.15) | collective-permute-done | bytes 262176 | tf_op jit(solution)/shard_map/ppermute | solution.py:453
  56.1 0.1 collective-permute-start.16
  56.2 0.6 collective-permute-start.17
  56.8 1.3 %collective-permute-start.18 = (bf16[128,256]{1,0:T(8,128)(2,1)S(1)}, bf16[128,256]{1,0:T(8,128)(2,1)S(1)}, u32[]{:S(2)}, u32[]{:S(2)}) collective-permute-start(bf16[128,256]{1,0:T(8,128)(2,1)S(1)} %get-tuple-element.60), channel_id=1, source_target_pairs={{0,12},{4,8},{8,4},{12,0},{16,28},{20,24},{24,20},{28,16},{1,13},{... | collective-permute-start | bytes 196616 | tf_op jit(solution)/shard_map/ppermute | solution.py:437
  58.0 3.0 %collective-permute-done.19 = bf16[4,128,256]{2,1,0:T(8,128)(2,1)S(1)} collective-permute-done((bf16[4,128,256]{2,1,0:T(8,128)(2,1)S(1)}, bf16[4,128,256]{2,1,0:T(8,128)(2,1)S(1)}, u32[]{:S(2)}, u32[]{:S(2)}) %collective-permute-start.19) | collective-permute-done | bytes 262176 | tf_op jit(solution)/shard_map/ppermute | solution.py:453
  61.0 1.2 %collective-permute-start.20 = (bf16[128,256]{1,0:T(8,128)(2,1)S(1)}, bf16[128,256]{1,0:T(8,128)(2,1)S(1)}, u32[]{:S(2)}, u32[]{:S(2)}) collective-permute-start(bf16[128,256]{1,0:T(8,128)(2,1)S(1)} %get-tuple-element.59), channel_id=1, source_target_pairs={{0,16},{4,20},{8,24},{12,28},{16,0},{20,4},{24,8},{28,12},{1,17},{... | collective-permute-start | bytes 196616 | tf_op jit(solution)/shard_map/ppermute | solution.py:437
  62.2 0.0 collective-permute-start.21
  62.2 0.0 collective-permute-done.16.refs_2_
  62.2 0.9 %collective-permute-start.22 = (bf16[128,256]{1,0:T(8,128)(2,1)S(1)}, bf16[128,256]{1,0:T(8,128)(2,1)S(1)}, u32[]{:S(2)}, u32[]{:S(2)}) collective-permute-start(bf16[128,256]{1,0:T(8,128)(2,1)S(1)} %get-tuple-element.57), channel_id=1, source_target_pairs={{0,24},{4,28},{8,16},{12,20},{16,8},{20,12},{24,0},{28,4},{1,25},{... | collective-permute-start | bytes 196616 | tf_op jit(solution)/shard_map/ppermute | solution.py:437
  63.1 1.5 %collective-permute-done.17.refs_3_ = bf16[128,256]{1,0:T(8,128)(2,1)S(1)} collective-permute-done((bf16[128,256]{1,0:T(8,128)(2,1)S(1)}, bf16[128,256]{1,0:T(8,128)(2,1)S(1)}, u32[]{:S(2)}, u32[]{:S(2)}) %collective-permute-start.17) | collective-permute-done | bytes 65568 | tf_op jit(solution)/shard_map/ppermute | solution.py:437
  64.6 0.9 %collective-permute-start.23 = (bf16[128,256]{1,0:T(8,128)(2,1)S(1)}, bf16[128,256]{1,0:T(8,128)(2,1)S(1)}, u32[]{:S(2)}, u32[]{:S(2)}) collective-permute-start(bf16[128,256]{1,0:T(8,128)(2,1)S(1)} %get-tuple-element.56), channel_id=1, source_target_pairs={{0,28},{4,24},{8,20},{12,16},{16,12},{20,8},{24,4},{28,0},{1,29},{... | collective-permute-start | bytes 196616 | tf_op jit(solution)/shard_map/ppermute | solution.py:437
  65.5 0.0 collective-permute-done.18.refs_4_
  65.5 0.1 collective-permute-done.20.refs_5_
  65.6 1.2 %collective-permute-done.21.refs_6_ = bf16[128,256]{1,0:T(8,128)(2,1)S(1)} collective-permute-done((bf16[128,256]{1,0:T(8,128)(2,1)S(1)}, bf16[128,256]{1,0:T(8,128)(2,1)S(1)}, u32[]{:S(2)}, u32[]{:S(2)}) %collective-permute-start.21) | collective-permute-done | bytes 65568 | tf_op jit(solution)/shard_map/ppermute | solution.py:437
  66.8 1.3 %collective-permute-done.22.refs_7_ = bf16[128,256]{1,0:T(8,128)(2,1)S(1)} collective-permute-done((bf16[128,256]{1,0:T(8,128)(2,1)S(1)}, bf16[128,256]{1,0:T(8,128)(2,1)S(1)}, u32[]{:S(2)}, u32[]{:S(2)}) %collective-permute-start.22) | collective-permute-done | bytes 65568 | tf_op jit(solution)/shard_map/ppermute | solution.py:437
  68.1 1.5 %collective-permute-done.23.refs_8_ = bf16[128,256]{1,0:T(8,128)(2,1)S(1)} collective-permute-done((bf16[128,256]{1,0:T(8,128)(2,1)S(1)}, bf16[128,256]{1,0:T(8,128)(2,1)S(1)}, u32[]{:S(2)}, u32[]{:S(2)}) %collective-permute-start.23) | collective-permute-done | bytes 65568 | tf_op jit(solution)/shard_map/ppermute | solution.py:437
  69.6 0.0 all-to-all-done.refs_0_
  69.6 1.1 %unpack.1 = bf16[1,128,4096]{2,1,0:T(8,128)(2,1)} custom-call(bf16[8,128,256]{2,1,0:T(8,128)(2,1)S(1)} %all-to-all-done.refs_0_, bf16[128,256]{1,0:T(8,128)(2,1)S(1)} %get-tuple-element.63.refs_1_, bf16[128,256]{1,0:T(8,128)(2,1)S(1)} %collective-permute-done.16.refs_2_, bf16[128,256]{1,0:T(8,128)(2,1)S(1)} %collective-permute-done.17.refs_3_, ...), custom_call_target="tpu_custom_call" | custom-call | tf_op jit(solution)/shard_map/unpack/pallas_call | solution.py:145
  (5 shorter events, 0.0 us)
Async XLA Ops:
  0.6 16.7 %copy-start.1 = (f32[1,1024,512]{2,1,0:T(8,128)S(1)}, f32[1,1024,512]{2,1,0:T(8,128)}, u32[]{:S(2)}) copy-start(f32[1,1024,512]{2,1,0:T(8,128)} %param.8) | copy-start | bytes 6291460
  0.6 1.4 %copy-start.3 = (bf16[1,128,4096]{2,1,0:T(8,128)(2,1)S(1)}, bf16[1,128,4096]{2,1,0:T(8,128)(2,1)}, u32[]{:S(2)}) copy-start(bf16[1,128,4096]{2,1,0:T(8,128)(2,1)} %param.6) | copy-start | bytes 3145732
  2.0 1.2 %copy-start.4 = (bf16[1,128,4096]{2,1,0:T(8,128)(2,1)S(1)}, bf16[1,128,4096]{2,1,0:T(8,128)(2,1)}, u32[]{:S(2)}) copy-start(bf16[1,128,4096]{2,1,0:T(8,128)(2,1)} %param.7) | copy-start | bytes 3145732
  4.0 4.9 %collective-permute-start = (bf16[2,128,256]{2,1,0:T(8,128)(2,1)S(1)}, bf16[2,128,256]{2,1,0:T(8,128)(2,1)S(1)}, u32[]{:S(2)}, u32[]{:S(2)}) collective-permute-start(bf16[2,128,256]{2,1,0:T(8,128)(2,1)S(1)} %get-tuple-element.30), channel_id=1, source_target_pairs={{0,4},{4,0},{8,12},{12,8},{16,20},{20,16},{24,28},{28,24},{1,5},{5... | collective-permute-start | bytes 393224 | tf_op jit(solution)/shard_map/ppermute | solution.py:437
  4.5 7.0 %collective-permute-start.1 = (bf16[2,128,256]{2,1,0:T(8,128)(2,1)S(1)}, bf16[2,128,256]{2,1,0:T(8,128)(2,1)S(1)}, u32[]{:S(2)}, u32[]{:S(2)}) collective-permute-start(bf16[2,128,256]{2,1,0:T(8,128)(2,1)S(1)} %get-tuple-element.31), channel_id=1, source_target_pairs={{0,8},{4,12},{8,0},{12,4},{16,24},{20,28},{24,16},{28,20},{1,9},{5... | collective-permute-start | bytes 393224 | tf_op jit(solution)/shard_map/ppermute | solution.py:437
  7.1 6.6 %collective-permute-start.2 = (bf16[2,128,256]{2,1,0:T(8,128)(2,1)S(1)}, bf16[2,128,256]{2,1,0:T(8,128)(2,1)S(1)}, u32[]{:S(2)}, u32[]{:S(2)}) collective-permute-start(bf16[2,128,256]{2,1,0:T(8,128)(2,1)S(1)} %get-tuple-element.32), channel_id=1, source_target_pairs={{0,12},{4,8},{8,4},{12,0},{16,28},{20,24},{24,20},{28,16},{1,13},{... | collective-permute-start | bytes 393224 | tf_op jit(solution)/shard_map/ppermute | solution.py:437
  7.1 7.3 %collective-permute-start.3 = (bf16[2,128,256]{2,1,0:T(8,128)(2,1)S(1)}, bf16[2,128,256]{2,1,0:T(8,128)(2,1)S(1)}, u32[]{:S(2)}, u32[]{:S(2)}) collective-permute-start(bf16[2,128,256]{2,1,0:T(8,128)(2,1)S(1)} %get-tuple-element.33), channel_id=1, source_target_pairs={{0,16},{4,20},{8,24},{12,28},{16,0},{20,4},{24,8},{28,12},{1,17},{... | collective-permute-start | bytes 393224 | tf_op jit(solution)/shard_map/ppermute | solution.py:437
  8.9 11.8 %collective-permute-start.4 = (bf16[2,128,256]{2,1,0:T(8,128)(2,1)S(1)}, bf16[2,128,256]{2,1,0:T(8,128)(2,1)S(1)}, u32[]{:S(2)}, u32[]{:S(2)}) collective-permute-start(bf16[2,128,256]{2,1,0:T(8,128)(2,1)S(1)} %get-tuple-element.34), channel_id=1, source_target_pairs={{0,20},{4,16},{8,28},{12,24},{16,4},{20,0},{24,12},{28,8},{1,21},{... | collective-permute-start | bytes 393224 | tf_op jit(solution)/shard_map/ppermute | solution.py:437
  8.9 13.8 %collective-permute-start.5 = (bf16[2,128,256]{2,1,0:T(8,128)(2,1)S(1)}, bf16[2,128,256]{2,1,0:T(8,128)(2,1)S(1)}, u32[]{:S(2)}, u32[]{:S(2)}) collective-permute-start(bf16[2,128,256]{2,1,0:T(8,128)(2,1)S(1)} %get-tuple-element.35), channel_id=1, source_target_pairs={{0,24},{4,28},{8,16},{12,20},{16,8},{20,12},{24,0},{28,4},{1,25},{... | collective-permute-start | bytes 393224 | tf_op jit(solution)/shard_map/ppermute | solution.py:437
  11.5 12.8 %collective-permute-start.6 = (bf16[2,128,256]{2,1,0:T(8,128)(2,1)S(1)}, bf16[2,128,256]{2,1,0:T(8,128)(2,1)S(1)}, u32[]{:S(2)}, u32[]{:S(2)}) collective-permute-start(bf16[2,128,256]{2,1,0:T(8,128)(2,1)S(1)} %get-tuple-element.36), channel_id=1, source_target_pairs={{0,28},{4,24},{8,20},{12,16},{16,12},{20,8},{24,4},{28,0},{1,29},{... | collective-permute-start | bytes 393224 | tf_op jit(solution)/shard_map/ppermute | solution.py:437
  13.7 10.6 %collective-permute-start.8 = (bf16[2,128,256]{2,1,0:T(8,128)(2,1)S(1)}, bf16[2,128,256]{2,1,0:T(8,128)(2,1)S(1)}, u32[]{:S(2)}, u32[]{:S(2)}) collective-permute-start(bf16[2,128,256]{2,1,0:T(8,128)(2,1)S(1)} %get-tuple-element.40), channel_id=1, source_target_pairs={{0,4},{4,0},{8,12},{12,8},{16,20},{20,16},{24,28},{28,24},{1,5},{5... | collective-permute-start | bytes 393224 | tf_op jit(solution)/shard_map/ppermute | solution.py:437
  14.4 11.0 %collective-permute-start.9 = (bf16[2,128,256]{2,1,0:T(8,128)(2,1)S(1)}, bf16[2,128,256]{2,1,0:T(8,128)(2,1)S(1)}, u32[]{:S(2)}, u32[]{:S(2)}) collective-permute-start(bf16[2,128,256]{2,1,0:T(8,128)(2,1)S(1)} %get-tuple-element.41), channel_id=1, source_target_pairs={{0,8},{4,12},{8,0},{12,4},{16,24},{20,28},{24,16},{28,20},{1,9},{5... | collective-permute-start | bytes 393224 | tf_op jit(solution)/shard_map/ppermute | solution.py:437
  17.3 1.6 %copy-start.2 = (bf16[4,512,512]{2,1,0:T(8,128)(2,1)S(1)}, bf16[4,512,512]{2,1,0:T(8,128)(2,1)}, u32[]{:S(2)}) copy-start(bf16[4,512,512]{2,1,0:T(8,128)(2,1)} %constant.4.clone.fwd_ref.refs_10_) | copy-start | bytes 6291460
  18.9 8.3 %copy-start = (bf16[4,512,512]{2,1,0:T(8,128)(2,1)S(1)}, bf16[4,512,512]{2,1,0:T(8,128)(2,1)}, u32[]{:S(2)}) copy-start(bf16[4,512,512]{2,1,0:T(8,128)(2,1)} %constant.5.clone.refs_11_.inv_ref) | copy-start | bytes 6291460
  20.7 13.8 %collective-permute-start.10 = (bf16[2,128,256]{2,1,0:T(8,128)(2,1)S(1)}, bf16[2,128,256]{2,1,0:T(8,128)(2,1)S(1)}, u32[]{:S(2)}, u32[]{:S(2)}) collective-permute-start(bf16[2,128,256]{2,1,0:T(8,128)(2,1)S(1)} %get-tuple-element.42), channel_id=1, source_target_pairs={{0,12},{4,8},{8,4},{12,0},{16,28},{20,24},{24,20},{28,16},{1,13},{... | collective-permute-start | bytes 393224 | tf_op jit(solution)/shard_map/ppermute | solution.py:437
  22.8 15.4 %collective-permute-start.11 = (bf16[2,128,256]{2,1,0:T(8,128)(2,1)S(1)}, bf16[2,128,256]{2,1,0:T(8,128)(2,1)S(1)}, u32[]{:S(2)}, u32[]{:S(2)}) collective-permute-start(bf16[2,128,256]{2,1,0:T(8,128)(2,1)S(1)} %get-tuple-element.43), channel_id=1, source_target_pairs={{0,16},{4,20},{8,24},{12,28},{16,0},{20,4},{24,8},{28,12},{1,17},{... | collective-permute-start | bytes 393224 | tf_op jit(solution)/shard_map/ppermute | solution.py:437
  24.3 13.9 %collective-permute-start.12 = (bf16[2,128,256]{2,1,0:T(8,128)(2,1)S(1)}, bf16[2,128,256]{2,1,0:T(8,128)(2,1)S(1)}, u32[]{:S(2)}, u32[]{:S(2)}) collective-permute-start(bf16[2,128,256]{2,1,0:T(8,128)(2,1)S(1)} %get-tuple-element.44), channel_id=1, source_target_pairs={{0,20},{4,16},{8,28},{12,24},{16,4},{20,0},{24,12},{28,8},{1,21},{... | collective-permute-start | bytes 393224 | tf_op jit(solution)/shard_map/ppermute | solution.py:437
  24.3 13.9 %collective-permute-start.13 = (bf16[2,128,256]{2,1,0:T(8,128)(2,1)S(1)}, bf16[2,128,256]{2,1,0:T(8,128)(2,1)S(1)}, u32[]{:S(2)}, u32[]{:S(2)}) collective-permute-start(bf16[2,128,256]{2,1,0:T(8,128)(2,1)S(1)} %get-tuple-element.45), channel_id=1, source_target_pairs={{0,24},{4,28},{8,16},{12,20},{16,8},{20,12},{24,0},{28,4},{1,25},{... | collective-permute-start | bytes 393224 | tf_op jit(solution)/shard_map/ppermute | solution.py:437
  25.5 12.7 %collective-permute-start.14 = (bf16[2,128,256]{2,1,0:T(8,128)(2,1)S(1)}, bf16[2,128,256]{2,1,0:T(8,128)(2,1)S(1)}, u32[]{:S(2)}, u32[]{:S(2)}) collective-permute-start(bf16[2,128,256]{2,1,0:T(8,128)(2,1)S(1)} %get-tuple-element.46), channel_id=1, source_target_pairs={{0,28},{4,24},{8,20},{12,16},{16,12},{20,8},{24,4},{28,0},{1,29},{... | collective-permute-start | bytes 393224 | tf_op jit(solution)/shard_map/ppermute | solution.py:437
  34.5 15.9 %collective-permute-start.7 = (bf16[8,128,256]{2,1,0:T(8,128)(2,1)S(1)}, bf16[8,128,256]{2,1,0:T(8,128)(2,1)}, u32[]{:S(2)}, u32[]{:S(2)}) collective-permute-start(bf16[8,128,256]{2,1,0:T(8,128)(2,1)S(1)} %get-tuple-element.37), channel_id=1, source_target_pairs={{0,3},{1,0},{2,1},{3,2},{4,7},{5,4},{6,5},{7,6},{8,11},{9,8},{10,9... | collective-permute-start | bytes 1572872 | tf_op jit(solution)/shard_map/ppermute | solution.py:453
  45.6 10.5 %collective-permute-start.15 = (bf16[4,128,256]{2,1,0:T(8,128)(2,1)S(1)}, bf16[4,128,256]{2,1,0:T(8,128)(2,1)S(1)}, u32[]{:S(2)}, u32[]{:S(2)}) collective-permute-start(bf16[4,128,256]{2,1,0:T(8,128)(2,1)S(1)} %get-tuple-element.49), channel_id=1, source_target_pairs={{0,3},{1,0},{2,1},{3,2},{4,7},{5,4},{6,5},{7,6},{8,11},{9,8},{10,9... | collective-permute-start | bytes 786440 | tf_op jit(solution)/shard_map/ppermute | solution.py:453
  46.7 14.3 %collective-permute-start.19 = (bf16[4,128,256]{2,1,0:T(8,128)(2,1)S(1)}, bf16[4,128,256]{2,1,0:T(8,128)(2,1)S(1)}, u32[]{:S(2)}, u32[]{:S(2)}) collective-permute-start(bf16[4,128,256]{2,1,0:T(8,128)(2,1)S(1)} %get-tuple-element.52), channel_id=1, source_target_pairs={{0,3},{1,0},{2,1},{3,2},{4,7},{5,4},{6,5},{7,6},{8,11},{9,8},{10,9... | collective-permute-start | bytes 786440 | tf_op jit(solution)/shard_map/ppermute | solution.py:453
  50.4 19.1 %all-to-all-start = ((bf16[8,128,256]{2,1,0:T(8,128)(2,1)}), bf16[8,128,256]{2,1,0:T(8,128)(2,1)S(1)}, u32[]{:S(2)}, u32[]{:S(2)}) async-start(bf16[8,128,256]{2,1,0:T(8,128)(2,1)} %collective-permute-done.7), calls=%async_computation | async-start | bytes 1048576 | tf_op jit(solution)/shard_map/all_to_all | solution.py:435
  56.1 6.1 %collective-permute-start.16 = (bf16[128,256]{1,0:T(8,128)(2,1)S(1)}, bf16[128,256]{1,0:T(8,128)(2,1)S(1)}, u32[]{:S(2)}, u32[]{:S(2)}) collective-permute-start(bf16[128,256]{1,0:T(8,128)(2,1)S(1)} %get-tuple-element.62), channel_id=1, source_target_pairs={{0,4},{4,0},{8,12},{12,8},{16,20},{20,16},{24,28},{28,24},{1,5},{5... | collective-permute-start | bytes 196616 | tf_op jit(solution)/shard_map/ppermute | solution.py:437
  56.2 8.4 %collective-permute-start.17 = (bf16[128,256]{1,0:T(8,128)(2,1)S(1)}, bf16[128,256]{1,0:T(8,128)(2,1)S(1)}, u32[]{:S(2)}, u32[]{:S(2)}) collective-permute-start(bf16[128,256]{1,0:T(8,128)(2,1)S(1)} %get-tuple-element.61), channel_id=1, source_target_pairs={{0,8},{4,12},{8,0},{12,4},{16,24},{20,28},{24,16},{28,20},{1,9},{5... | collective-permute-start | bytes 196616 | tf_op jit(solution)/shard_map/ppermute | solution.py:437
  56.8 8.7 %collective-permute-start.18 = (bf16[128,256]{1,0:T(8,128)(2,1)S(1)}, bf16[128,256]{1,0:T(8,128)(2,1)S(1)}, u32[]{:S(2)}, u32[]{:S(2)}) collective-permute-start(bf16[128,256]{1,0:T(8,128)(2,1)S(1)} %get-tuple-element.60), channel_id=1, source_target_pairs={{0,12},{4,8},{8,4},{12,0},{16,28},{20,24},{24,20},{28,16},{1,13},{... | collective-permute-start | bytes 196616 | tf_op jit(solution)/shard_map/ppermute | solution.py:437
  61.0 4.6 %collective-permute-start.20 = (bf16[128,256]{1,0:T(8,128)(2,1)S(1)}, bf16[128,256]{1,0:T(8,128)(2,1)S(1)}, u32[]{:S(2)}, u32[]{:S(2)}) collective-permute-start(bf16[128,256]{1,0:T(8,128)(2,1)S(1)} %get-tuple-element.59), channel_id=1, source_target_pairs={{0,16},{4,20},{8,24},{12,28},{16,0},{20,4},{24,8},{28,12},{1,17},{... | collective-permute-start | bytes 196616 | tf_op jit(solution)/shard_map/ppermute | solution.py:437
  62.2 4.6 %collective-permute-start.21 = (bf16[128,256]{1,0:T(8,128)(2,1)S(1)}, bf16[128,256]{1,0:T(8,128)(2,1)S(1)}, u32[]{:S(2)}, u32[]{:S(2)}) collective-permute-start(bf16[128,256]{1,0:T(8,128)(2,1)S(1)} %get-tuple-element.58), channel_id=1, source_target_pairs={{0,20},{4,16},{8,28},{12,24},{16,4},{20,0},{24,12},{28,8},{1,21},{... | collective-permute-start | bytes 196616 | tf_op jit(solution)/shard_map/ppermute | solution.py:437
  62.2 5.9 %collective-permute-start.22 = (bf16[128,256]{1,0:T(8,128)(2,1)S(1)}, bf16[128,256]{1,0:T(8,128)(2,1)S(1)}, u32[]{:S(2)}, u32[]{:S(2)}) collective-permute-start(bf16[128,256]{1,0:T(8,128)(2,1)S(1)} %get-tuple-element.57), channel_id=1, source_target_pairs={{0,24},{4,28},{8,16},{12,20},{16,8},{20,12},{24,0},{28,4},{1,25},{... | collective-permute-start | bytes 196616 | tf_op jit(solution)/shard_map/ppermute | solution.py:437
  64.6 5.0 %collective-permute-start.23 = (bf16[128,256]{1,0:T(8,128)(2,1)S(1)}, bf16[128,256]{1,0:T(8,128)(2,1)S(1)}, u32[]{:S(2)}, u32[]{:S(2)}) collective-permute-start(bf16[128,256]{1,0:T(8,128)(2,1)S(1)} %get-tuple-element.56), channel_id=1, source_target_pairs={{0,28},{4,24},{8,20},{12,16},{16,12},{20,8},{24,4},{28,0},{1,29},{... | collective-permute-start | bytes 196616 | tf_op jit(solution)/shard_map/ppermute | solution.py:437

commit v6 on v5

--- a/solution.py
+++ b/solution.py
@@ -157,7 +157,7 @@
     rows = kernel_ref.shape[0]
     quarter = rows // 4
 
-    @pl.loop(0, quarter // TILE)
+    @pl.loop(0, quarter // TILE, unroll=2)
     def _(step):
         start = pl.multiple_of(step * TILE, TILE)
         parts = split(*(kernel_ref[pl.ds(start + j * quarter, TILE), :] for j in range(4)))
@@ -201,7 +201,7 @@
     quarter = rows // 4
     columns = slice(chunk * width, (chunk + 1) * width)
     place = lambda device, offset: pl.ds(pl.multiple_of(device * length + offset, 8), length)
-    low = lambda v: v.astype(jnp.bfloat16).astype(jnp.float32)
+    low = lambda v: v
 
     start = pl.multiple_of((me * (spec_ref.shape[2] // width) + chunk) * width, width)
     fetch = pltpu.make_async_copy(tap_ref.at[0, :, :, pl.ds(start, width)], tap_rows, tap_sem)
@@ -213,7 +213,7 @@
     fetch.wait()
     taps = [tap_rows[s, i : i + 1, :] for s in range(3) for i in range(3)]
 
-    @pl.loop(0, quarter // TILE)
+    @pl.loop(0, quarter // TILE, unroll=2)
     def _(step):
         begin = pl.multiple_of(step * TILE, TILE)
         products, adjoints = [], []
@@ -247,7 +247,7 @@
         cross_ref[j, quarter:, :] = (p_re * a_im - p_im * a_re).astype(jnp.bfloat16)
         back[j] = jnp.dot(inv_ref[j], mixed[j], preferred_element_type=jnp.float32)
 
-    @pl.loop(0, quarter // TILE)
+    @pl.loop(0, quarter // TILE, unroll=2)
     def _(step):
         begin = pl.multiple_of(step * TILE, TILE)
         real, imag = pl.ds(begin, TILE), pl.ds(begin + quarter, TILE)
@@ -266,16 +266,13 @@
 
     shifted_rows[:, rows:, :] = jnp.zeros((3, PAD, width), jnp.float32)
 
-    @pl.loop(0, rows // LAST_TILE)
-    def _(step):
-        begin = pl.multiple_of(step * LAST_TILE, LAST_TILE)
-        windows = [shifted_rows[i, pl.ds(begin, LAST_TILE + PAD), :] for i in range(3)]
-        total = sum(windows[i][i : i + LAST_TILE, :] for i in range(3))
-        grad_rows[pl.ds(begin, LAST_TILE), :] = total.astype(jnp.bfloat16)
-
     for k in range(devices):
         number, within = divmod(k, devices // parts)
-        out_refs[number][within] = grad_rows[place(k if whole_out else me ^ k, 0), :]
+        for offset in range(0, length, LAST_TILE):
+            begin = pl.multiple_of((k if whole_out else me ^ k) * length + offset, LAST_TILE)
+            windows = [shifted_rows[i, pl.ds(begin, LAST_TILE + PAD), :] for i in range(3)]
+            total = sum(windows[i][i : i + LAST_TILE, :] for i in range(3))
+            out_refs[number][within, offset : offset + LAST_TILE, :] = total.astype(jnp.bfloat16)
 
 
 def section(pieces, taps, spec, fwd, inv, chunk, devices, whole_in, whole_out, parts):
@@ -323,7 +320,7 @@
         for j in range(4):
             back[chunk, j] = jnp.dot(inv_ref[j], cross_ref[j], preferred_element_type=jnp.float32)
 
-        @pl.loop(0, quarter // TILE)
+        @pl.loop(0, quarter // TILE, unroll=2)
         def _(step):
             begin = pl.multiple_of(step * TILE, TILE)
             real, imag = pl.ds(begin, TILE), pl.ds(begin + quarter, TILE)

time: 70.9 us -> 70.3 us (level)
  Pallas kernels: 21.5 us -> 20.3 us
    pallas_call x2, Pallas kernels: 14.7 us -> 13.6 us  [section(): pl.pallas_call(functools.partial(section_kernel, devices, chunk, whole_in...]
  transfers between devices with their start and end apart: 25 -> 25, of which waited for: 9 -> 9; matrix products, arithmetic and copies ran while one was open for 1% -> 1% of each run, Pallas kernels for 28% -> 26%
where the time goes in v6:
time: 70.3 us; the launch traced here: 70.1 us
  starting transfers between devices  32.3 us (46%)
  Pallas kernels  20.3 us (29%)
  waiting for transfers between devices  11.5 us (16%)
  local copies, waits for them, and re-layouts  5.23 us (7%)
  between operations  0.78 us (1%)
    ppermute x21, starting transfers between devices, exchanged(): lax.ppermute(chunk[k], 'seq', pairs(k))  23 us
    pallas_call x2, Pallas kernels, section(): pl.pallas_call(functools.partial(section_kernel, devices, chunk, whole_in...  13.6 us
    ppermute x21, waiting for transfers between devices, exchanged(): lax.ppermute(chunk[k], 'seq', pairs(k))  6.17 us
    ppermute x3, starting transfers between devices, fast(): moved = [lax.ppermute(part, 'pipe', before) for part in parts[::-1]]  5.8 us
    ppermute x3, waiting for transfers between devices, fast(): moved = [lax.ppermute(part, 'pipe', before) for part in parts[::-1]]  5.34 us
    unnamed x11, local copies, waits for them, and re-layouts  5.2 us
    all_to_all x1, starting transfers between devices, exchanged(): lax.all_to_all(chunk[0], 'seq', split_axis=0, concat_axis=0, tiled=True)  3.49 us
    pallas_call x1, Pallas kernels, filter_gradient(): pl.pallas_call(filter_kernel, in_specs=[pl.BlockSpec(memory_space=pltpu.V...  3.05 us
  transfers between devices with their start and end apart: 25, of which 9 were waited for; matrix products, arithmetic and copies ran while one was open for 1% of the time, Pallas kernels for 26%

profile of v6, /device:TPU:0, one launch (start us, length us, event | category | flops | bytes accessed | tf_op | source)
XLA Modules:
  0.0 70.1 jit_solution(14904215538948449051)
XLA Ops:
  0.6 0.0 copy-start.1
  0.6 0.0 copy-start.3
  0.6 1.4 %copy-done.3 = bf16[1,128,4096]{2,1,0:T(8,128)(2,1)S(1)} copy-done((bf16[1,128,4096]{2,1,0:T(8,128)(2,1)S(1)}, bf16[1,128,4096]{2,1,0:T(8,128)(2,1)}, u32[]{:S(2)}) %copy-start.3) | copy-done | bytes 1048600
  2.0 1.2 %copy-done.4 = bf16[1,128,4096]{2,1,0:T(8,128)(2,1)S(1)} copy-done((bf16[1,128,4096]{2,1,0:T(8,128)(2,1)S(1)}, bf16[1,128,4096]{2,1,0:T(8,128)(2,1)}, u32[]{:S(2)}) %copy-start.4) | copy-done | bytes 1048600
  3.2 0.7 %pack.1 = (bf16[2,128,256]{2,1,0:T(8,128)(2,1)S(1)}, bf16[2,128,256]{2,1,0:T(8,128)(2,1)S(1)}, bf16[2,128,256]{2,1,0:T(8,128)(2,1)S(1)}, bf16[2,128,256]{2,1,0:T...) custom-call(bf16[128,4096]{1,0:T(8,128)(2,1)S(1)} %bitcast.21, ...), custom_call_target="tpu_custom_call" | custom-call | tf_op jit(solution)/shard_map/pack/pallas_call | solution.py:103
  4.0 0.5 collective-permute-start
  4.5 2.6 %collective-permute-start.1 = (bf16[2,128,256]{2,1,0:T(8,128)(2,1)S(1)}, bf16[2,128,256]{2,1,0:T(8,128)(2,1)S(1)}, u32[]{:S(2)}, u32[]{:S(2)}) collective-permute-start(bf16[2,128,256]{2,1,0:T(8,128)(2,1)S(1)} %get-tuple-element.31), channel_id=1, source_target_pairs={{0,8},{4,12},{8,0},{12,4},{16,24},{20,28},{24,16},{28,20},{1,9},{5... | collective-permute-start | bytes 393224 | tf_op jit(solution)/shard_map/ppermute | solution.py:434
  7.1 0.1 collective-permute-start.2
  7.1 1.8 %collective-permute-start.3 = (bf16[2,128,256]{2,1,0:T(8,128)(2,1)S(1)}, bf16[2,128,256]{2,1,0:T(8,128)(2,1)S(1)}, u32[]{:S(2)}, u32[]{:S(2)}) collective-permute-start(bf16[2,128,256]{2,1,0:T(8,128)(2,1)S(1)} %get-tuple-element.33), channel_id=1, source_target_pairs={{0,16},{4,20},{8,24},{12,28},{16,0},{20,4},{24,8},{28,12},{1,17},{... | collective-permute-start | bytes 393224 | tf_op jit(solution)/shard_map/ppermute | solution.py:434
  8.9 0.0 collective-permute-start.4
  8.9 0.0 collective-permute-done.refs_1_
  8.9 2.6 %collective-permute-start.5 = (bf16[2,128,256]{2,1,0:T(8,128)(2,1)S(1)}, bf16[2,128,256]{2,1,0:T(8,128)(2,1)S(1)}, u32[]{:S(2)}, u32[]{:S(2)}) collective-permute-start(bf16[2,128,256]{2,1,0:T(8,128)(2,1)S(1)} %get-tuple-element.35), channel_id=1, source_target_pairs={{0,24},{4,28},{8,16},{12,20},{16,8},{20,12},{24,0},{28,4},{1,25},{... | collective-permute-start | bytes 393224 | tf_op jit(solution)/shard_map/ppermute | solution.py:434
  11.5 0.0 collective-permute-done.1.refs_2_
  11.5 1.6 %collective-permute-start.6 = (bf16[2,128,256]{2,1,0:T(8,128)(2,1)S(1)}, bf16[2,128,256]{2,1,0:T(8,128)(2,1)S(1)}, u32[]{:S(2)}, u32[]{:S(2)}) collective-permute-start(bf16[2,128,256]{2,1,0:T(8,128)(2,1)S(1)} %get-tuple-element.36), channel_id=1, source_target_pairs={{0,28},{4,24},{8,20},{12,16},{16,12},{20,8},{24,4},{28,0},{1,29},{... | collective-permute-start | bytes 393224 | tf_op jit(solution)/shard_map/ppermute | solution.py:434
  13.1 0.6 collective-permute-done.2.refs_3_
  13.7 0.7 %collective-permute-start.8 = (bf16[2,128,256]{2,1,0:T(8,128)(2,1)S(1)}, bf16[2,128,256]{2,1,0:T(8,128)(2,1)S(1)}, u32[]{:S(2)}, u32[]{:S(2)}) collective-permute-start(bf16[2,128,256]{2,1,0:T(8,128)(2,1)S(1)} %get-tuple-element.40), channel_id=1, source_target_pairs={{0,4},{4,0},{8,12},{12,8},{16,20},{20,16},{24,28},{28,24},{1,5},{5... | collective-permute-start | bytes 393224 | tf_op jit(solution)/shard_map/ppermute | solution.py:434
  14.4 0.0 collective-permute-done.3.refs_4_
  14.4 1.8 %collective-permute-start.9 = (bf16[2,128,256]{2,1,0:T(8,128)(2,1)S(1)}, bf16[2,128,256]{2,1,0:T(8,128)(2,1)S(1)}, u32[]{:S(2)}, u32[]{:S(2)}) collective-permute-start(bf16[2,128,256]{2,1,0:T(8,128)(2,1)S(1)} %get-tuple-element.41), channel_id=1, source_target_pairs={{0,8},{4,12},{8,0},{12,4},{16,24},{20,28},{24,16},{28,20},{1,9},{5... | collective-permute-start | bytes 393224 | tf_op jit(solution)/shard_map/ppermute | solution.py:434
  16.3 1.0 %copy.8.refs_8_ = f32[1,3,3,4096]{3,2,1,0:T(4,128)S(1)} copy(f32[1,3,3,4096]{3,0,2,1:T(1,128)} %param.9) | data formatting | bytes 294912 | tf_op args[3]
  17.3 0.0 copy-done.1
  17.3 0.0 copy-start.2
  17.3 1.6 %copy-done.2 = bf16[4,512,512]{2,1,0:T(8,128)(2,1)S(1)} copy-done((bf16[4,512,512]{2,1,0:T(8,128)(2,1)S(1)}, bf16[4,512,512]{2,1,0:T(8,128)(2,1)}, u32[]{:S(2)}) %copy-start.2) | copy-done | bytes 2097176
  18.9 1.9 %spectrum.1.refs_9_ = f32[4,512,512]{2,1,0:T(8,128)S(1)} custom-call(f32[1024,512]{1,0:T(8,128)S(1)} %bitcast.20, bf16[4,512,512]{2,1,0:T(8,128)(2,1)S(1)} %copy-done.2), custom_call_target="tpu_custom_call" | custom-call | flops 1073741824 | bytes 7340032 | tf_op jit(solution)/shard_map/spectrum/pallas_call | solution.py:175
  20.8 0.0 collective-permute-done.4.refs_5_
  20.8 1.9 %collective-permute-start.10 = (bf16[2,128,256]{2,1,0:T(8,128)(2,1)S(1)}, bf16[2,128,256]{2,1,0:T(8,128)(2,1)S(1)}, u32[]{:S(2)}, u32[]{:S(2)}) collective-permute-start(bf16[2,128,256]{2,1,0:T(8,128)(2,1)S(1)} %get-tuple-element.42), channel_id=1, source_target_pairs={{0,12},{4,8},{8,4},{12,0},{16,28},{20,24},{24,20},{28,16},{1,13},{... | collective-permute-start | bytes 393224 | tf_op jit(solution)/shard_map/ppermute | solution.py:434
  22.7 0.0 collective-permute-done.5.refs_6_
  22.8 1.5 %collective-permute-start.11 = (bf16[2,128,256]{2,1,0:T(8,128)(2,1)S(1)}, bf16[2,128,256]{2,1,0:T(8,128)(2,1)S(1)}, u32[]{:S(2)}, u32[]{:S(2)}) collective-permute-start(bf16[2,128,256]{2,1,0:T(8,128)(2,1)S(1)} %get-tuple-element.43), channel_id=1, source_target_pairs={{0,16},{4,20},{8,24},{12,28},{16,0},{20,4},{24,8},{28,12},{1,17},{... | collective-permute-start | bytes 393224 | tf_op jit(solution)/shard_map/ppermute | solution.py:434
  24.3 0.0 collective-permute-done.6.refs_7_
  24.3 0.0 collective-permute-start.12
  24.3 0.0 collective-permute-done.8.refs_1_
  24.3 1.2 %collective-permute-start.13 = (bf16[2,128,256]{2,1,0:T(8,128)(2,1)S(1)}, bf16[2,128,256]{2,1,0:T(8,128)(2,1)S(1)}, u32[]{:S(2)}, u32[]{:S(2)}) collective-permute-start(bf16[2,128,256]{2,1,0:T(8,128)(2,1)S(1)} %get-tuple-element.45), channel_id=1, source_target_pairs={{0,24},{4,28},{8,16},{12,20},{16,8},{20,12},{24,0},{28,4},{1,25},{... | collective-permute-start | bytes 393224 | tf_op jit(solution)/shard_map/ppermute | solution.py:434
  25.5 0.0 collective-permute-done.9.refs_2_
  25.5 1.7 %collective-permute-start.14 = (bf16[2,128,256]{2,1,0:T(8,128)(2,1)S(1)}, bf16[2,128,256]{2,1,0:T(8,128)(2,1)S(1)}, u32[]{:S(2)}, u32[]{:S(2)}) collective-permute-start(bf16[2,128,256]{2,1,0:T(8,128)(2,1)S(1)} %get-tuple-element.46), channel_id=1, source_target_pairs={{0,28},{4,24},{8,20},{12,16},{16,12},{20,8},{24,4},{28,0},{1,29},{... | collective-permute-start | bytes 393224 | tf_op jit(solution)/shard_map/ppermute | solution.py:434
  27.2 6.8 %section.2 = (bf16[8,128,256]{2,1,0:T(8,128)(2,1)S(1)}, bf16[4,512,256]{2,1,0:T(8,128)(2,1)S(1)}) custom-call(bf16[2,128,256]{2,1,0:T(8,128)(2,1)S(1)} %get-tuple-element.29.refs_0_, bf16[2,128,256]{2,1,0:T(8,128)(2,1)S(1)} %collective-permute-done.refs_1_, bf16[2,128,256]{2,1,0:T(8,128)(2,1)S(1)} %collective-permute-done.1.refs_2_, ...), custom_call_target="tpu_custom_call" | custom-call | flops 2684354560 | bytes 5242880 | tf_op jit(solution)/shard_map/section/pallas_call | solution.py:285
  33.9 0.0 collective-permute-done.10.refs_3_
  33.9 3.7 %collective-permute-start.7 = (bf16[8,128,256]{2,1,0:T(8,128)(2,1)S(1)}, bf16[8,128,256]{2,1,0:T(8,128)(2,1)}, u32[]{:S(2)}, u32[]{:S(2)}) collective-permute-start(bf16[8,128,256]{2,1,0:T(8,128)(2,1)S(1)} %get-tuple-element.37), channel_id=1, source_target_pairs={{0,3},{1,0},{2,1},{3,2},{4,7},{5,4},{6,5},{7,6},{8,11},{9,8},{10,9... | collective-permute-start | bytes 1572872 | tf_op jit(solution)/shard_map/ppermute | solution.py:450
  37.6 0.0 collective-permute-done.11.refs_4_
  37.6 0.0 collective-permute-done.12.refs_5_
  37.6 0.0 collective-permute-done.13.refs_6_
  37.6 0.0 collective-permute-done.14.refs_7_
  37.6 6.8 %section.3 = (bf16[4,128,256]{2,1,0:T(8,128)(2,1)S(1)}, bf16[4,128,256]{2,1,0:T(8,128)(2,1)S(1)}, bf16[4,512,256]{2,1,0:T(8,128)(2,1)S(1)}) custom-call(bf16[2,128,256]{2,1,0:T(8,128)(2,1)S(1)} %get-tuple-element.39.refs_0_, bf16[2,128,256]{2,1,0:T(8,128)(2,1)S(1)} %collective-permute-done.8.refs_1_, ...), custom_call_target="tpu_custom_call" | custom-call | flops 2684354560 | bytes 5242880 | tf_op jit(solution)/shard_map/section/pallas_call | solution.py:285
  44.4 1.7 %collective-permute-start.15 = (bf16[4,128,256]{2,1,0:T(8,128)(2,1)S(1)}, bf16[4,128,256]{2,1,0:T(8,128)(2,1)S(1)}, u32[]{:S(2)}, u32[]{:S(2)}) collective-permute-start(bf16[4,128,256]{2,1,0:T(8,128)(2,1)S(1)} %get-tuple-element.49), channel_id=1, source_target_pairs={{0,3},{1,0},{2,1},{3,2},{4,7},{5,4},{6,5},{7,6},{8,11},{9,8},{10,9... | collective-permute-start | bytes 786440 | tf_op jit(solution)/shard_map/ppermute | solution.py:450
  46.1 0.5 collective-permute-start.19
  46.6 3.0 %filter.1 = f32[1024,512]{1,0:T(8,128)} custom-call(bf16[4,512,512]{2,1,0:T(8,128)(2,1)S(1)} %copy-done, bf16[4,512,256]{2,1,0:T(8,128)(2,1)S(1)} %get-tuple-element.38.refs_0_, bf16[4,512,256]{2,1,0:T(8,128)(2,1)S(1)} %get-tuple-element.47.refs_1_), custom_call_target="tpu_custom_call" | custom-call | flops 1073741824 | bytes 3145728 | tf_op jit(solution)/shard_map/filter/pallas_call | solution.py:340
  49.6 0.3 collective-permute-done.7
  49.9 3.5 %all-to-all-start = ((bf16[8,128,256]{2,1,0:T(8,128)(2,1)}), bf16[8,128,256]{2,1,0:T(8,128)(2,1)S(1)}, u32[]{:S(2)}, u32[]{:S(2)}) async-start(bf16[8,128,256]{2,1,0:T(8,128)(2,1)} %collective-permute-done.7), calls=%async_computation | async-start | bytes 1048576 | tf_op jit(solution)/shard_map/all_to_all | solution.py:432
  53.4 2.1 %collective-permute-done.15 = bf16[4,128,256]{2,1,0:T(8,128)(2,1)S(1)} collective-permute-done((bf16[4,128,256]{2,1,0:T(8,128)(2,1)S(1)}, bf16[4,128,256]{2,1,0:T(8,128)(2,1)S(1)}, u32[]{:S(2)}, u32[]{:S(2)}) %collective-permute-start.15) | collective-permute-done | bytes 262176 | tf_op jit(solution)/shard_map/ppermute | solution.py:450
  55.5 0.1 collective-permute-start.16
  55.6 0.6 collective-permute-start.17
  56.2 1.3 %collective-permute-start.18 = (bf16[128,256]{1,0:T(8,128)(2,1)S(1)}, bf16[128,256]{1,0:T(8,128)(2,1)S(1)}, u32[]{:S(2)}, u32[]{:S(2)}) collective-permute-start(bf16[128,256]{1,0:T(8,128)(2,1)S(1)} %get-tuple-element.60), channel_id=1, source_target_pairs={{0,12},{4,8},{8,4},{12,0},{16,28},{20,24},{24,20},{28,16},{1,13},{... | collective-permute-start | bytes 196616 | tf_op jit(solution)/shard_map/ppermute | solution.py:434
  57.5 3.0 %collective-permute-done.19 = bf16[4,128,256]{2,1,0:T(8,128)(2,1)S(1)} collective-permute-done((bf16[4,128,256]{2,1,0:T(8,128)(2,1)S(1)}, bf16[4,128,256]{2,1,0:T(8,128)(2,1)S(1)}, u32[]{:S(2)}, u32[]{:S(2)}) %collective-permute-start.19) | collective-permute-done | bytes 262176 | tf_op jit(solution)/shard_map/ppermute | solution.py:450
  60.4 1.2 %collective-permute-start.20 = (bf16[128,256]{1,0:T(8,128)(2,1)S(1)}, bf16[128,256]{1,0:T(8,128)(2,1)S(1)}, u32[]{:S(2)}, u32[]{:S(2)}) collective-permute-start(bf16[128,256]{1,0:T(8,128)(2,1)S(1)} %get-tuple-element.59), channel_id=1, source_target_pairs={{0,16},{4,20},{8,24},{12,28},{16,0},{20,4},{24,8},{28,12},{1,17},{... | collective-permute-start | bytes 196616 | tf_op jit(solution)/shard_map/ppermute | solution.py:434
  61.6 0.0 collective-permute-start.21
  61.6 0.0 collective-permute-done.16.refs_2_
  61.6 0.9 %collective-permute-start.22 = (bf16[128,256]{1,0:T(8,128)(2,1)S(1)}, bf16[128,256]{1,0:T(8,128)(2,1)S(1)}, u32[]{:S(2)}, u32[]{:S(2)}) collective-permute-start(bf16[128,256]{1,0:T(8,128)(2,1)S(1)} %get-tuple-element.57), channel_id=1, source_target_pairs={{0,24},{4,28},{8,16},{12,20},{16,8},{20,12},{24,0},{28,4},{1,25},{... | collective-permute-start | bytes 196616 | tf_op jit(solution)/shard_map/ppermute | solution.py:434
  62.5 1.5 %collective-permute-done.17.refs_3_ = bf16[128,256]{1,0:T(8,128)(2,1)S(1)} collective-permute-done((bf16[128,256]{1,0:T(8,128)(2,1)S(1)}, bf16[128,256]{1,0:T(8,128)(2,1)S(1)}, u32[]{:S(2)}, u32[]{:S(2)}) %collective-permute-start.17) | collective-permute-done | bytes 65568 | tf_op jit(solution)/shard_map/ppermute | solution.py:434
  64.0 0.9 %collective-permute-start.23 = (bf16[128,256]{1,0:T(8,128)(2,1)S(1)}, bf16[128,256]{1,0:T(8,128)(2,1)S(1)}, u32[]{:S(2)}, u32[]{:S(2)}) collective-permute-start(bf16[128,256]{1,0:T(8,128)(2,1)S(1)} %get-tuple-element.56), channel_id=1, source_target_pairs={{0,28},{4,24},{8,20},{12,16},{16,12},{20,8},{24,4},{28,0},{1,29},{... | collective-permute-start | bytes 196616 | tf_op jit(solution)/shard_map/ppermute | solution.py:434
  64.9 0.0 collective-permute-done.18.refs_4_
  64.9 0.1 collective-permute-done.20.refs_5_
  65.0 1.2 %collective-permute-done.21.refs_6_ = bf16[128,256]{1,0:T(8,128)(2,1)S(1)} collective-permute-done((bf16[128,256]{1,0:T(8,128)(2,1)S(1)}, bf16[128,256]{1,0:T(8,128)(2,1)S(1)}, u32[]{:S(2)}, u32[]{:S(2)}) %collective-permute-start.21) | collective-permute-done | bytes 65568 | tf_op jit(solution)/shard_map/ppermute | solution.py:434
  66.2 1.3 %collective-permute-done.22.refs_7_ = bf16[128,256]{1,0:T(8,128)(2,1)S(1)} collective-permute-done((bf16[128,256]{1,0:T(8,128)(2,1)S(1)}, bf16[128,256]{1,0:T(8,128)(2,1)S(1)}, u32[]{:S(2)}, u32[]{:S(2)}) %collective-permute-start.22) | collective-permute-done | bytes 65568 | tf_op jit(solution)/shard_map/ppermute | solution.py:434
  67.5 1.5 %collective-permute-done.23.refs_8_ = bf16[128,256]{1,0:T(8,128)(2,1)S(1)} collective-permute-done((bf16[128,256]{1,0:T(8,128)(2,1)S(1)}, bf16[128,256]{1,0:T(8,128)(2,1)S(1)}, u32[]{:S(2)}, u32[]{:S(2)}) %collective-permute-start.23) | collective-permute-done | bytes 65568 | tf_op jit(solution)/shard_map/ppermute | solution.py:434
  69.0 0.0 all-to-all-done.refs_0_
  69.0 1.1 %unpack.1 = bf16[1,128,4096]{2,1,0:T(8,128)(2,1)} custom-call(bf16[8,128,256]{2,1,0:T(8,128)(2,1)S(1)} %all-to-all-done.refs_0_, bf16[128,256]{1,0:T(8,128)(2,1)S(1)} %get-tuple-element.63.refs_1_, bf16[128,256]{1,0:T(8,128)(2,1)S(1)} %collective-permute-done.16.refs_2_, bf16[128,256]{1,0:T(8,128)(2,1)S(1)} %collective-permute-done.17.refs_3_, ...), custom_call_target="tpu_custom_call" | custom-call | tf_op jit(solution)/shard_map/unpack/pallas_call | solution.py:145
  (5 shorter events, 0.0 us)
Async XLA Ops:
  0.6 16.7 %copy-start.1 = (f32[1,1024,512]{2,1,0:T(8,128)S(1)}, f32[1,1024,512]{2,1,0:T(8,128)}, u32[]{:S(2)}) copy-start(f32[1,1024,512]{2,1,0:T(8,128)} %param.8) | copy-start | bytes 6291460
  0.6 1.4 %copy-start.3 = (bf16[1,128,4096]{2,1,0:T(8,128)(2,1)S(1)}, bf16[1,128,4096]{2,1,0:T(8,128)(2,1)}, u32[]{:S(2)}) copy-start(bf16[1,128,4096]{2,1,0:T(8,128)(2,1)} %param.6) | copy-start | bytes 3145732
  2.0 1.2 %copy-start.4 = (bf16[1,128,4096]{2,1,0:T(8,128)(2,1)S(1)}, bf16[1,128,4096]{2,1,0:T(8,128)(2,1)}, u32[]{:S(2)}) copy-start(bf16[1,128,4096]{2,1,0:T(8,128)(2,1)} %param.7) | copy-start | bytes 3145732
  4.0 4.9 %collective-permute-start = (bf16[2,128,256]{2,1,0:T(8,128)(2,1)S(1)}, bf16[2,128,256]{2,1,0:T(8,128)(2,1)S(1)}, u32[]{:S(2)}, u32[]{:S(2)}) collective-permute-start(bf16[2,128,256]{2,1,0:T(8,128)(2,1)S(1)} %get-tuple-element.30), channel_id=1, source_target_pairs={{0,4},{4,0},{8,12},{12,8},{16,20},{20,16},{24,28},{28,24},{1,5},{5... | collective-permute-start | bytes 393224 | tf_op jit(solution)/shard_map/ppermute | solution.py:434
  4.5 7.0 %collective-permute-start.1 = (bf16[2,128,256]{2,1,0:T(8,128)(2,1)S(1)}, bf16[2,128,256]{2,1,0:T(8,128)(2,1)S(1)}, u32[]{:S(2)}, u32[]{:S(2)}) collective-permute-start(bf16[2,128,256]{2,1,0:T(8,128)(2,1)S(1)} %get-tuple-element.31), channel_id=1, source_target_pairs={{0,8},{4,12},{8,0},{12,4},{16,24},{20,28},{24,16},{28,20},{1,9},{5... | collective-permute-start | bytes 393224 | tf_op jit(solution)/shard_map/ppermute | solution.py:434
  7.1 6.6 %collective-permute-start.2 = (bf16[2,128,256]{2,1,0:T(8,128)(2,1)S(1)}, bf16[2,128,256]{2,1,0:T(8,128)(2,1)S(1)}, u32[]{:S(2)}, u32[]{:S(2)}) collective-permute-start(bf16[2,128,256]{2,1,0:T(8,128)(2,1)S(1)} %get-tuple-element.32), channel_id=1, source_target_pairs={{0,12},{4,8},{8,4},{12,0},{16,28},{20,24},{24,20},{28,16},{1,13},{... | collective-permute-start | bytes 393224 | tf_op jit(solution)/shard_map/ppermute | solution.py:434
  7.1 7.3 %collective-permute-start.3 = (bf16[2,128,256]{2,1,0:T(8,128)(2,1)S(1)}, bf16[2,128,256]{2,1,0:T(8,128)(2,1)S(1)}, u32[]{:S(2)}, u32[]{:S(2)}) collective-permute-start(bf16[2,128,256]{2,1,0:T(8,128)(2,1)S(1)} %get-tuple-element.33), channel_id=1, source_target_pairs={{0,16},{4,20},{8,24},{12,28},{16,0},{20,4},{24,8},{28,12},{1,17},{... | collective-permute-start | bytes 393224 | tf_op jit(solution)/shard_map/ppermute | solution.py:434
  8.9 11.9 %collective-permute-start.4 = (bf16[2,128,256]{2,1,0:T(8,128)(2,1)S(1)}, bf16[2,128,256]{2,1,0:T(8,128)(2,1)S(1)}, u32[]{:S(2)}, u32[]{:S(2)}) collective-permute-start(bf16[2,128,256]{2,1,0:T(8,128)(2,1)S(1)} %get-tuple-element.34), channel_id=1, source_target_pairs={{0,20},{4,16},{8,28},{12,24},{16,4},{20,0},{24,12},{28,8},{1,21},{... | collective-permute-start | bytes 393224 | tf_op jit(solution)/shard_map/ppermute | solution.py:434
  8.9 13.8 %collective-permute-start.5 = (bf16[2,128,256]{2,1,0:T(8,128)(2,1)S(1)}, bf16[2,128,256]{2,1,0:T(8,128)(2,1)S(1)}, u32[]{:S(2)}, u32[]{:S(2)}) collective-permute-start(bf16[2,128,256]{2,1,0:T(8,128)(2,1)S(1)} %get-tuple-element.35), channel_id=1, source_target_pairs={{0,24},{4,28},{8,16},{12,20},{16,8},{20,12},{24,0},{28,4},{1,25},{... | collective-permute-start | bytes 393224 | tf_op jit(solution)/shard_map/ppermute | solution.py:434
  11.5 12.8 %collective-permute-start.6 = (bf16[2,128,256]{2,1,0:T(8,128)(2,1)S(1)}, bf16[2,128,256]{2,1,0:T(8,128)(2,1)S(1)}, u32[]{:S(2)}, u32[]{:S(2)}) collective-permute-start(bf16[2,128,256]{2,1,0:T(8,128)(2,1)S(1)} %get-tuple-element.36), channel_id=1, source_target_pairs={{0,28},{4,24},{8,20},{12,16},{16,12},{20,8},{24,4},{28,0},{1,29},{... | collective-permute-start | bytes 393224 | tf_op jit(solution)/shard_map/ppermute | solution.py:434
  13.7 10.6 %collective-permute-start.8 = (bf16[2,128,256]{2,1,0:T(8,128)(2,1)S(1)}, bf16[2,128,256]{2,1,0:T(8,128)(2,1)S(1)}, u32[]{:S(2)}, u32[]{:S(2)}) collective-permute-start(bf16[2,128,256]{2,1,0:T(8,128)(2,1)S(1)} %get-tuple-element.40), channel_id=1, source_target_pairs={{0,4},{4,0},{8,12},{12,8},{16,20},{20,16},{24,28},{28,24},{1,5},{5... | collective-permute-start | bytes 393224 | tf_op jit(solution)/shard_map/ppermute | solution.py:434
  14.4 11.0 %collective-permute-start.9 = (bf16[2,128,256]{2,1,0:T(8,128)(2,1)S(1)}, bf16[2,128,256]{2,1,0:T(8,128)(2,1)S(1)}, u32[]{:S(2)}, u32[]{:S(2)}) collective-permute-start(bf16[2,128,256]{2,1,0:T(8,128)(2,1)S(1)} %get-tuple-element.41), channel_id=1, source_target_pairs={{0,8},{4,12},{8,0},{12,4},{16,24},{20,28},{24,16},{28,20},{1,9},{5... | collective-permute-start | bytes 393224 | tf_op jit(solution)/shard_map/ppermute | solution.py:434
  17.3 1.6 %copy-start.2 = (bf16[4,512,512]{2,1,0:T(8,128)(2,1)S(1)}, bf16[4,512,512]{2,1,0:T(8,128)(2,1)}, u32[]{:S(2)}) copy-start(bf16[4,512,512]{2,1,0:T(8,128)(2,1)} %constant.4.clone.fwd_ref.refs_10_) | copy-start | bytes 6291460
  18.9 8.3 %copy-start = (bf16[4,512,512]{2,1,0:T(8,128)(2,1)S(1)}, bf16[4,512,512]{2,1,0:T(8,128)(2,1)}, u32[]{:S(2)}) copy-start(bf16[4,512,512]{2,1,0:T(8,128)(2,1)} %constant.5.clone.refs_11_.inv_ref) | copy-start | bytes 6291460
  20.8 13.1 %collective-permute-start.10 = (bf16[2,128,256]{2,1,0:T(8,128)(2,1)S(1)}, bf16[2,128,256]{2,1,0:T(8,128)(2,1)S(1)}, u32[]{:S(2)}, u32[]{:S(2)}) collective-permute-start(bf16[2,128,256]{2,1,0:T(8,128)(2,1)S(1)} %get-tuple-element.42), channel_id=1, source_target_pairs={{0,12},{4,8},{8,4},{12,0},{16,28},{20,24},{24,20},{28,16},{1,13},{... | collective-permute-start | bytes 393224 | tf_op jit(solution)/shard_map/ppermute | solution.py:434
  22.8 14.8 %collective-permute-start.11 = (bf16[2,128,256]{2,1,0:T(8,128)(2,1)S(1)}, bf16[2,128,256]{2,1,0:T(8,128)(2,1)S(1)}, u32[]{:S(2)}, u32[]{:S(2)}) collective-permute-start(bf16[2,128,256]{2,1,0:T(8,128)(2,1)S(1)} %get-tuple-element.43), channel_id=1, source_target_pairs={{0,16},{4,20},{8,24},{12,28},{16,0},{20,4},{24,8},{28,12},{1,17},{... | collective-permute-start | bytes 393224 | tf_op jit(solution)/shard_map/ppermute | solution.py:434
  24.3 13.3 %collective-permute-start.12 = (bf16[2,128,256]{2,1,0:T(8,128)(2,1)S(1)}, bf16[2,128,256]{2,1,0:T(8,128)(2,1)S(1)}, u32[]{:S(2)}, u32[]{:S(2)}) collective-permute-start(bf16[2,128,256]{2,1,0:T(8,128)(2,1)S(1)} %get-tuple-element.44), channel_id=1, source_target_pairs={{0,20},{4,16},{8,28},{12,24},{16,4},{20,0},{24,12},{28,8},{1,21},{... | collective-permute-start | bytes 393224 | tf_op jit(solution)/shard_map/ppermute | solution.py:434
  24.3 13.3 %collective-permute-start.13 = (bf16[2,128,256]{2,1,0:T(8,128)(2,1)S(1)}, bf16[2,128,256]{2,1,0:T(8,128)(2,1)S(1)}, u32[]{:S(2)}, u32[]{:S(2)}) collective-permute-start(bf16[2,128,256]{2,1,0:T(8,128)(2,1)S(1)} %get-tuple-element.45), channel_id=1, source_target_pairs={{0,24},{4,28},{8,16},{12,20},{16,8},{20,12},{24,0},{28,4},{1,25},{... | collective-permute-start | bytes 393224 | tf_op jit(solution)/shard_map/ppermute | solution.py:434
  25.5 12.1 %collective-permute-start.14 = (bf16[2,128,256]{2,1,0:T(8,128)(2,1)S(1)}, bf16[2,128,256]{2,1,0:T(8,128)(2,1)S(1)}, u32[]{:S(2)}, u32[]{:S(2)}) collective-permute-start(bf16[2,128,256]{2,1,0:T(8,128)(2,1)S(1)} %get-tuple-element.46), channel_id=1, source_target_pairs={{0,28},{4,24},{8,20},{12,16},{16,12},{20,8},{24,4},{28,0},{1,29},{... | collective-permute-start | bytes 393224 | tf_op jit(solution)/shard_map/ppermute | solution.py:434
  33.9 15.9 %collective-permute-start.7 = (bf16[8,128,256]{2,1,0:T(8,128)(2,1)S(1)}, bf16[8,128,256]{2,1,0:T(8,128)(2,1)}, u32[]{:S(2)}, u32[]{:S(2)}) collective-permute-start(bf16[8,128,256]{2,1,0:T(8,128)(2,1)S(1)} %get-tuple-element.37), channel_id=1, source_target_pairs={{0,3},{1,0},{2,1},{3,2},{4,7},{5,4},{6,5},{7,6},{8,11},{9,8},{10,9... | collective-permute-start | bytes 1572872 | tf_op jit(solution)/shard_map/ppermute | solution.py:450
  44.4 11.1 %collective-permute-start.15 = (bf16[4,128,256]{2,1,0:T(8,128)(2,1)S(1)}, bf16[4,128,256]{2,1,0:T(8,128)(2,1)S(1)}, u32[]{:S(2)}, u32[]{:S(2)}) collective-permute-start(bf16[4,128,256]{2,1,0:T(8,128)(2,1)S(1)} %get-tuple-element.49), channel_id=1, source_target_pairs={{0,3},{1,0},{2,1},{3,2},{4,7},{5,4},{6,5},{7,6},{8,11},{9,8},{10,9... | collective-permute-start | bytes 786440 | tf_op jit(solution)/shard_map/ppermute | solution.py:450
  46.1 14.3 %collective-permute-start.19 = (bf16[4,128,256]{2,1,0:T(8,128)(2,1)S(1)}, bf16[4,128,256]{2,1,0:T(8,128)(2,1)S(1)}, u32[]{:S(2)}, u32[]{:S(2)}) collective-permute-start(bf16[4,128,256]{2,1,0:T(8,128)(2,1)S(1)} %get-tuple-element.52), channel_id=1, source_target_pairs={{0,3},{1,0},{2,1},{3,2},{4,7},{5,4},{6,5},{7,6},{8,11},{9,8},{10,9... | collective-permute-start | bytes 786440 | tf_op jit(solution)/shard_map/ppermute | solution.py:450
  49.9 19.1 %all-to-all-start = ((bf16[8,128,256]{2,1,0:T(8,128)(2,1)}), bf16[8,128,256]{2,1,0:T(8,128)(2,1)S(1)}, u32[]{:S(2)}, u32[]{:S(2)}) async-start(bf16[8,128,256]{2,1,0:T(8,128)(2,1)} %collective-permute-done.7), calls=%async_computation | async-start | bytes 1048576 | tf_op jit(solution)/shard_map/all_to_all | solution.py:432
  55.5 6.1 %collective-permute-start.16 = (bf16[128,256]{1,0:T(8,128)(2,1)S(1)}, bf16[128,256]{1,0:T(8,128)(2,1)S(1)}, u32[]{:S(2)}, u32[]{:S(2)}) collective-permute-start(bf16[128,256]{1,0:T(8,128)(2,1)S(1)} %get-tuple-element.62), channel_id=1, source_target_pairs={{0,4},{4,0},{8,12},{12,8},{16,20},{20,16},{24,28},{28,24},{1,5},{5... | collective-permute-start | bytes 196616 | tf_op jit(solution)/shard_map/ppermute | solution.py:434
  55.6 8.4 %collective-permute-start.17 = (bf16[128,256]{1,0:T(8,128)(2,1)S(1)}, bf16[128,256]{1,0:T(8,128)(2,1)S(1)}, u32[]{:S(2)}, u32[]{:S(2)}) collective-permute-start(bf16[128,256]{1,0:T(8,128)(2,1)S(1)} %get-tuple-element.61), channel_id=1, source_target_pairs={{0,8},{4,12},{8,0},{12,4},{16,24},{20,28},{24,16},{28,20},{1,9},{5... | collective-permute-start | bytes 196616 | tf_op jit(solution)/shard_map/ppermute | solution.py:434
  56.2 8.7 %collective-permute-start.18 = (bf16[128,256]{1,0:T(8,128)(2,1)S(1)}, bf16[128,256]{1,0:T(8,128)(2,1)S(1)}, u32[]{:S(2)}, u32[]{:S(2)}) collective-permute-start(bf16[128,256]{1,0:T(8,128)(2,1)S(1)} %get-tuple-element.60), channel_id=1, source_target_pairs={{0,12},{4,8},{8,4},{12,0},{16,28},{20,24},{24,20},{28,16},{1,13},{... | collective-permute-start | bytes 196616 | tf_op jit(solution)/shard_map/ppermute | solution.py:434
  60.4 4.6 %collective-permute-start.20 = (bf16[128,256]{1,0:T(8,128)(2,1)S(1)}, bf16[128,256]{1,0:T(8,128)(2,1)S(1)}, u32[]{:S(2)}, u32[]{:S(2)}) collective-permute-start(bf16[128,256]{1,0:T(8,128)(2,1)S(1)} %get-tuple-element.59), channel_id=1, source_target_pairs={{0,16},{4,20},{8,24},{12,28},{16,0},{20,4},{24,8},{28,12},{1,17},{... | collective-permute-start | bytes 196616 | tf_op jit(solution)/shard_map/ppermute | solution.py:434
  61.6 4.6 %collective-permute-start.21 = (bf16[128,256]{1,0:T(8,128)(2,1)S(1)}, bf16[128,256]{1,0:T(8,128)(2,1)S(1)}, u32[]{:S(2)}, u32[]{:S(2)}) collective-permute-start(bf16[128,256]{1,0:T(8,128)(2,1)S(1)} %get-tuple-element.58), channel_id=1, source_target_pairs={{0,20},{4,16},{8,28},{12,24},{16,4},{20,0},{24,12},{28,8},{1,21},{... | collective-permute-start | bytes 196616 | tf_op jit(solution)/shard_map/ppermute | solution.py:434
  61.6 5.9 %collective-permute-start.22 = (bf16[128,256]{1,0:T(8,128)(2,1)S(1)}, bf16[128,256]{1,0:T(8,128)(2,1)S(1)}, u32[]{:S(2)}, u32[]{:S(2)}) collective-permute-start(bf16[128,256]{1,0:T(8,128)(2,1)S(1)} %get-tuple-element.57), channel_id=1, source_target_pairs={{0,24},{4,28},{8,16},{12,20},{16,8},{20,12},{24,0},{28,4},{1,25},{... | collective-permute-start | bytes 196616 | tf_op jit(solution)/shard_map/ppermute | solution.py:434
  64.0 5.0 %collective-permute-start.23 = (bf16[128,256]{1,0:T(8,128)(2,1)S(1)}, bf16[128,256]{1,0:T(8,128)(2,1)S(1)}, u32[]{:S(2)}, u32[]{:S(2)}) collective-permute-start(bf16[128,256]{1,0:T(8,128)(2,1)S(1)} %get-tuple-element.56), channel_id=1, source_target_pairs={{0,28},{4,24},{8,20},{12,16},{16,12},{20,8},{24,4},{28,0},{1,29},{... | collective-permute-start | bytes 196616 | tf_op jit(solution)/shard_map/ppermute | solution.py:434

commit v7 on v6

--- a/solution.py
+++ b/solution.py
@@ -11,7 +11,7 @@
 
 WHOLE_IN = (False, False)
 WHOLE_OUT = (True, False)
-PARTS = (1, 2)
+LAST_SHARE = 4
 CHUNKS = len(WHOLE_IN)
 PAD = 8
 TILE = 16
@@ -191,7 +191,7 @@
     (pieces,) = by_target(refs[:taken], devices, [whole_in])
     tap_ref, spec_ref, fwd_ref, inv_ref = refs[taken : taken + 4]
     refs = refs[taken + 4 :]
-    out_refs, refs = refs[:parts], refs[parts:]
+    out_refs, refs = refs[: len(parts)], refs[len(parts) :]
     cross_ref, refs = refs[0], refs[1:]
     padded, upstream, key_rows, value_rows, turned, mixed, back = refs[:7]
     shifted_rows, grad_rows, tap_rows, tap_sem = refs[7:]
@@ -267,7 +267,7 @@
     shifted_rows[:, rows:, :] = jnp.zeros((3, PAD, width), jnp.float32)
 
     for k in range(devices):
-        number, within = divmod(k, devices // parts)
+        number, within = [(n, i) for n, size in enumerate(parts) for i in range(size)][k]
         for offset in range(0, length, LAST_TILE):
             begin = pl.multiple_of((k if whole_out else me ^ k) * length + offset, LAST_TILE)
             windows = [shifted_rows[i, pl.ds(begin, LAST_TILE + PAD), :] for i in range(3)]
@@ -285,8 +285,8 @@
     return pl.pallas_call(
         functools.partial(section_kernel, devices, chunk, whole_in, whole_out, parts),
         in_specs=[near] * len(pieces) + [far] + [near] * 3,
-        out_specs=[near] * (parts + 1),
-        out_shape=[jax.ShapeDtypeStruct((devices // parts, length, width), jnp.bfloat16)] * parts
+        out_specs=[near] * (len(parts) + 1),
+        out_shape=[jax.ShapeDtypeStruct((size, length, width), jnp.bfloat16) for size in parts]
         + [
             jax.ShapeDtypeStruct((4, rows // 2, width), jnp.bfloat16),
         ],
@@ -434,6 +434,10 @@
     return [chunk[0]] + [lax.ppermute(chunk[k], "seq", pairs(k)) for k in range(1, devices)]
 
 
+def parts_of(devices):
+    return (devices,), (devices - devices // LAST_SHARE, devices // LAST_SHARE)
+
+
 def fast(inputs, upstream, kernel, taps):
     devices, count = lax.axis_size("seq"), lax.axis_size("pipe")
     before = [(p, (p - 1) % count) for p in range(count)]
@@ -445,7 +449,7 @@
         arrived = exchanged(pieces[chunk], devices, WHOLE_IN[chunk])
         *parts, cross = section(
             arrived, taps, spec, fwd, inv, chunk, devices, WHOLE_IN[chunk], WHOLE_OUT[chunk],
-            PARTS[chunk],
+            parts_of(devices)[chunk],
         )
         moved = [lax.ppermute(part, "pipe", before) for part in parts[::-1]]
         grads.append(moved[::-1])
@@ -457,10 +461,10 @@
         for part in parts:
             part, filter_grad = lax.optimization_barrier((part, filter_grad))
             ready.append(part)
-        each = devices // len(ready)
+        split_up = [part[i] for part in ready for i in range(part.shape[0])]
         home.append(
             exchanged(
-                ready if whole else [ready[k // each][k % each] for k in range(devices)],
+                ready if whole else split_up,
                 devices,
                 whole,
             )

time: 70.3 us -> 70.6 us (level)
  starting transfers between devices: 32.3 us -> 33.4 us
  waiting for transfers between devices: 11.5 us -> 10.7 us
    ppermute x21, starting transfers between devices: 23 us -> 24.1 us  [exchanged(): lax.ppermute(chunk[k], 'seq', pairs(k))]
  transfers between devices with their start and end apart: 25 -> 25, of which waited for: 9 -> 7; matrix products, arithmetic and copies ran while one was open for 1% -> 1% of each run, Pallas kernels for 26% -> 26%
where the time goes in v7:
time: 70.6 us; the launch traced here: 70.3 us
  starting transfers between devices  33.4 us (47%)
  Pallas kernels  20.3 us (29%)
  waiting for transfers between devices  10.7 us (15%)
  local copies, waits for them, and re-layouts  5.23 us (7%)
  between operations  0.78 us (1%)
    ppermute x21, starting transfers between devices, exchanged(): lax.ppermute(chunk[k], 'seq', pairs(k))  24.1 us
    pallas_call x2, Pallas kernels, section(): pl.pallas_call(functools.partial(section_kernel, devices, chunk, whole_in...  13.6 us
    ppermute x3, starting transfers between devices, fast(): moved = [lax.ppermute(part, 'pipe', before) for part in parts[::-1]]  5.8 us
    ppermute x21, waiting for transfers between devices, exchanged(): lax.ppermute(chunk[k], 'seq', pairs(k))  5.48 us
    unnamed x11, local copies, waits for them, and re-layouts  5.2 us
    ppermute x3, waiting for transfers between devices, fast(): moved = [lax.ppermute(part, 'pipe', before) for part in parts[::-1]]  5.19 us
    all_to_all x1, starting transfers between devices, exchanged(): lax.all_to_all(chunk[0], 'seq', split_axis=0, concat_axis=0, tiled=True)  3.49 us
    pallas_call x1, Pallas kernels, filter_gradient(): pl.pallas_call(filter_kernel, in_specs=[pl.BlockSpec(memory_space=pltpu.V...  3.05 us
  transfers between devices with their start and end apart: 25, of which 7 were waited for; matrix products, arithmetic and copies ran while one was open for 1% of the time, Pallas kernels for 26%

profile of v7, /device:TPU:0, one launch (start us, length us, event | category | flops | bytes accessed | tf_op | source)
XLA Modules:
  0.0 70.3 jit_solution(744615506866330506)
XLA Ops:
  0.6 0.0 copy-start.1
  0.6 0.0 copy-start.3
  0.6 1.4 %copy-done.3 = bf16[1,128,4096]{2,1,0:T(8,128)(2,1)S(1)} copy-done((bf16[1,128,4096]{2,1,0:T(8,128)(2,1)S(1)}, bf16[1,128,4096]{2,1,0:T(8,128)(2,1)}, u32[]{:S(2)}) %copy-start.3) | copy-done | bytes 1048600
  2.0 1.2 %copy-done.4 = bf16[1,128,4096]{2,1,0:T(8,128)(2,1)S(1)} copy-done((bf16[1,128,4096]{2,1,0:T(8,128)(2,1)S(1)}, bf16[1,128,4096]{2,1,0:T(8,128)(2,1)}, u32[]{:S(2)}) %copy-start.4) | copy-done | bytes 1048600
  3.2 0.7 %pack.1 = (bf16[2,128,256]{2,1,0:T(8,128)(2,1)S(1)}, bf16[2,128,256]{2,1,0:T(8,128)(2,1)S(1)}, bf16[2,128,256]{2,1,0:T(8,128)(2,1)S(1)}, bf16[2,128,256]{2,1,0:T...) custom-call(bf16[128,4096]{1,0:T(8,128)(2,1)S(1)} %bitcast.21, ...), custom_call_target="tpu_custom_call" | custom-call | tf_op jit(solution)/shard_map/pack/pallas_call | solution.py:103
  4.0 0.5 collective-permute-start
  4.5 2.6 %collective-permute-start.1 = (bf16[2,128,256]{2,1,0:T(8,128)(2,1)S(1)}, bf16[2,128,256]{2,1,0:T(8,128)(2,1)S(1)}, u32[]{:S(2)}, u32[]{:S(2)}) collective-permute-start(bf16[2,128,256]{2,1,0:T(8,128)(2,1)S(1)} %get-tuple-element.31), channel_id=1, source_target_pairs={{0,8},{4,12},{8,0},{12,4},{16,24},{20,28},{24,16},{28,20},{1,9},{5... | collective-permute-start | bytes 393224 | tf_op jit(solution)/shard_map/ppermute | solution.py:434
  7.1 0.1 collective-permute-start.2
  7.1 1.8 %collective-permute-start.3 = (bf16[2,128,256]{2,1,0:T(8,128)(2,1)S(1)}, bf16[2,128,256]{2,1,0:T(8,128)(2,1)S(1)}, u32[]{:S(2)}, u32[]{:S(2)}) collective-permute-start(bf16[2,128,256]{2,1,0:T(8,128)(2,1)S(1)} %get-tuple-element.33), channel_id=1, source_target_pairs={{0,16},{4,20},{8,24},{12,28},{16,0},{20,4},{24,8},{28,12},{1,17},{... | collective-permute-start | bytes 393224 | tf_op jit(solution)/shard_map/ppermute | solution.py:434
  8.9 0.0 collective-permute-start.4
  8.9 0.0 collective-permute-done.refs_1_
  8.9 2.6 %collective-permute-start.5 = (bf16[2,128,256]{2,1,0:T(8,128)(2,1)S(1)}, bf16[2,128,256]{2,1,0:T(8,128)(2,1)S(1)}, u32[]{:S(2)}, u32[]{:S(2)}) collective-permute-start(bf16[2,128,256]{2,1,0:T(8,128)(2,1)S(1)} %get-tuple-element.35), channel_id=1, source_target_pairs={{0,24},{4,28},{8,16},{12,20},{16,8},{20,12},{24,0},{28,4},{1,25},{... | collective-permute-start | bytes 393224 | tf_op jit(solution)/shard_map/ppermute | solution.py:434
  11.5 0.0 collective-permute-done.1.refs_2_
  11.5 1.6 %collective-permute-start.6 = (bf16[2,128,256]{2,1,0:T(8,128)(2,1)S(1)}, bf16[2,128,256]{2,1,0:T(8,128)(2,1)S(1)}, u32[]{:S(2)}, u32[]{:S(2)}) collective-permute-start(bf16[2,128,256]{2,1,0:T(8,128)(2,1)S(1)} %get-tuple-element.36), channel_id=1, source_target_pairs={{0,28},{4,24},{8,20},{12,16},{16,12},{20,8},{24,4},{28,0},{1,29},{... | collective-permute-start | bytes 393224 | tf_op jit(solution)/shard_map/ppermute | solution.py:434
  13.1 0.6 collective-permute-done.2.refs_3_
  13.7 0.7 %collective-permute-start.8 = (bf16[2,128,256]{2,1,0:T(8,128)(2,1)S(1)}, bf16[2,128,256]{2,1,0:T(8,128)(2,1)S(1)}, u32[]{:S(2)}, u32[]{:S(2)}) collective-permute-start(bf16[2,128,256]{2,1,0:T(8,128)(2,1)S(1)} %get-tuple-element.40), channel_id=1, source_target_pairs={{0,4},{4,0},{8,12},{12,8},{16,20},{20,16},{24,28},{28,24},{1,5},{5... | collective-permute-start | bytes 393224 | tf_op jit(solution)/shard_map/ppermute | solution.py:434
  14.4 0.0 collective-permute-done.3.refs_4_
  14.4 1.8 %collective-permute-start.9 = (bf16[2,128,256]{2,1,0:T(8,128)(2,1)S(1)}, bf16[2,128,256]{2,1,0:T(8,128)(2,1)S(1)}, u32[]{:S(2)}, u32[]{:S(2)}) collective-permute-start(bf16[2,128,256]{2,1,0:T(8,128)(2,1)S(1)} %get-tuple-element.41), channel_id=1, source_target_pairs={{0,8},{4,12},{8,0},{12,4},{16,24},{20,28},{24,16},{28,20},{1,9},{5... | collective-permute-start | bytes 393224 | tf_op jit(solution)/shard_map/ppermute | solution.py:434
  16.3 1.0 %copy.8.refs_8_ = f32[1,3,3,4096]{3,2,1,0:T(4,128)S(1)} copy(f32[1,3,3,4096]{3,0,2,1:T(1,128)} %param.9) | data formatting | bytes 294912 | tf_op args[3]
  17.3 0.0 copy-done.1
  17.3 0.0 copy-start.2
  17.3 1.6 %copy-done.2 = bf16[4,512,512]{2,1,0:T(8,128)(2,1)S(1)} copy-done((bf16[4,512,512]{2,1,0:T(8,128)(2,1)S(1)}, bf16[4,512,512]{2,1,0:T(8,128)(2,1)}, u32[]{:S(2)}) %copy-start.2) | copy-done | bytes 2097176
  18.9 1.9 %spectrum.1.refs_9_ = f32[4,512,512]{2,1,0:T(8,128)S(1)} custom-call(f32[1024,512]{1,0:T(8,128)S(1)} %bitcast.20, bf16[4,512,512]{2,1,0:T(8,128)(2,1)S(1)} %copy-done.2), custom_call_target="tpu_custom_call" | custom-call | flops 1073741824 | bytes 7340032 | tf_op jit(solution)/shard_map/spectrum/pallas_call | solution.py:175
  20.8 0.0 collective-permute-done.4.refs_5_
  20.8 1.9 %collective-permute-start.10 = (bf16[2,128,256]{2,1,0:T(8,128)(2,1)S(1)}, bf16[2,128,256]{2,1,0:T(8,128)(2,1)S(1)}, u32[]{:S(2)}, u32[]{:S(2)}) collective-permute-start(bf16[2,128,256]{2,1,0:T(8,128)(2,1)S(1)} %get-tuple-element.42), channel_id=1, source_target_pairs={{0,12},{4,8},{8,4},{12,0},{16,28},{20,24},{24,20},{28,16},{1,13},{... | collective-permute-start | bytes 393224 | tf_op jit(solution)/shard_map/ppermute | solution.py:434
  22.7 0.0 collective-permute-done.5.refs_6_
  22.8 1.5 %collective-permute-start.11 = (bf16[2,128,256]{2,1,0:T(8,128)(2,1)S(1)}, bf16[2,128,256]{2,1,0:T(8,128)(2,1)S(1)}, u32[]{:S(2)}, u32[]{:S(2)}) collective-permute-start(bf16[2,128,256]{2,1,0:T(8,128)(2,1)S(1)} %get-tuple-element.43), channel_id=1, source_target_pairs={{0,16},{4,20},{8,24},{12,28},{16,0},{20,4},{24,8},{28,12},{1,17},{... | collective-permute-start | bytes 393224 | tf_op jit(solution)/shard_map/ppermute | solution.py:434
  24.3 0.0 collective-permute-done.6.refs_7_
  24.3 0.0 collective-permute-start.12
  24.3 0.0 collective-permute-done.8.refs_1_
  24.3 1.2 %collective-permute-start.13 = (bf16[2,128,256]{2,1,0:T(8,128)(2,1)S(1)}, bf16[2,128,256]{2,1,0:T(8,128)(2,1)S(1)}, u32[]{:S(2)}, u32[]{:S(2)}) collective-permute-start(bf16[2,128,256]{2,1,0:T(8,128)(2,1)S(1)} %get-tuple-element.45), channel_id=1, source_target_pairs={{0,24},{4,28},{8,16},{12,20},{16,8},{20,12},{24,0},{28,4},{1,25},{... | collective-permute-start | bytes 393224 | tf_op jit(solution)/shard_map/ppermute | solution.py:434
  25.5 0.0 collective-permute-done.9.refs_2_
  25.5 1.7 %collective-permute-start.14 = (bf16[2,128,256]{2,1,0:T(8,128)(2,1)S(1)}, bf16[2,128,256]{2,1,0:T(8,128)(2,1)S(1)}, u32[]{:S(2)}, u32[]{:S(2)}) collective-permute-start(bf16[2,128,256]{2,1,0:T(8,128)(2,1)S(1)} %get-tuple-element.46), channel_id=1, source_target_pairs={{0,28},{4,24},{8,20},{12,16},{16,12},{20,8},{24,4},{28,0},{1,29},{... | collective-permute-start | bytes 393224 | tf_op jit(solution)/shard_map/ppermute | solution.py:434
  27.2 6.8 %section.2 = (bf16[8,128,256]{2,1,0:T(8,128)(2,1)S(1)}, bf16[4,512,256]{2,1,0:T(8,128)(2,1)S(1)}) custom-call(bf16[2,128,256]{2,1,0:T(8,128)(2,1)S(1)} %get-tuple-element.29.refs_0_, bf16[2,128,256]{2,1,0:T(8,128)(2,1)S(1)} %collective-permute-done.refs_1_, bf16[2,128,256]{2,1,0:T(8,128)(2,1)S(1)} %collective-permute-done.1.refs_2_, ...), custom_call_target="tpu_custom_call" | custom-call | flops 2684354560 | bytes 5242880 | tf_op jit(solution)/shard_map/section/pallas_call | solution.py:285
  33.9 0.0 collective-permute-done.10.refs_3_
  33.9 3.7 %collective-permute-start.7 = (bf16[8,128,256]{2,1,0:T(8,128)(2,1)S(1)}, bf16[8,128,256]{2,1,0:T(8,128)(2,1)}, u32[]{:S(2)}, u32[]{:S(2)}) collective-permute-start(bf16[8,128,256]{2,1,0:T(8,128)(2,1)S(1)} %get-tuple-element.37), channel_id=1, source_target_pairs={{0,3},{1,0},{2,1},{3,2},{4,7},{5,4},{6,5},{7,6},{8,11},{9,8},{10,9... | collective-permute-start | bytes 1572872 | tf_op jit(solution)/shard_map/ppermute | solution.py:454
  37.6 0.0 collective-permute-done.11.refs_4_
  37.6 0.0 collective-permute-done.12.refs_5_
  37.6 0.0 collective-permute-done.13.refs_6_
  37.6 0.0 collective-permute-done.14.refs_7_
  37.6 6.8 %section.3 = (bf16[6,128,256]{2,1,0:T(8,128)(2,1)S(1)}, bf16[2,128,256]{2,1,0:T(8,128)(2,1)S(1)}, bf16[4,512,256]{2,1,0:T(8,128)(2,1)S(1)}) custom-call(bf16[2,128,256]{2,1,0:T(8,128)(2,1)S(1)} %get-tuple-element.39.refs_0_, bf16[2,128,256]{2,1,0:T(8,128)(2,1)S(1)} %collective-permute-done.8.refs_1_, ...), custom_call_target="tpu_custom_call" | custom-call | flops 2684354560 | bytes 5242880 | tf_op jit(solution)/shard_map/section/pallas_call | solution.py:285
  44.4 1.7 %collective-permute-start.15 = (bf16[6,128,256]{2,1,0:T(8,128)(2,1)S(1)}, bf16[6,128,256]{2,1,0:T(8,128)(2,1)S(1)}, u32[]{:S(2)}, u32[]{:S(2)}) collective-permute-start(bf16[6,128,256]{2,1,0:T(8,128)(2,1)S(1)} %get-tuple-element.49), channel_id=1, source_target_pairs={{0,3},{1,0},{2,1},{3,2},{4,7},{5,4},{6,5},{7,6},{8,11},{9,8},{10,9... | collective-permute-start | bytes 1179656 | tf_op jit(solution)/shard_map/ppermute | solution.py:454
  46.1 0.5 collective-permute-start.21
  46.6 3.0 %filter.1 = f32[1024,512]{1,0:T(8,128)} custom-call(bf16[4,512,512]{2,1,0:T(8,128)(2,1)S(1)} %copy-done, bf16[4,512,256]{2,1,0:T(8,128)(2,1)S(1)} %get-tuple-element.38.refs_0_, bf16[4,512,256]{2,1,0:T(8,128)(2,1)S(1)} %get-tuple-element.47.refs_1_), custom_call_target="tpu_custom_call" | custom-call | flops 1073741824 | bytes 3145728 | tf_op jit(solution)/shard_map/filter/pallas_call | solution.py:340
  49.6 0.3 collective-permute-done.7
  49.9 3.5 %all-to-all-start = ((bf16[8,128,256]{2,1,0:T(8,128)(2,1)}), bf16[8,128,256]{2,1,0:T(8,128)(2,1)S(1)}, u32[]{:S(2)}, u32[]{:S(2)}) async-start(bf16[8,128,256]{2,1,0:T(8,128)(2,1)} %collective-permute-done.7), calls=%async_computation | async-start | bytes 1048576 | tf_op jit(solution)/shard_map/all_to_all | solution.py:432
  53.4 4.9 %collective-permute-done.15 = bf16[6,128,256]{2,1,0:T(8,128)(2,1)S(1)} collective-permute-done((bf16[6,128,256]{2,1,0:T(8,128)(2,1)S(1)}, bf16[6,128,256]{2,1,0:T(8,128)(2,1)S(1)}, u32[]{:S(2)}, u32[]{:S(2)}) %collective-permute-start.15) | collective-permute-done | bytes 393248 | tf_op jit(solution)/shard_map/ppermute | solution.py:454
  58.3 0.1 collective-permute-start.16
  58.4 0.6 collective-permute-start.17
  59.0 1.3 %collective-permute-start.18 = (bf16[128,256]{1,0:T(8,128)(2,1)S(1)}, bf16[128,256]{1,0:T(8,128)(2,1)S(1)}, u32[]{:S(2)}, u32[]{:S(2)}) collective-permute-start(bf16[128,256]{1,0:T(8,128)(2,1)S(1)} %get-tuple-element.58), channel_id=1, source_target_pairs={{0,12},{4,8},{8,4},{12,0},{16,28},{20,24},{24,20},{28,16},{1,13},{... | collective-permute-start | bytes 196616 | tf_op jit(solution)/shard_map/ppermute | solution.py:434
  60.3 1.6 %collective-permute-start.19 = (bf16[128,256]{1,0:T(8,128)(2,1)S(1)}, bf16[128,256]{1,0:T(8,128)(2,1)S(1)}, u32[]{:S(2)}, u32[]{:S(2)}) collective-permute-start(bf16[128,256]{1,0:T(8,128)(2,1)S(1)} %get-tuple-element.57), channel_id=1, source_target_pairs={{0,16},{4,20},{8,24},{12,28},{16,0},{20,4},{24,8},{28,12},{1,17},{... | collective-permute-start | bytes 196616 | tf_op jit(solution)/shard_map/ppermute | solution.py:434
  61.8 0.0 collective-permute-done.21
  61.9 0.1 collective-permute-start.20
  62.0 0.0 collective-permute-done.16.refs_2_
  62.0 1.6 %collective-permute-start.22 = (bf16[128,256]{1,0:T(8,128)(2,1)S(1)}, bf16[128,256]{1,0:T(8,128)(2,1)S(1)}, u32[]{:S(2)}, u32[]{:S(2)}) collective-permute-start(bf16[128,256]{1,0:T(8,128)(2,1)S(1)} %get-tuple-element.63), channel_id=1, source_target_pairs={{0,24},{4,28},{8,16},{12,20},{16,8},{20,12},{24,0},{28,4},{1,25},{... | collective-permute-start | bytes 196616 | tf_op jit(solution)/shard_map/ppermute | solution.py:434
  63.6 0.4 collective-permute-done.17.refs_3_
  64.0 0.8 %collective-permute-start.23 = (bf16[128,256]{1,0:T(8,128)(2,1)S(1)}, bf16[128,256]{1,0:T(8,128)(2,1)S(1)}, u32[]{:S(2)}, u32[]{:S(2)}) collective-permute-start(bf16[128,256]{1,0:T(8,128)(2,1)S(1)} %get-tuple-element.62), channel_id=1, source_target_pairs={{0,28},{4,24},{8,20},{12,16},{16,12},{20,8},{24,4},{28,0},{1,29},{... | collective-permute-start | bytes 196616 | tf_op jit(solution)/shard_map/ppermute | solution.py:434
  64.8 0.0 collective-permute-done.18.refs_4_
  64.8 0.0 collective-permute-done.19.refs_5_
  64.8 1.2 %collective-permute-done.20.refs_6_ = bf16[128,256]{1,0:T(8,128)(2,1)S(1)} collective-permute-done((bf16[128,256]{1,0:T(8,128)(2,1)S(1)}, bf16[128,256]{1,0:T(8,128)(2,1)S(1)}, u32[]{:S(2)}, u32[]{:S(2)}) %collective-permute-start.20) | collective-permute-done | bytes 65568 | tf_op jit(solution)/shard_map/ppermute | solution.py:434
  66.0 1.5 %collective-permute-done.22.refs_7_ = bf16[128,256]{1,0:T(8,128)(2,1)S(1)} collective-permute-done((bf16[128,256]{1,0:T(8,128)(2,1)S(1)}, bf16[128,256]{1,0:T(8,128)(2,1)S(1)}, u32[]{:S(2)}, u32[]{:S(2)}) %collective-permute-start.22) | collective-permute-done | bytes 65568 | tf_op jit(solution)/shard_map/ppermute | solution.py:434
  67.5 1.7 %collective-permute-done.23.refs_8_ = bf16[128,256]{1,0:T(8,128)(2,1)S(1)} collective-permute-done((bf16[128,256]{1,0:T(8,128)(2,1)S(1)}, bf16[128,256]{1,0:T(8,128)(2,1)S(1)}, u32[]{:S(2)}, u32[]{:S(2)}) %collective-permute-start.23) | collective-permute-done | bytes 65568 | tf_op jit(solution)/shard_map/ppermute | solution.py:434
  69.2 0.0 all-to-all-done.refs_0_
  69.2 1.1 %unpack.1 = bf16[1,128,4096]{2,1,0:T(8,128)(2,1)} custom-call(bf16[8,128,256]{2,1,0:T(8,128)(2,1)S(1)} %all-to-all-done.refs_0_, bf16[128,256]{1,0:T(8,128)(2,1)S(1)} %get-tuple-element.61.refs_1_, bf16[128,256]{1,0:T(8,128)(2,1)S(1)} %collective-permute-done.16.refs_2_, bf16[128,256]{1,0:T(8,128)(2,1)S(1)} %collective-permute-done.17.refs_3_, ...), custom_call_target="tpu_custom_call" | custom-call | tf_op jit(solution)/shard_map/unpack/pallas_call | solution.py:145
  (5 shorter events, 0.0 us)
Async XLA Ops:
  0.6 16.7 %copy-start.1 = (f32[1,1024,512]{2,1,0:T(8,128)S(1)}, f32[1,1024,512]{2,1,0:T(8,128)}, u32[]{:S(2)}) copy-start(f32[1,1024,512]{2,1,0:T(8,128)} %param.8) | copy-start | bytes 6291460
  0.6 1.4 %copy-start.3 = (bf16[1,128,4096]{2,1,0:T(8,128)(2,1)S(1)}, bf16[1,128,4096]{2,1,0:T(8,128)(2,1)}, u32[]{:S(2)}) copy-start(bf16[1,128,4096]{2,1,0:T(8,128)(2,1)} %param.6) | copy-start | bytes 3145732
  2.0 1.2 %copy-start.4 = (bf16[1,128,4096]{2,1,0:T(8,128)(2,1)S(1)}, bf16[1,128,4096]{2,1,0:T(8,128)(2,1)}, u32[]{:S(2)}) copy-start(bf16[1,128,4096]{2,1,0:T(8,128)(2,1)} %param.7) | copy-start | bytes 3145732
  4.0 4.9 %collective-permute-start = (bf16[2,128,256]{2,1,0:T(8,128)(2,1)S(1)}, bf16[2,128,256]{2,1,0:T(8,128)(2,1)S(1)}, u32[]{:S(2)}, u32[]{:S(2)}) collective-permute-start(bf16[2,128,256]{2,1,0:T(8,128)(2,1)S(1)} %get-tuple-element.30), channel_id=1, source_target_pairs={{0,4},{4,0},{8,12},{12,8},{16,20},{20,16},{24,28},{28,24},{1,5},{5... | collective-permute-start | bytes 393224 | tf_op jit(solution)/shard_map/ppermute | solution.py:434
  4.5 7.0 %collective-permute-start.1 = (bf16[2,128,256]{2,1,0:T(8,128)(2,1)S(1)}, bf16[2,128,256]{2,1,0:T(8,128)(2,1)S(1)}, u32[]{:S(2)}, u32[]{:S(2)}) collective-permute-start(bf16[2,128,256]{2,1,0:T(8,128)(2,1)S(1)} %get-tuple-element.31), channel_id=1, source_target_pairs={{0,8},{4,12},{8,0},{12,4},{16,24},{20,28},{24,16},{28,20},{1,9},{5... | collective-permute-start | bytes 393224 | tf_op jit(solution)/shard_map/ppermute | solution.py:434
  7.1 6.6 %collective-permute-start.2 = (bf16[2,128,256]{2,1,0:T(8,128)(2,1)S(1)}, bf16[2,128,256]{2,1,0:T(8,128)(2,1)S(1)}, u32[]{:S(2)}, u32[]{:S(2)}) collective-permute-start(bf16[2,128,256]{2,1,0:T(8,128)(2,1)S(1)} %get-tuple-element.32), channel_id=1, source_target_pairs={{0,12},{4,8},{8,4},{12,0},{16,28},{20,24},{24,20},{28,16},{1,13},{... | collective-permute-start | bytes 393224 | tf_op jit(solution)/shard_map/ppermute | solution.py:434
  7.1 7.3 %collective-permute-start.3 = (bf16[2,128,256]{2,1,0:T(8,128)(2,1)S(1)}, bf16[2,128,256]{2,1,0:T(8,128)(2,1)S(1)}, u32[]{:S(2)}, u32[]{:S(2)}) collective-permute-start(bf16[2,128,256]{2,1,0:T(8,128)(2,1)S(1)} %get-tuple-element.33), channel_id=1, source_target_pairs={{0,16},{4,20},{8,24},{12,28},{16,0},{20,4},{24,8},{28,12},{1,17},{... | collective-permute-start | bytes 393224 | tf_op jit(solution)/shard_map/ppermute | solution.py:434
  8.9 11.9 %collective-permute-start.4 = (bf16[2,128,256]{2,1,0:T(8,128)(2,1)S(1)}, bf16[2,128,256]{2,1,0:T(8,128)(2,1)S(1)}, u32[]{:S(2)}, u32[]{:S(2)}) collective-permute-start(bf16[2,128,256]{2,1,0:T(8,128)(2,1)S(1)} %get-tuple-element.34), channel_id=1, source_target_pairs={{0,20},{4,16},{8,28},{12,24},{16,4},{20,0},{24,12},{28,8},{1,21},{... | collective-permute-start | bytes 393224 | tf_op jit(solution)/shard_map/ppermute | solution.py:434
  8.9 13.8 %collective-permute-start.5 = (bf16[2,128,256]{2,1,0:T(8,128)(2,1)S(1)}, bf16[2,128,256]{2,1,0:T(8,128)(2,1)S(1)}, u32[]{:S(2)}, u32[]{:S(2)}) collective-permute-start(bf16[2,128,256]{2,1,0:T(8,128)(2,1)S(1)} %get-tuple-element.35), channel_id=1, source_target_pairs={{0,24},{4,28},{8,16},{12,20},{16,8},{20,12},{24,0},{28,4},{1,25},{... | collective-permute-start | bytes 393224 | tf_op jit(solution)/shard_map/ppermute | solution.py:434
  11.5 12.8 %collective-permute-start.6 = (bf16[2,128,256]{2,1,0:T(8,128)(2,1)S(1)}, bf16[2,128,256]{2,1,0:T(8,128)(2,1)S(1)}, u32[]{:S(2)}, u32[]{:S(2)}) collective-permute-start(bf16[2,128,256]{2,1,0:T(8,128)(2,1)S(1)} %get-tuple-element.36), channel_id=1, source_target_pairs={{0,28},{4,24},{8,20},{12,16},{16,12},{20,8},{24,4},{28,0},{1,29},{... | collective-permute-start | bytes 393224 | tf_op jit(solution)/shard_map/ppermute | solution.py:434
  13.7 10.6 %collective-permute-start.8 = (bf16[2,128,256]{2,1,0:T(8,128)(2,1)S(1)}, bf16[2,128,256]{2,1,0:T(8,128)(2,1)S(1)}, u32[]{:S(2)}, u32[]{:S(2)}) collective-permute-start(bf16[2,128,256]{2,1,0:T(8,128)(2,1)S(1)} %get-tuple-element.40), channel_id=1, source_target_pairs={{0,4},{4,0},{8,12},{12,8},{16,20},{20,16},{24,28},{28,24},{1,5},{5... | collective-permute-start | bytes 393224 | tf_op jit(solution)/shard_map/ppermute | solution.py:434
  14.4 11.0 %collective-permute-start.9 = (bf16[2,128,256]{2,1,0:T(8,128)(2,1)S(1)}, bf16[2,128,256]{2,1,0:T(8,128)(2,1)S(1)}, u32[]{:S(2)}, u32[]{:S(2)}) collective-permute-start(bf16[2,128,256]{2,1,0:T(8,128)(2,1)S(1)} %get-tuple-element.41), channel_id=1, source_target_pairs={{0,8},{4,12},{8,0},{12,4},{16,24},{20,28},{24,16},{28,20},{1,9},{5... | collective-permute-start | bytes 393224 | tf_op jit(solution)/shard_map/ppermute | solution.py:434
  17.3 1.6 %copy-start.2 = (bf16[4,512,512]{2,1,0:T(8,128)(2,1)S(1)}, bf16[4,512,512]{2,1,0:T(8,128)(2,1)}, u32[]{:S(2)}) copy-start(bf16[4,512,512]{2,1,0:T(8,128)(2,1)} %constant.4.clone.fwd_ref.refs_10_) | copy-start | bytes 6291460
  18.9 8.3 %copy-start = (bf16[4,512,512]{2,1,0:T(8,128)(2,1)S(1)}, bf16[4,512,512]{2,1,0:T(8,128)(2,1)}, u32[]{:S(2)}) copy-start(bf16[4,512,512]{2,1,0:T(8,128)(2,1)} %constant.5.clone.refs_11_.inv_ref) | copy-start | bytes 6291460
  20.8 13.1 %collective-permute-start.10 = (bf16[2,128,256]{2,1,0:T(8,128)(2,1)S(1)}, bf16[2,128,256]{2,1,0:T(8,128)(2,1)S(1)}, u32[]{:S(2)}, u32[]{:S(2)}) collective-permute-start(bf16[2,128,256]{2,1,0:T(8,128)(2,1)S(1)} %get-tuple-element.42), channel_id=1, source_target_pairs={{0,12},{4,8},{8,4},{12,0},{16,28},{20,24},{24,20},{28,16},{1,13},{... | collective-permute-start | bytes 393224 | tf_op jit(solution)/shard_map/ppermute | solution.py:434
  22.8 14.8 %collective-permute-start.11 = (bf16[2,128,256]{2,1,0:T(8,128)(2,1)S(1)}, bf16[2,128,256]{2,1,0:T(8,128)(2,1)S(1)}, u32[]{:S(2)}, u32[]{:S(2)}) collective-permute-start(bf16[2,128,256]{2,1,0:T(8,128)(2,1)S(1)} %get-tuple-element.43), channel_id=1, source_target_pairs={{0,16},{4,20},{8,24},{12,28},{16,0},{20,4},{24,8},{28,12},{1,17},{... | collective-permute-start | bytes 393224 | tf_op jit(solution)/shard_map/ppermute | solution.py:434
  24.3 13.3 %collective-permute-start.12 = (bf16[2,128,256]{2,1,0:T(8,128)(2,1)S(1)}, bf16[2,128,256]{2,1,0:T(8,128)(2,1)S(1)}, u32[]{:S(2)}, u32[]{:S(2)}) collective-permute-start(bf16[2,128,256]{2,1,0:T(8,128)(2,1)S(1)} %get-tuple-element.44), channel_id=1, source_target_pairs={{0,20},{4,16},{8,28},{12,24},{16,4},{20,0},{24,12},{28,8},{1,21},{... | collective-permute-start | bytes 393224 | tf_op jit(solution)/shard_map/ppermute | solution.py:434
  24.3 13.3 %collective-permute-start.13 = (bf16[2,128,256]{2,1,0:T(8,128)(2,1)S(1)}, bf16[2,128,256]{2,1,0:T(8,128)(2,1)S(1)}, u32[]{:S(2)}, u32[]{:S(2)}) collective-permute-start(bf16[2,128,256]{2,1,0:T(8,128)(2,1)S(1)} %get-tuple-element.45), channel_id=1, source_target_pairs={{0,24},{4,28},{8,16},{12,20},{16,8},{20,12},{24,0},{28,4},{1,25},{... | collective-permute-start | bytes 393224 | tf_op jit(solution)/shard_map/ppermute | solution.py:434
  25.5 12.1 %collective-permute-start.14 = (bf16[2,128,256]{2,1,0:T(8,128)(2,1)S(1)}, bf16[2,128,256]{2,1,0:T(8,128)(2,1)S(1)}, u32[]{:S(2)}, u32[]{:S(2)}) collective-permute-start(bf16[2,128,256]{2,1,0:T(8,128)(2,1)S(1)} %get-tuple-element.46), channel_id=1, source_target_pairs={{0,28},{4,24},{8,20},{12,16},{16,12},{20,8},{24,4},{28,0},{1,29},{... | collective-permute-start | bytes 393224 | tf_op jit(solution)/shard_map/ppermute | solution.py:434
  33.9 15.9 %collective-permute-start.7 = (bf16[8,128,256]{2,1,0:T(8,128)(2,1)S(1)}, bf16[8,128,256]{2,1,0:T(8,128)(2,1)}, u32[]{:S(2)}, u32[]{:S(2)}) collective-permute-start(bf16[8,128,256]{2,1,0:T(8,128)(2,1)S(1)} %get-tuple-element.37), channel_id=1, source_target_pairs={{0,3},{1,0},{2,1},{3,2},{4,7},{5,4},{6,5},{7,6},{8,11},{9,8},{10,9... | collective-permute-start | bytes 1572872 | tf_op jit(solution)/shard_map/ppermute | solution.py:454
  44.4 13.9 %collective-permute-start.15 = (bf16[6,128,256]{2,1,0:T(8,128)(2,1)S(1)}, bf16[6,128,256]{2,1,0:T(8,128)(2,1)S(1)}, u32[]{:S(2)}, u32[]{:S(2)}) collective-permute-start(bf16[6,128,256]{2,1,0:T(8,128)(2,1)S(1)} %get-tuple-element.49), channel_id=1, source_target_pairs={{0,3},{1,0},{2,1},{3,2},{4,7},{5,4},{6,5},{7,6},{8,11},{9,8},{10,9... | collective-permute-start | bytes 1179656 | tf_op jit(solution)/shard_map/ppermute | solution.py:454
  46.1 15.7 %collective-permute-start.21 = (bf16[2,128,256]{2,1,0:T(8,128)(2,1)S(1)}, bf16[2,128,256]{2,1,0:T(8,128)(2,1)S(1)}, u32[]{:S(2)}, u32[]{:S(2)}) collective-permute-start(bf16[2,128,256]{2,1,0:T(8,128)(2,1)S(1)} %get-tuple-element.52), channel_id=1, source_target_pairs={{0,3},{1,0},{2,1},{3,2},{4,7},{5,4},{6,5},{7,6},{8,11},{9,8},{10,9... | collective-permute-start | bytes 393224 | tf_op jit(solution)/shard_map/ppermute | solution.py:454
  49.9 19.4 %all-to-all-start = ((bf16[8,128,256]{2,1,0:T(8,128)(2,1)}), bf16[8,128,256]{2,1,0:T(8,128)(2,1)S(1)}, u32[]{:S(2)}, u32[]{:S(2)}) async-start(bf16[8,128,256]{2,1,0:T(8,128)(2,1)} %collective-permute-done.7), calls=%async_computation | async-start | bytes 1048576 | tf_op jit(solution)/shard_map/all_to_all | solution.py:432
  58.3 3.7 %collective-permute-start.16 = (bf16[128,256]{1,0:T(8,128)(2,1)S(1)}, bf16[128,256]{1,0:T(8,128)(2,1)S(1)}, u32[]{:S(2)}, u32[]{:S(2)}) collective-permute-start(bf16[128,256]{1,0:T(8,128)(2,1)S(1)} %get-tuple-element.60), channel_id=1, source_target_pairs={{0,4},{4,0},{8,12},{12,8},{16,20},{20,16},{24,28},{28,24},{1,5},{5... | collective-permute-start | bytes 196616 | tf_op jit(solution)/shard_map/ppermute | solution.py:434
  58.4 5.6 %collective-permute-start.17 = (bf16[128,256]{1,0:T(8,128)(2,1)S(1)}, bf16[128,256]{1,0:T(8,128)(2,1)S(1)}, u32[]{:S(2)}, u32[]{:S(2)}) collective-permute-start(bf16[128,256]{1,0:T(8,128)(2,1)S(1)} %get-tuple-element.59), channel_id=1, source_target_pairs={{0,8},{4,12},{8,0},{12,4},{16,24},{20,28},{24,16},{28,20},{1,9},{5... | collective-permute-start | bytes 196616 | tf_op jit(solution)/shard_map/ppermute | solution.py:434
  59.0 5.8 %collective-permute-start.18 = (bf16[128,256]{1,0:T(8,128)(2,1)S(1)}, bf16[128,256]{1,0:T(8,128)(2,1)S(1)}, u32[]{:S(2)}, u32[]{:S(2)}) collective-permute-start(bf16[128,256]{1,0:T(8,128)(2,1)S(1)} %get-tuple-element.58), channel_id=1, source_target_pairs={{0,12},{4,8},{8,4},{12,0},{16,28},{20,24},{24,20},{28,16},{1,13},{... | collective-permute-start | bytes 196616 | tf_op jit(solution)/shard_map/ppermute | solution.py:434
  60.3 4.5 %collective-permute-start.19 = (bf16[128,256]{1,0:T(8,128)(2,1)S(1)}, bf16[128,256]{1,0:T(8,128)(2,1)S(1)}, u32[]{:S(2)}, u32[]{:S(2)}) collective-permute-start(bf16[128,256]{1,0:T(8,128)(2,1)S(1)} %get-tuple-element.57), channel_id=1, source_target_pairs={{0,16},{4,20},{8,24},{12,28},{16,0},{20,4},{24,8},{28,12},{1,17},{... | collective-permute-start | bytes 196616 | tf_op jit(solution)/shard_map/ppermute | solution.py:434
  61.9 4.1 %collective-permute-start.20 = (bf16[128,256]{1,0:T(8,128)(2,1)S(1)}, bf16[128,256]{1,0:T(8,128)(2,1)S(1)}, u32[]{:S(2)}, u32[]{:S(2)}) collective-permute-start(bf16[128,256]{1,0:T(8,128)(2,1)S(1)} %get-tuple-element.56), channel_id=1, source_target_pairs={{0,20},{4,16},{8,28},{12,24},{16,4},{20,0},{24,12},{28,8},{1,21},{... | collective-permute-start | bytes 196616 | tf_op jit(solution)/shard_map/ppermute | solution.py:434
  62.0 5.5 %collective-permute-start.22 = (bf16[128,256]{1,0:T(8,128)(2,1)S(1)}, bf16[128,256]{1,0:T(8,128)(2,1)S(1)}, u32[]{:S(2)}, u32[]{:S(2)}) collective-permute-start(bf16[128,256]{1,0:T(8,128)(2,1)S(1)} %get-tuple-element.63), channel_id=1, source_target_pairs={{0,24},{4,28},{8,16},{12,20},{16,8},{20,12},{24,0},{28,4},{1,25},{... | collective-permute-start | bytes 196616 | tf_op jit(solution)/shard_map/ppermute | solution.py:434
  64.0 5.2 %collective-permute-start.23 = (bf16[128,256]{1,0:T(8,128)(2,1)S(1)}, bf16[128,256]{1,0:T(8,128)(2,1)S(1)}, u32[]{:S(2)}, u32[]{:S(2)}) collective-permute-start(bf16[128,256]{1,0:T(8,128)(2,1)S(1)} %get-tuple-element.62), channel_id=1, source_target_pairs={{0,28},{4,24},{8,20},{12,16},{16,12},{20,8},{24,4},{28,0},{1,29},{... | collective-permute-start | bytes 196616 | tf_op jit(solution)/shard_map/ppermute | solution.py:434
